TPU v7x, 512 devices: a whole 4x4x16 slice. The times are simulated.
512 devices in a mesh: dom: 128 (over z, y, core), feat: 4 (over x).
Axes of the slice: x: 4, y: 4, z: 16, core: 2. Of those that a mesh axis runs over, the one named last changes fastest.
Arguments:
- edge_feats: bfloat16 [65536, 1024], P('dom', 'feat'), may hold values from -6 to 6
- cotangent: bfloat16 [65536, 1024], P('dom', 'feat'), may hold values from -6 to 6
- w_down: bfloat16 [1024, 128], P('feat'), may hold values from -0.1875 to 0.1875
- w_up: bfloat16 [128, 1024], P(None, 'feat'), may hold values from -0.5 to 0.5
- w_bil: bfloat16 [4096, 128], replicated, may hold values from -0.09375 to 0.09375
- basis: float32 [16, 32, 65536], P(None, None, 'dom'), may hold values from -3 to 3
- trip_k: int32 [65536, 16], P('dom'), may hold values from 0 to 1279, as said below
- trip_count: int32 [65536], P('dom'), may hold values from 1 to 16, as said below
- send_rows: int32 [128, 6, 128], P('dom'), may hold values from 0 to 511, as said below
Outputs:
- input_grad: bfloat16 [65536, 1024], P('dom', 'feat')
- w_down_grad: float32 [1024, 128], P('feat')
- w_up_grad: float32 [128, 1024], P(None, 'feat')
- w_bil_grad: float32 [4096, 128], P('feat')
Inputs may be any that keep to these rules, and one draw needn't show every extreme that they name: `send_rows`: entry [p, j, s] is an edge of domain p (a row of its 512) placed in slot s of p's block for domain (p + o(j)) mod 128. The filled slots of a block come first and hold distinct edges; every block has one to 128 filled slots; some domain receives 128 filled slots from each of its neighbours; empty slots hold 0. `trip_k`: each entry is a row of the extended table of the edge's own domain: below 512 its own edges, else row 512 + j * 128 + s, which is always a filled slot of the block that the domain receives from its neighbour j. `trip_count`: the live triplets of an edge are its first ones; every domain has an edge with all 16 live.
All inputs are finite; a program needn't handle non-finite values.
Results may differ from a plain program's by a relative error of at most 0.012.
Values may be sent and summed in bfloat16 or wider, within the bound.
No kernel may reach another device: no remote copies, remote signals or barrier semaphores. Data moves between devices by JAX's collectives and lax.ppermute only.
A program may use at most 64 MiB of HBM per device.

v0:
```python
import math

import jax
import jax.numpy as jnp
from jax import lax
from jax.sharding import PartitionSpec as P

ALONG_ROWS = (((1,), (1,)), ((), ()))
ALONG_COLS = (((0,), (0,)), ((), ()))


def passed_along(value, axis, steps):
    count = lax.axis_size(axis)
    pairs = [(source, (source + steps) % count) for source in range(count)]
    return lax.ppermute(value, axis, pairs)


def silu_grad(value):
    sigma = jax.nn.sigmoid(value)
    return sigma * (1.0 + value * (1.0 - sigma))


def neighbour_offset(block, reach):
    if block < reach:
        return block + 1
    return reach - block - 1


def local(edge_feats, cotangent, w_down, w_up, w_bil, basis, trip_k, trip_count, send_rows):
    part_pre = jnp.dot(edge_feats, w_down, preferred_element_type=jnp.float32)
    part_bar = lax.dot_general(cotangent, w_up, ALONG_ROWS, preferred_element_type=jnp.float32)
    preact, bar_total = lax.psum((part_pre, part_bar), "feat")
    down_rows = jax.nn.silu(preact).astype(jnp.bfloat16)
    agg_bar = bar_total.astype(jnp.bfloat16)
    edge_count, feat_width = down_rows.shape
    sent_rows = send_rows[0]
    block_count, slot_count = sent_rows.shape
    reach = block_count // 2
    sent_flat = sent_rows.reshape(-1)
    outgoing = jnp.take(down_rows, sent_flat, axis=0).reshape(block_count, slot_count, feat_width)
    arrived = []
    for block in range(block_count):
        offset = neighbour_offset(block, reach)
        arrived.append(passed_along(outgoing[block], "dom", offset))
    incoming = jnp.stack(arrived, axis=0)
    ext_down = jnp.concatenate(
        [down_rows, incoming.reshape(block_count * slot_count, feat_width)], axis=0
    )
    gathered = jnp.take(ext_down, trip_k, axis=0)
    trip_width = trip_k.shape[1]
    live_mask = (jnp.arange(trip_width, dtype=jnp.int32)[:, None] < trip_count[None, :]).astype(
        jnp.float32
    )
    weights = basis * live_mask[:, None, :]
    basis_total = basis.shape[1]
    shard_total = lax.axis_size("feat")
    own_index = lax.axis_index("feat")
    basis_span = basis_total // shard_total
    summed = jnp.einsum("knE,Ekc->Enc", weights, gathered, preferred_element_type=jnp.float32)
    summed = summed.reshape(edge_count, basis_total * feat_width).astype(jnp.bfloat16)
    agg_part = jnp.dot(summed, w_bil, preferred_element_type=jnp.float32)
    grad_in = lax.dot_general(
        agg_bar, w_bil, ALONG_ROWS, preferred_element_type=jnp.float32
    ).astype(jnp.bfloat16)
    grad_in = grad_in.reshape(edge_count, basis_total, feat_width)
    d_gathered = jnp.einsum("knE,Enc->Ekc", weights, grad_in, preferred_element_type=jnp.float32)
    d_ext = jax.ops.segment_sum(
        d_gathered.reshape(-1, feat_width),
        trip_k.reshape(-1),
        num_segments=edge_count + block_count * slot_count,
    )
    own_summed = lax.dynamic_slice_in_dim(
        summed, own_index * basis_span * feat_width, basis_span * feat_width, 1
    )
    bil_term = lax.dot_general(own_summed, agg_bar, ALONG_COLS, preferred_element_type=jnp.float32)
    columns = d_ext.shape[1]
    remote_part = d_ext[edge_count:].reshape(block_count, slot_count, columns)
    sent_back = []
    for block in range(block_count):
        offset = neighbour_offset(block, reach)
        sent_back.append(passed_along(remote_part[block], "dom", -offset))
    returned = jnp.stack(sent_back, axis=0)
    d_down = d_ext[:edge_count] + jax.ops.segment_sum(
        returned.reshape(-1, columns), sent_flat, num_segments=edge_count
    )
    pre_bar = (d_down * silu_grad(preact)).astype(jnp.bfloat16)
    input_grad = (
        cotangent.astype(jnp.float32)
        + lax.dot_general(pre_bar, w_down, ALONG_ROWS, preferred_element_type=jnp.float32)
    ).astype(jnp.bfloat16)
    down_term = lax.dot_general(edge_feats, pre_bar, ALONG_COLS, preferred_element_type=jnp.float32)
    up_term = lax.dot_general(
        agg_part.astype(jnp.bfloat16), cotangent, ALONG_COLS, preferred_element_type=jnp.float32
    )
    down_total, up_total, bil_total = lax.psum((down_term, up_term, bil_term), "dom")
    factor = 1.0 / math.sqrt(edge_count * lax.axis_size("dom"))
    return (input_grad, down_total * factor, up_total * factor, bil_total * factor)


def solution(mesh):
    return jax.shard_map(
        local,
        mesh=mesh,
        in_specs=(
            P("dom", "feat"),
            P("dom", "feat"),
            P("feat", None),
            P(None, "feat"),
            P(),
            P(None, None, "dom"),
            P("dom", None),
            P("dom"),
            P("dom", None, None),
        ),
        out_specs=(P("dom", "feat"), P("feat", None), P(None, "feat"), P("feat", None)),
        check_vma=False,
    )
```

profile of v0, /device:TPU:1, one launch (start us, length us, event | category | flops | bytes accessed | tf_op | source)
XLA Modules:
  0.0 589.9 jit_solution(2114055972863416310)
XLA Ops:
  7.2 0.0 copy-start
  7.2 0.0 all-reduce.5.cloned.1.call-start
  7.2 1.2 fusion.18
  8.5 16.9 %all-reduce.8 = bf16[512,128]{1,0:T(8,128)(2,1)S(1)} all-reduce(f32[512,128]{1,0:T(8,128)S(1)} %fusion.18), channel_id=1, replica_groups=mesh['dom'=128,'feat'=4] {'feat'}, use_global_device_ids=true, to_apply=%region_0.0 | all-reduce | flops 65536 | bytes 393216 | tf_op jit(solution)/shard_map/psum | solution.py:32
  25.4 1.3 fusion
  26.7 0.0 copy-start.15
  26.7 0.0 copy-start.8
  26.7 3.2 copy.23
  29.9 0.9 broadcast_multiply_fusion
  30.9 2.9 copy.18
  33.8 0.1 copy.17
  33.9 0.1 reshape.127
  34.0 0.0 copy-start.9
  34.1 0.0 copy-start.12
  34.1 0.0 copy-start.14
  34.1 5.9 fusion.19
  40.0 44.5 %scatter_custom_fusion = f32[1280,128]{1,0:T(8,128)S(1)} fusion(s32[8192]{0:T(1024)S(1)} %reshape.127, f32[8192,128]{1,0:T(8,128)} %bitcast.64, f32[]{:T(128)} %constant.16.clone.1), kind=kCustom, calls=%fused_computation.20 | custom fusion | flops 1048576 | bytes 655872 | tf_op jit(solution)/shard_map/scatter-add | solution.py:67
  84.5 9.0 %collective-permute-start = (f32[128,128]{1,0:T(8,128)S(1)}, f32[128,128]{1,0:T(8,128)S(1)}, u32[]{:S(2)}, u32[]{:S(2)}) collective-permute-start(f32[128,128]{1,0:T(8,128)S(1)} %get-tuple-element.20), channel_id=1, source_target_pairs={{0,508},{4,0},{8,4},{12,8},{16,12},{20,16},{24,20},{28,24},{32,28}... | collective-permute-start | bytes 196616 | tf_op jit(solution)/shard_map/ppermute | solution.py:15
  93.5 11.0 %collective-permute-start.1 = (f32[128,128]{1,0:T(8,128)S(1)}, f32[128,128]{1,0:T(8,128)S(1)}, u32[]{:S(2)}, u32[]{:S(2)}) collective-permute-start(f32[128,128]{1,0:T(8,128)S(1)} %get-tuple-element.19), channel_id=1, source_target_pairs={{0,504},{4,508},{8,0},{12,4},{16,8},{20,12},{24,16},{28,20},{32,24... | collective-permute-start | bytes 196616 | tf_op jit(solution)/shard_map/ppermute | solution.py:15
  104.5 2.5 collective-permute-start.2
  107.1 2.6 collective-permute-start.3
  109.7 3.5 collective-permute-start.4
  113.2 0.9 fusion.20
  114.1 0.0 all-reduce.5.cloned.1.call-update
  114.2 0.0 all-reduce.7.cloned.1.call-start
  114.3 0.1 copy.20
  114.5 0.1 reshape.119
  114.6 0.8 copy.19
  115.4 0.0 collective-permute-done
  115.4 2.2 collective-permute-start.5
  117.7 0.0 collective-permute-done.1
  117.7 0.0 collective-permute-done.2
  117.8 0.9 collective-permute-done.4
  118.7 5.8 collective-permute-done.5
  124.5 6.4 %scatter_fusion = f32[512,128]{1,0:T(8,128)S(1)} fusion(f32[512,128]{1,0:T(8,128)S(1)} %slice.75, s32[768]{0:T(1024)S(1)} %bitcast.67, f32[768,128]{1,0:T(8,128)S(1)} %bitcast.65), kind=kCustom, calls=%fused_computation.3 | custom fusion | flops 98304 | bytes 1182720 | tf_op jit(solution)/shard_map/scatter-add | solution.py:83
  130.8 31.6 %all-reduce.5.cloned.1.call-done = f32[512,128]{1,0:T(8,128)} async-done(((f32[512,128]{1,0:T(8,128)}), f32[512,128]{1,0:T(8,128)}) %all-reduce.5.cloned.1.call-update) | async-done | bytes 262160 | tf_op jit(solution)/shard_map/psum | solution.py:32
  162.4 1.1 multiply_convert_fusion
  163.5 0.0 copy-start.6
  163.5 1.9 gather_fusion
  165.4 0.2 broadcast_select_fusion
  165.6 5.8 collective-permute-start.6
  171.4 3.1 collective-permute-start.7
  174.5 3.4 collective-permute-start.8
  178.0 1.9 collective-permute-start.9
  179.9 5.6 collective-permute-start.10
  185.4 0.9 convolution_bitcast_fusion
  186.3 3.9 collective-permute-start.11
  190.3 0.0 collective-permute-done.7
  190.3 0.0 collective-permute-done.8
  190.3 0.0 collective-permute-done.9
  190.4 2.7 collective-permute-done.11
  193.1 29.4 %gather_fusion.1 = bf16[8192,128]{1,0:T(8,128)(2,1)} fusion(bf16[1280,128]{1,0:T(8,128)(2,1)S(1)} %pad_maximum_fusion, s32[8192]{0:T(1024)S(1)} %broadcast_clamp_fusion), kind=kCustom, calls=%fused_computation.1 | custom fusion | bytes 4227072 | tf_op jit(solution)/shard_map/jit(_take)/gather | solution.py:49
  222.5 4.3 convolution_convert_fusion.1
  226.8 2.0 copy-done.3
  228.8 6.1 %copy.28 = bf16[64,8,32,128]{3,1,2,0:T(8,128)(2,1)} copy(bf16[64,8,32,128]{3,2,1,0:T(8,128)(2,1)S(1)} %bitcast.60) | data formatting | bytes 8388608
  234.9 4.4 fusion.4
  239.3 2.5 fusion.5
  241.8 0.0 all-reduce.7.cloned.1.call-update
  241.9 0.9 fusion.3
  242.8 335.1 %all-reduce.7.cloned.1.call-done = (f32[256,128]{0,1:T(8,128)}, f32[128,256]{1,0:T(8,128)}, f32[1024,128]{1,0:T(8,128)}) async-done(((f32[256,128]{0,1:T(8,128)}, f32[128,256]{1,0:T(8,128)}, f32[1024,128]{1,0:T(8,128)}), (f32[256,128]{0,1:T(8,128)}, f32[128,256]{1,0:T(8,128)}, f32[1024,128]{1,0:T(8,128)})) %all-reduce.7.cloned.1.call-update) | async-done | bytes 786448 | tf_op jit(solution)/shard_map/psum | solution.py:95
  577.9 1.9 broadcast_multiply_fusion.1
  579.8 0.9 broadcast_multiply_fusion.3
  580.7 0.8 copy.22
  581.5 1.6 broadcast_multiply_fusion.2
  (51 shorter events, 0.3 us)
Async XLA Ops:
  7.2 18.2 %copy-start = (bf16[4096,128]{1,0:T(8,128)(2,1)S(1)}, bf16[4096,128]{1,0:T(8,128)(2,1)}, u32[]{:S(2)}) copy-start(bf16[4096,128]{1,0:T(8,128)(2,1)} %param.13) | copy-start | bytes 3145732
  7.2 155.2 %all-reduce.5.cloned.1.call-start = ((), (), s32[]{:S(2)}) async-start(), calls=%async_computation | async-start | bytes 524288 | tf_op jit(solution)/shard_map/psum | solution.py:32
  25.4 4.5 copy-start.4
  26.7 3.3 copy-start.15
  26.7 3.3 copy-start.8
  29.9 3.8 copy-start.11
  33.8 6.2 %copy-start.1 = (bf16[16,32,512]{1,0,2:T(8,128)(2,1)}, bf16[16,32,512]{1,0,2:T(8,128)(2,1)S(1)}, u32[]{:S(2)}) copy-start(bf16[16,32,512]{1,0,2:T(8,128)(2,1)S(1)} %copy.18) | copy-start | bytes 1572868
  34.0 79.1 %copy-start.9 = (bf16[512,256]{1,0:T(8,128)(2,1)S(1)}, bf16[512,256]{1,0:T(8,128)(2,1)}, u32[]{:S(2)}) copy-start(bf16[512,256]{1,0:T(8,128)(2,1)} %param.9) | copy-start | bytes 786436
  34.1 79.1 %copy-start.12 = (bf16[256,128]{1,0:T(8,128)(2,1)S(1)}, bf16[256,128]{1,0:T(8,128)(2,1)}, u32[]{:S(2)}) copy-start(bf16[256,128]{1,0:T(8,128)(2,1)} %param.11) | copy-start | bytes 196612
  34.1 80.2 %copy-start.14 = (s32[1,6,128]{2,0,1:T(1,128)S(1)}, s32[1,6,128]{2,0,1:T(1,128)}, u32[]{:S(2)}) copy-start(s32[1,6,128]{2,0,1:T(1,128)} %param.17) | copy-start | bytes 9220
  84.5 30.9 %collective-permute-start = (f32[128,128]{1,0:T(8,128)S(1)}, f32[128,128]{1,0:T(8,128)S(1)}, u32[]{:S(2)}, u32[]{:S(2)}) collective-permute-start(f32[128,128]{1,0:T(8,128)S(1)} %get-tuple-element.20), channel_id=1, source_target_pairs={{0,508},{4,0},{8,4},{12,8},{16,12},{20,16},{24,20},{28,24},{32,28}... | collective-permute-start | bytes 196616 | tf_op jit(solution)/shard_map/ppermute | solution.py:15
  93.5 24.2 %collective-permute-start.1 = (f32[128,128]{1,0:T(8,128)S(1)}, f32[128,128]{1,0:T(8,128)S(1)}, u32[]{:S(2)}, u32[]{:S(2)}) collective-permute-start(f32[128,128]{1,0:T(8,128)S(1)} %get-tuple-element.19), channel_id=1, source_target_pairs={{0,504},{4,508},{8,0},{12,4},{16,8},{20,12},{24,16},{28,20},{32,24... | collective-permute-start | bytes 196616 | tf_op jit(solution)/shard_map/ppermute | solution.py:15
  104.5 13.2 %collective-permute-start.2 = (f32[128,128]{1,0:T(8,128)S(1)}, f32[128,128]{1,0:T(8,128)S(1)}, u32[]{:S(2)}, u32[]{:S(2)}) collective-permute-start(f32[128,128]{1,0:T(8,128)S(1)} %get-tuple-element.18), channel_id=1, source_target_pairs={{0,500},{4,504},{8,508},{12,0},{16,4},{20,8},{24,12},{28,16},{32,2... | collective-permute-start | bytes 196616 | tf_op jit(solution)/shard_map/ppermute | solution.py:15
  107.1 10.7 %collective-permute-start.3 = (f32[128,128]{1,0:T(8,128)S(1)}, f32[128,128]{1,0:T(8,128)S(1)}, u32[]{:S(2)}, u32[]{:S(2)}) collective-permute-start(f32[128,128]{1,0:T(8,128)S(1)} %get-tuple-element.17), channel_id=1, source_target_pairs={{0,4},{4,8},{8,12},{12,16},{16,20},{20,24},{24,28},{28,32},{32,36}... | collective-permute-start | bytes 196616 | tf_op jit(solution)/shard_map/ppermute | solution.py:15
  109.7 9.0 %collective-permute-start.4 = (f32[128,128]{1,0:T(8,128)S(1)}, f32[128,128]{1,0:T(8,128)S(1)}, u32[]{:S(2)}, u32[]{:S(2)}) collective-permute-start(f32[128,128]{1,0:T(8,128)S(1)} %get-tuple-element.16), channel_id=1, source_target_pairs={{0,8},{4,12},{8,16},{12,20},{16,24},{20,28},{24,32},{28,36},{32,40... | collective-permute-start | bytes 196616 | tf_op jit(solution)/shard_map/ppermute | solution.py:15
  114.2 463.8 %all-reduce.7.cloned.1.call-start = ((), (), s32[]{:S(2)}) async-start(), calls=%async_computation.1 | async-start | bytes 1572864 | tf_op jit(solution)/shard_map/psum | solution.py:95
  115.4 9.0 %collective-permute-start.5 = (f32[128,128]{1,0:T(8,128)S(1)}, f32[128,128]{1,0:T(8,128)S(1)}, u32[]{:S(2)}, u32[]{:S(2)}) collective-permute-start(f32[128,128]{1,0:T(8,128)S(1)} %get-tuple-element.15), channel_id=1, source_target_pairs={{0,12},{4,16},{8,20},{12,24},{16,28},{20,32},{24,36},{28,40},{32,4... | collective-permute-start | bytes 196616 | tf_op jit(solution)/shard_map/ppermute | solution.py:15
  163.5 29.6 %copy-start.6 = (bf16[512,128]{1,0:T(8,128)(2,1)}, bf16[512,128]{1,0:T(8,128)(2,1)S(1)}, u32[]{:S(2)}) copy-start(bf16[512,128]{1,0:T(8,128)(2,1)S(1)} %get-tuple-element.22) | copy-start | bytes 393220
  165.6 20.8 %collective-permute-start.6 = (bf16[128,128]{1,0:T(8,128)(2,1)S(1)}, bf16[128,128]{1,0:T(8,128)(2,1)S(1)}, u32[]{:S(2)}, u32[]{:S(2)}) collective-permute-start(bf16[128,128]{1,0:T(8,128)(2,1)S(1)} %get-tuple-element.28), channel_id=1, source_target_pairs={{0,4},{4,8},{8,12},{12,16},{16,20},{20,24},{24,28},{28,32},{32,36}... | collective-permute-start | bytes 98312 | tf_op jit(solution)/shard_map/ppermute | solution.py:15
  171.4 18.9 %collective-permute-start.7 = (bf16[128,128]{1,0:T(8,128)(2,1)S(1)}, bf16[128,128]{1,0:T(8,128)(2,1)S(1)}, u32[]{:S(2)}, u32[]{:S(2)}) collective-permute-start(bf16[128,128]{1,0:T(8,128)(2,1)S(1)} %get-tuple-element.27), channel_id=1, source_target_pairs={{0,8},{4,12},{8,16},{12,20},{16,24},{20,28},{24,32},{28,36},{32,40... | collective-permute-start | bytes 98312 | tf_op jit(solution)/shard_map/ppermute | solution.py:15
  174.5 15.8 %collective-permute-start.8 = (bf16[128,128]{1,0:T(8,128)(2,1)S(1)}, bf16[128,128]{1,0:T(8,128)(2,1)S(1)}, u32[]{:S(2)}, u32[]{:S(2)}) collective-permute-start(bf16[128,128]{1,0:T(8,128)(2,1)S(1)} %get-tuple-element.26), channel_id=1, source_target_pairs={{0,12},{4,16},{8,20},{12,24},{16,28},{20,32},{24,36},{28,40},{32,4... | collective-permute-start | bytes 98312 | tf_op jit(solution)/shard_map/ppermute | solution.py:15
  178.0 12.4 %collective-permute-start.9 = (bf16[128,128]{1,0:T(8,128)(2,1)S(1)}, bf16[128,128]{1,0:T(8,128)(2,1)S(1)}, u32[]{:S(2)}, u32[]{:S(2)}) collective-permute-start(bf16[128,128]{1,0:T(8,128)(2,1)S(1)} %get-tuple-element.25), channel_id=1, source_target_pairs={{0,508},{4,0},{8,4},{12,8},{16,12},{20,16},{24,20},{28,24},{32,28}... | collective-permute-start | bytes 98312 | tf_op jit(solution)/shard_map/ppermute | solution.py:15
  179.9 10.5 %collective-permute-start.10 = (bf16[128,128]{1,0:T(8,128)(2,1)S(1)}, bf16[128,128]{1,0:T(8,128)(2,1)S(1)}, u32[]{:S(2)}, u32[]{:S(2)}) collective-permute-start(bf16[128,128]{1,0:T(8,128)(2,1)S(1)} %get-tuple-element.24), channel_id=1, source_target_pairs={{0,504},{4,508},{8,0},{12,4},{16,8},{20,12},{24,16},{28,20},{32,24... | collective-permute-start | bytes 98312 | tf_op jit(solution)/shard_map/ppermute | solution.py:15
  186.3 6.7 %collective-permute-start.11 = (bf16[128,128]{1,0:T(8,128)(2,1)S(1)}, bf16[128,128]{1,0:T(8,128)(2,1)S(1)}, u32[]{:S(2)}, u32[]{:S(2)}) collective-permute-start(bf16[128,128]{1,0:T(8,128)(2,1)S(1)} %get-tuple-element.23), channel_id=1, source_target_pairs={{0,500},{4,504},{8,508},{12,0},{16,4},{20,8},{24,12},{28,16},{32,2... | collective-permute-start | bytes 98312 | tf_op jit(solution)/shard_map/ppermute | solution.py:15
  193.1 29.4 %copy-start.2 = (bf16[16,32,512]{1,0,2:T(8,128)(2,1)S(1)}, bf16[16,32,512]{1,0,2:T(8,128)(2,1)}, u32[]{:S(2)}) copy-start(bf16[16,32,512]{1,0,2:T(8,128)(2,1)} %copy-done.1) | copy-start | bytes 1572868
  226.8 2.0 copy-start.3
  228.8 6.1 %copy-start.10 = (bf16[512,256]{1,0:T(8,128)(2,1)S(1)}, bf16[512,256]{1,0:T(8,128)(2,1)}, u32[]{:S(2)}) copy-start(bf16[512,256]{1,0:T(8,128)(2,1)} %param.10) | copy-start | bytes 786436
  234.9 4.4 copy-start.5
  234.9 7.0 %copy-start.7 = (bf16[512,128]{1,0:T(8,128)(2,1)S(1)}, bf16[512,128]{1,0:T(8,128)(2,1)}, u32[]{:S(2)}) copy-start(bf16[512,128]{1,0:T(8,128)(2,1)} %copy-done.6) | copy-start | bytes 393220
  234.9 7.0 %copy-start.13 = (bf16[256,128]{1,0:T(8,128)(2,1)S(1)}, bf16[256,128]{1,0:T(8,128)(2,1)}, u32[]{:S(2)}) copy-start(bf16[256,128]{1,0:T(8,128)(2,1)} %param.11) | copy-start | bytes 196612
Sparse Core Ops, SparseCore 0:
  114.3 48.0 all-reduce.4
  242.0 335.9 all-reduce.6
where the time goes:
time: 591 us; the launch traced here: 590 us
  waiting for transfers between devices  376 us (64%)
  other arithmetic  57.5 us (10%)
  starting transfers between devices  54.7 us (9%)
  local copies, waits for them, and re-layouts  47.8 us (8%)
  matrix products  22.3 us (4%)
  blocking collectives  16.9 us (3%)
  between operations  14.6 us (2%)
    psum x1, waiting for transfers between devices, local(): lax.psum((down_term, up_term, bil_term), 'dom')  335 us
    ppermute x12, starting transfers between devices, passed_along(): return lax.ppermute(value, axis, pairs)  54.6 us
    scatter-add x1, other arithmetic, local(): jax.ops.segment_sum(d_gathered.reshape(-1, feat_width), trip_k.reshape(-1...  44.5 us
    psum x1, waiting for transfers between devices, local(): preact, bar_total = lax.psum((part_pre, part_bar), 'feat')  31.6 us
    gather x1, local copies, waits for them, and re-layouts, local(): gathered = jnp.take(ext_down, trip_k, axis=0)  29.4 us
    psum x1, blocking collectives, local(): preact, bar_total = lax.psum((part_pre, part_bar), 'feat')  16.9 us
    unnamed x46, local copies, waits for them, and re-layouts  12.4 us
  transfers between devices with their start and end apart: 14, of which 5 were waited for; matrix products, arithmetic and copies ran while one was open for 2% of the time, Pallas kernels for 0%

commit v1 on v0

v1 whole, which is shorter than its diff:
```python
import functools
import math

import jax
import jax.numpy as jnp
from jax import lax
from jax.experimental import pallas as pl
from jax.experimental.pallas import tpu as pltpu
from jax.sharding import Mesh
from jax.sharding import PartitionSpec as P

BF = jnp.bfloat16
F32 = jnp.float32
NT = (((1,), (1,)), ((), ()))
TN = (((0,), (0,)), ((), ()))
DOM = ("zh", "zl", "y", "core")
GROUP = 16


def dot(a, b, dims=(((1,), (0,)), ((), ()))):
    return lax.dot_general(a, b, dims, preferred_element_type=F32)


def ones_where(cond):
    return jnp.where(cond, 1.0, 0.0).astype(BF)


def iota(shape, dim):
    return lax.broadcasted_iota(jnp.int32, shape, dim)


def silu_grad(value):
    sigma = jax.nn.sigmoid(value)
    return sigma * (1.0 + value * (1.0 - sigma))


def call(kernel, outs, scratch, flops, *args):
    moved = sum(a.size * a.dtype.itemsize for a in args)
    return pl.pallas_call(
        kernel,
        out_shape=outs,
        scratch_shapes=scratch,
        compiler_params=pltpu.CompilerParams(vmem_limit_bytes=40 << 20),
        cost_estimate=pl.CostEstimate(flops=flops, bytes_accessed=moved, transcendentals=0),
    )(*args)


def down_kernel(pre_ref, send_ref, down_ref, *out_refs):
    pre = pre_ref[...].astype(F32)
    down = (pre * jax.nn.sigmoid(pre)).astype(BF)
    down_ref[...] = down
    slots = out_refs[0].shape[0]
    edges = down.shape[0]
    for j, out_ref in enumerate(out_refs):
        pick = ones_where(send_ref[j * slots : (j + 1) * slots, :] == iota((slots, edges), 1))
        out_ref[...] = dot(pick, down).astype(BF)


def back_kernel(bar_ref, wbil_ref, w_ref, k_ref, own_ref, *rest):
    rem_refs, grad_ref, mask_ref, acc_ref = rest[:-3], *rest[-3:]
    basis, edges, width = grad_ref.shape
    trips = w_ref.shape[0]
    rows, cols = trips * GROUP, basis * GROUP
    table = acc_ref.shape[0]
    bar = bar_ref[...]
    for b in range(basis):
        grad_ref[b] = dot(bar, wbil_ref[b * width : (b + 1) * width, :], NT).astype(BF)
    mask_ref[...] = ones_where(iota((rows, cols), 0) % GROUP == iota((rows, cols), 1) % GROUP)
    spread = ones_where(iota((basis, cols), 0) == iota((basis, cols), 1) // GROUP)
    acc_ref[...] = jnp.zeros_like(acc_ref)

    def body(g, carry):
        at = pl.ds(pl.multiple_of(g * GROUP, GROUP), GROUP)
        w = w_ref[:, at, :].reshape(rows, basis)
        diag = dot(w, spread).astype(BF) * mask_ref[...]
        grad = grad_ref[:, at, :].reshape(cols, width)
        d_rows = dot(diag, grad).astype(BF)
        pick = ones_where(k_ref[g] == iota((table, rows), 0))
        acc_ref[...] += dot(pick, d_rows)
        return carry

    lax.fori_loop(0, edges // GROUP, body, 0)
    own_ref[...] = acc_ref[:edges, :]
    slots = rem_refs[0].shape[0]
    for j, rem_ref in enumerate(rem_refs):
        first = edges + j * slots
        rem_ref[...] = acc_ref[first : first + slots, :].astype(BF)


def fore_kernel(which_ref, down_ref, *rest):
    in_refs, (w_ref, k_ref, wbil_ref, bar_ref, cot_ref, out_ref, ext_ref, sum_ref, mask_ref) = (
        rest[:-9],
        rest[-9:],
    )
    basis, edges, width = sum_ref.shape
    trips = k_ref.shape[1]
    rows, cols = basis * GROUP, trips * GROUP
    table = ext_ref.shape[0]
    ext_ref[:edges, :] = down_ref[...]
    slots = in_refs[0].shape[0]
    for j, in_ref in enumerate(in_refs):
        first = edges + j * slots
        ext_ref[first : first + slots, :] = in_ref[...]
    mask_ref[...] = ones_where(iota((rows, cols), 0) % GROUP == iota((rows, cols), 1) % GROUP)
    spread = ones_where(iota((trips, cols), 0) == iota((trips, cols), 1) // GROUP)

    def body(g, carry):
        at = pl.ds(pl.multiple_of(g * GROUP, GROUP), GROUP)
        k = k_ref[at, :]
        lane = iota((GROUP, table), 1)
        pick = jnp.concatenate([ones_where(k[:, i : i + 1] == lane) for i in range(trips)], axis=0)
        got = dot(pick, ext_ref[...]).astype(BF)
        w = w_ref[:, at, :].reshape(rows, trips)
        diag = dot(w, spread).astype(BF) * mask_ref[...]
        sum_ref[:, at, :] = dot(diag, got).astype(BF).reshape(basis, GROUP, width)
        return carry

    lax.fori_loop(0, edges // GROUP, body, 0)
    agg = jnp.zeros((edges, width), F32)
    for b in range(0, basis, 2):
        pair = jnp.concatenate([sum_ref[b], sum_ref[b + 1]], axis=1)
        agg = agg + dot(pair, wbil_ref[b * width : (b + 2) * width, :])
    low = agg.astype(BF)
    span = out_ref.shape[0] // width - 2
    for h in range(2):
        part = dot(low, cot_ref[:, h * width : (h + 1) * width], TN)
        first = (span + h) * width
        out_ref[first : first + width, :] = part.astype(BF)
    bar = bar_ref[...]
    for j in range(span):
        part = dot(sum_ref[which_ref[0] * span + j], bar, TN)
        out_ref[j * width : (j + 1) * width, :] = part.astype(BF)


def last_kernel(own_ref, pre_ref, send_ref, wdown_ref, cot_ref, feats_ref, *rest):
    back_refs, (grad_ref, term_ref) = rest[:-2], rest[-2:]
    edges = own_ref.shape[0]
    slots = back_refs[0].shape[0]
    total = own_ref[...]
    for j, back_ref in enumerate(back_refs):
        place = ones_where(send_ref[:, j * slots : (j + 1) * slots] == iota((edges, slots), 0))
        total = total + dot(place, back_ref[...])
    pre_bar = (total * silu_grad(pre_ref[...].astype(F32))).astype(BF)
    grad_ref[...] = (cot_ref[...].astype(F32) + dot(pre_bar, wdown_ref[...], NT)).astype(BF)
    term_ref[...] = dot(feats_ref[...], pre_bar, TN).astype(BF)


def shifted(value, offset):
    count = lax.axis_size(DOM)
    return lax.ppermute(value, DOM, [(s, (s + offset) % count) for s in range(count)])


def scattered_sum(pieces, axis):
    arrived = lax.all_to_all(pieces, axis, 0, 0)
    return jnp.sum(arrived.astype(F32), axis=0).astype(BF)


def everywhere(value, axis):
    count = lax.axis_size(axis)
    copies = lax.optimization_barrier(jnp.broadcast_to(value[None], (count, *value.shape)))
    return lax.all_to_all(copies, axis, 0, 0)


def exchanged_sum(value, axis):
    return jnp.sum(everywhere(value, axis).astype(F32), axis=0).astype(BF)


def local(edge_feats, cotangent, w_down, w_up, w_bil, basis, trip_k, trip_count, send_rows):
    edges, span = edge_feats.shape
    width = w_down.shape[1]
    trips, basis_total, _ = basis.shape
    _, blocks, slots = send_rows.shape
    reach = blocks // 2
    offsets = [j + 1 if j < reach else reach - j - 1 for j in range(blocks)]
    feats = lax.axis_size("feat")
    groups = edges // GROUP
    low = lambda *shape: jax.ShapeDtypeStruct(shape, BF)

    part_pre = dot(edge_feats, w_down).astype(BF).reshape(feats, edges // feats, width)
    part_bar = dot(cotangent, w_up, NT).astype(BF).reshape(feats, edges // feats, width)
    both = scattered_sum(jnp.concatenate([part_pre, part_bar], axis=1), "feat")
    both = everywhere(both, "feat")
    pre = both[:, : edges // feats].reshape(edges, width)
    bar = both[:, edges // feats :].reshape(edges, width)

    live = jnp.arange(trips, dtype=jnp.int32)[:, None] < trip_count[None, :]
    weights = jnp.where(live[:, None, :], basis, 0.0).astype(BF)
    w_fore = weights.transpose(1, 2, 0)
    w_back = weights.transpose(0, 2, 1)
    k_rows = trip_k.T.reshape(trips, groups, GROUP).transpose(1, 0, 2).reshape(groups, 1, -1)

    down, *outgoing = call(
        down_kernel,
        [low(edges, width)] + [low(slots, width)] * blocks,
        [],
        2 * blocks * slots * edges * width,
        pre,
        send_rows.reshape(-1, 1),
    )
    incoming = [shifted(outgoing[j], offsets[j]) for j in range(blocks)]

    table = edges + blocks * slots
    big = 2 * edges * trips * width * (table + 3 * GROUP * basis_total)
    own, *remote = call(
        back_kernel,
        [jax.ShapeDtypeStruct((edges, width), F32)] + [low(slots, width)] * blocks,
        [
            pltpu.VMEM((basis_total, edges, width), BF),
            pltpu.VMEM((trips * GROUP, basis_total * GROUP), BF),
            pltpu.VMEM((table, width), F32),
        ],
        big,
        bar,
        w_bil,
        w_back,
        k_rows,
    )
    returned = [shifted(remote[j], -offsets[j]) for j in range(blocks)]

    own_rows = basis_total // feats * width
    which = lax.axis_index("feat").astype(jnp.int32).reshape(1)
    fore = functools.partial(
        pl.pallas_call,
        fore_kernel,
        in_specs=[pl.BlockSpec(memory_space=pltpu.SMEM)]
        + [pl.BlockSpec(memory_space=pltpu.VMEM)] * (blocks + 6),
        out_shape=low(own_rows + 2 * width, width),
        scratch_shapes=[
            pltpu.VMEM((table, width), BF),
            pltpu.VMEM((basis_total, edges, width), BF),
            pltpu.VMEM((basis_total * GROUP, trips * GROUP), BF),
        ],
        compiler_params=pltpu.CompilerParams(vmem_limit_bytes=40 << 20),
        cost_estimate=pl.CostEstimate(flops=big, bytes_accessed=8 << 20, transcendentals=0),
    )()
    early = fore(which, down, *incoming, w_fore, trip_k, w_bil, bar, cotangent)

    input_grad, late = call(
        last_kernel,
        [low(edges, span), low(span, width)],
        [],
        2 * edges * width * (blocks * slots + 2 * span),
        own,
        pre,
        send_rows.reshape(1, -1),
        w_down,
        cotangent,
        edge_feats,
        *returned,
    )

    near = ("y", "core")
    count = lax.axis_size(near)
    early = early.reshape(count, -1, width)
    late = late.reshape(count, -1, width)
    split = early.shape[1]
    total = scattered_sum(jnp.concatenate([early, late], axis=1), near)
    total = exchanged_sum(total, "zl")
    total = exchanged_sum(total, "zh")
    total = everywhere(total, near)
    factor = 1.0 / math.sqrt(edges * lax.axis_size(DOM))
    early = total[:, :split].reshape(-1, width).astype(F32) * factor
    late = total[:, split:].reshape(-1, width).astype(F32) * factor
    up = jnp.concatenate([early[own_rows : own_rows + width], early[own_rows + width :]], axis=1)
    return input_grad, late, up, early[:own_rows]


def solution(mesh):
    fine = Mesh(mesh.devices.reshape(4, 4, 4, 2, 4), (*DOM, "feat"))
    return jax.shard_map(
        local,
        mesh=fine,
        in_specs=(
            P(DOM, "feat"),
            P(DOM, "feat"),
            P("feat", None),
            P(None, "feat"),
            P(),
            P(None, None, DOM),
            P(DOM, None),
            P(DOM),
            P(DOM, None, None),
        ),
        out_specs=(P(DOM, "feat"), P("feat", None), P(None, "feat"), P("feat", None)),
        check_vma=False,
    )
```

time: 591 us -> 196 us (0.33)
  waiting for transfers between devices: 376 us -> 2.65 us
  other arithmetic: 57.5 us -> 3.24 us
  Pallas kernels: 0 us -> 48.7 us
  blocking collectives: 16.9 us -> 57.9 us
  local copies, waits for them, and re-layouts: 47.8 us -> 21.5 us
  matrix products: 22.3 us -> 2.35 us
  between operations: 14.6 us -> 1.05 us
    psum x2 -> x0, waiting for transfers between devices: 367 us -> none  [the longest x1 335 us: local(): lax.psum((down_term, up_term, bil_term), 'dom')]
    all_to_all x0 -> x4, blocking collectives: none -> 57.9 us  [the longest x3 47.9 us: everywhere(): return lax.all_to_all(copies, axis, 0, 0)]
    scatter-add x2 -> x0, other arithmetic: 50.9 us -> none  [the longest x1 44.5 us: local(): jax.ops.segment_sum(d_gathered.reshape(-1, feat_width), trip_k.reshape(-1...]
    pallas_call x0 -> x4, Pallas kernels: none -> 48.7 us  [the longest x1 24.8 us: local(): early = fore(which, down, *incoming, w_fore, trip_k, w_bil, bar, cotangent)]
    gather x2 -> x0, local copies, waits for them, and re-layouts: 31.3 us -> none  [the longest x1 29.4 us: local(): gathered = jnp.take(ext_down, trip_k, axis=0)]
    dot_general x9 -> x2, matrix products: 22.3 us -> 2.35 us  [dot(): return lax.dot_general(a, b, dims, preferred_element_type=F32)]
    psum x1 -> x0, blocking collectives: 16.9 us -> none  [local(): preact, bar_total = lax.psum((part_pre, part_bar), 'feat')]
    ppermute x12, waiting for transfers between devices: 9.38 us -> 0.03 us  [shifted(): lax.ppermute(value, DOM, [(s, (s + offset) % count) for s in range(count)])]
  transfers between devices with their start and end apart: 14 -> 14, of which waited for: 5 -> 1; matrix products, arithmetic and copies ran while one was open for 2% -> 7% of each run, Pallas kernels for 0% -> 12%
where the time goes in v1:
time: 196 us; the launch traced here: 195 us
  starting transfers between devices  57.9 us (30%)
  blocking collectives  57.9 us (30%)
  Pallas kernels  48.7 us (25%)
  local copies, waits for them, and re-layouts  21.5 us (11%)
  other arithmetic  3.24 us (2%)
  waiting for transfers between devices  2.65 us (1%)
  matrix products  2.35 us (1%)
    ppermute x12, starting transfers between devices, shifted(): lax.ppermute(value, DOM, [(s, (s + offset) % count) for s in range(count)])  49 us
    all_to_all x3, blocking collectives, everywhere(): return lax.all_to_all(copies, axis, 0, 0)  47.9 us
    pallas_call x1, Pallas kernels, local(): early = fore(which, down, *incoming, w_fore, trip_k, w_bil, bar, cotangent)  24.8 us
    pallas_call x3, Pallas kernels, call(): pl.pallas_call(kernel, out_shape=outs, scratch_shapes=scratch, compiler_p...  23.9 us
    all_to_all x1, blocking collectives, scattered_sum(): arrived = lax.all_to_all(pieces, axis, 0, 0)  10 us
    transpose x1, local copies, waits for them, and re-layouts, local(): w_back = weights.transpose(0, 2, 1)  7.23 us
    unnamed x20, local copies, waits for them, and re-layouts  6.47 us
    all_to_all x1, starting transfers between devices, scattered_sum(): arrived = lax.all_to_all(pieces, axis, 0, 0)  4.82 us
  transfers between devices with their start and end apart: 14, of which 1 were waited for; matrix products, arithmetic and copies ran while one was open for 7% of the time, Pallas kernels for 12%

profile of v1, /device:TPU:1, one launch (start us, length us, event | category | flops | bytes accessed | tf_op | source)
XLA Modules:
  0.0 195.2 jit_solution(17772187710268106809)
XLA Ops:
  0.6 0.0 copy-start
  0.6 0.0 copy-start.8
  0.7 0.8 copy-done
  1.5 1.2 convolution_convert_fusion
  2.7 1.2 convolution_convert_fusion.1
  3.8 0.7 pad_maximum_fusion.1
  4.6 4.8 %all-to-all-start = ((bf16[4,256,128]{2,1,0:T(8,128)(2,1)}), bf16[4,256,128]{2,1,0:T(8,128)(2,1)S(1)}, u32[]{:S(2)}, u32[]{:S(2)}) async-start(bf16[4,256,128]{2,1,0:T(8,128)(2,1)} %pad_maximum_fusion.1), calls=%async_computation | async-start | bytes 524288 | tf_op jit(solution)/shard_map/all_to_all | solution.py:154
  9.4 0.8 iota_compare_fusion
  10.2 0.1 copy.42
  10.3 0.9 reshape.73
  11.2 0.1 copy.37
  11.3 0.1 copy.39.k_ref
  11.4 0.9 copy.40.send_ref
  12.3 2.6 %all-to-all-done = bf16[4,256,128]{2,1,0:T(8,128)(2,1)S(1)} async-done(((bf16[4,256,128]{2,1,0:T(8,128)(2,1)}), bf16[4,256,128]{2,1,0:T(8,128)(2,1)S(1)}, u32[]{:S(2)}, u32[]{:S(2)}) %all-to-all-start) | async-done | bytes 262176 | tf_op jit(solution)/shard_map/all_to_all | solution.py:154
  15.0 0.7 broadcast_in_dim.20
  15.7 4.1 %all-to-all-start.1 = ((bf16[4,256,128]{2,1,0:T(8,128)(2,1)}), bf16[4,256,128]{2,1,0:T(8,128)(2,1)}, u32[]{:S(2)}, u32[]{:S(2)}) async-start(bf16[4,256,128]{2,1,0:T(8,128)(2,1)} %broadcast_in_dim.20), calls=%async_computation.1 | async-start | bytes 524288 | tf_op jit(solution)/shard_map/all_to_all | solution.py:161
  19.8 0.1 broadcast_select_fusion
  19.9 3.2 %copy.36 = bf16[16,32,512]{0,2,1:T(8,128)(2,1)} copy(bf16[16,32,512]{2,1,0:T(8,128)(2,1)S(1)} %broadcast_select_fusion) | data formatting | bytes 1048576 | tf_op jit(solution)/shard_map/jit(_where)/select_n | solution.py:187
  23.1 7.2 %copy.38.w_ref = bf16[16,512,32]{2,1,0:T(8,128)(2,1)S(1)} copy(bf16[16,512,32]{0,1,2:T(8,128)(2,1)} %bitcast.24) | data formatting | bytes 1048576 | tf_op jit(solution)/shard_map/transpose | solution.py:189
  30.4 0.0 all-to-all-done.1
  30.4 1.0 fusion.1
  31.4 1.0 shard_map.122
  32.4 5.2 %collective-permute-start.6 = (bf16[128,128]{1,0:T(8,128)(2,1)S(1)}, bf16[128,128]{1,0:T(8,128)(2,1)S(1)}, u32[]{:S(2)}, u32[]{:S(2)}) collective-permute-start(bf16[128,128]{1,0:T(8,128)(2,1)S(1)} %get-tuple-element.29), channel_id=1, source_target_pairs={{0,4},{4,8},{8,12},{12,16},{16,20},{20,24},{24,28},{28,32},{32,36}... | collective-permute-start | bytes 98312 | tf_op jit(solution)/shard_map/ppermute | solution.py:150
  37.6 0.0 copy-start.6
  37.6 1.2 copy-done.6
  38.8 21.5 %shard_map.120 = (f32[512,128]{1,0:T(8,128)S(1)}, bf16[128,128]{1,0:T(8,128)(2,1)S(1)}, bf16[128,128]{1,0:T(8,128)(2,1)S(1)}, bf16[128,128]{1,0:T(8,128)(2,1)S(1...) custom-call(bf16[512,128]{1,0:T(8,128)(2,1)S(1)} %bitcast.29, ...), custom_call_target="tpu_custom_call" | custom-call | flops 5905580032 | bytes 1736704 | tf_op jit(solution)/shard_map/pallas_call | solution.py:39
  60.4 5.2 %collective-permute-start = (bf16[128,128]{1,0:T(8,128)(2,1)S(1)}, bf16[128,128]{1,0:T(8,128)(2,1)S(1)}, u32[]{:S(2)}, u32[]{:S(2)}) collective-permute-start(bf16[128,128]{1,0:T(8,128)(2,1)S(1)} %get-tuple-element.21), channel_id=1, source_target_pairs={{0,508},{4,0},{8,4},{12,8},{16,12},{20,16},{24,20},{28,24},{32,28}... | collective-permute-start | bytes 98312 | tf_op jit(solution)/shard_map/ppermute | solution.py:150
  65.5 9.1 %collective-permute-start.1 = (bf16[128,128]{1,0:T(8,128)(2,1)S(1)}, bf16[128,128]{1,0:T(8,128)(2,1)S(1)}, u32[]{:S(2)}, u32[]{:S(2)}) collective-permute-start(bf16[128,128]{1,0:T(8,128)(2,1)S(1)} %get-tuple-element.22), channel_id=1, source_target_pairs={{0,504},{4,508},{8,0},{12,4},{16,8},{20,12},{24,16},{28,20},{32,24... | collective-permute-start | bytes 98312 | tf_op jit(solution)/shard_map/ppermute | solution.py:150
  74.7 4.3 %collective-permute-start.2 = (bf16[128,128]{1,0:T(8,128)(2,1)S(1)}, bf16[128,128]{1,0:T(8,128)(2,1)S(1)}, u32[]{:S(2)}, u32[]{:S(2)}) collective-permute-start(bf16[128,128]{1,0:T(8,128)(2,1)S(1)} %get-tuple-element.23), channel_id=1, source_target_pairs={{0,500},{4,504},{8,508},{12,0},{16,4},{20,8},{24,12},{28,16},{32,2... | collective-permute-start | bytes 98312 | tf_op jit(solution)/shard_map/ppermute | solution.py:150
  79.0 1.9 collective-permute-start.3
  80.9 0.0 collective-permute-done.6.rest_0_
  80.9 2.9 %collective-permute-start.4 = (bf16[128,128]{1,0:T(8,128)(2,1)S(1)}, bf16[128,128]{1,0:T(8,128)(2,1)S(1)}, u32[]{:S(2)}, u32[]{:S(2)}) collective-permute-start(bf16[128,128]{1,0:T(8,128)(2,1)S(1)} %get-tuple-element.25), channel_id=1, source_target_pairs={{0,8},{4,12},{8,16},{12,20},{16,24},{20,28},{24,32},{28,36},{32,40... | collective-permute-start | bytes 98312 | tf_op jit(solution)/shard_map/ppermute | solution.py:150
  83.8 0.0 collective-permute-done.rest_0_
  83.8 1.9 collective-permute-start.5
  85.8 0.0 collective-permute-done.1.rest_1_
  85.8 1.9 collective-permute-start.7
  87.7 0.0 collective-permute-done.2.rest_2_
  87.7 1.9 collective-permute-start.8
  89.6 0.0 collective-permute-done.3.rest_3_
  89.6 2.7 %collective-permute-start.9 = (bf16[128,128]{1,0:T(8,128)(2,1)}, bf16[128,128]{1,0:T(8,128)(2,1)S(1)}, u32[]{:S(2)}, u32[]{:S(2)}) collective-permute-start(bf16[128,128]{1,0:T(8,128)(2,1)} %get-tuple-element.32), channel_id=1, source_target_pairs={{0,508},{4,0},{8,4},{12,8},{16,12},{20,16},{24,20},{28,24},{32,28}... | collective-permute-start | bytes 98312 | tf_op jit(solution)/shard_map/ppermute | solution.py:150
  92.3 0.0 collective-permute-done.4.rest_4_
  92.3 7.0 %collective-permute-start.10 = (bf16[128,128]{1,0:T(8,128)(2,1)}, bf16[128,128]{1,0:T(8,128)(2,1)S(1)}, u32[]{:S(2)}, u32[]{:S(2)}) collective-permute-start(bf16[128,128]{1,0:T(8,128)(2,1)} %get-tuple-element.33), channel_id=1, source_target_pairs={{0,504},{4,508},{8,0},{12,4},{16,8},{20,12},{24,16},{28,20},{32,24... | collective-permute-start | bytes 98312 | tf_op jit(solution)/shard_map/ppermute | solution.py:150
  99.3 0.0 collective-permute-done.5.rest_5_
  99.3 5.0 %collective-permute-start.11 = (bf16[128,128]{1,0:T(8,128)(2,1)}, bf16[128,128]{1,0:T(8,128)(2,1)S(1)}, u32[]{:S(2)}, u32[]{:S(2)}) collective-permute-start(bf16[128,128]{1,0:T(8,128)(2,1)} %get-tuple-element.34), channel_id=1, source_target_pairs={{0,500},{4,504},{8,508},{12,0},{16,4},{20,8},{24,12},{28,16},{32,2... | collective-permute-start | bytes 98312 | tf_op jit(solution)/shard_map/ppermute | solution.py:150
  104.3 0.9 copy.41.rest_7_
  105.3 1.4 shard_map.121
  106.6 0.0 collective-permute-done.7.rest_1_
  106.6 0.0 collective-permute-done.8.rest_2_
  106.6 0.0 collective-permute-done.9.rest_3_
  106.6 0.0 collective-permute-done.10.rest_4_
  106.6 0.0 collective-permute-done.11.rest_5_
  106.7 0.0 copy-start.1
  106.7 2.2 %copy-done.1 = bf16[16,32,512]{0,2,1:T(8,128)(2,1)S(1)} copy-done((bf16[16,32,512]{0,2,1:T(8,128)(2,1)S(1)}, bf16[16,32,512]{0,2,1:T(8,128)(2,1)}, u32[]{:S(2)}) %copy-start.1) | copy-done | bytes 524312
  108.8 1.2 copy-done.7
  110.1 24.8 %shard_map.123 = bf16[1280,128]{1,0:T(8,128)(2,1)S(1)} custom-call(s32[1]{0:T(128)} %bitcast.9.which_ref, bf16[512,128]{1,0:T(8,128)(2,1)S(1)} %get-tuple-element.28.down_ref, bf16[128,128]{1,0:T(8,128)(2,1)S(1)} %collective-permute-done.6.rest_0_, bf16[128,128]{1,0:T(8,128)(2,1)S(1)} %collective-permute-done.7.rest_1_, ...), custom_call_target="tpu_custom_call" | custom-call | flops 5905580032 | bytes 8388608 | tf_op jit(solution)/shard_map/pallas_call | solution.py:236
  134.9 10.0 %all_to_all.30 = bf16[8,192,128]{2,1,0:T(8,128)(2,1)S(1)} all-to-all(bf16[8,192,128]{2,1,0:T(8,128)(2,1)S(1)} %pad_maximum_fusion), channel_id=1, replica_groups=mesh['zh'=4,'zl'=4,'y'=4,'core'=2,'feat'=4] {'y','core'}, dimensions={0} | all-to-all | bytes 786432 | tf_op jit(solution)/shard_map/all_to_all | solution.py:154
  144.9 0.1 reduce_sum.49
  145.0 8.5 %all_to_all.31 = bf16[4,192,128]{2,1,0:T(8,128)(2,1)S(1)} all-to-all(bf16[4,192,128]{2,1,0:T(8,128)(2,1)S(1)} %broadcast_in_dim.23), channel_id=1, replica_groups=mesh['zh'=4,'zl'=4,'y'=4,'core'=2,'feat'=4] {'zl'}, dimensions={0} | all-to-all | bytes 393216 | tf_op jit(solution)/shard_map/all_to_all | solution.py:161
  153.5 25.4 %all_to_all.32 = bf16[4,192,128]{2,1,0:T(8,128)(2,1)S(1)} all-to-all(bf16[4,192,128]{2,1,0:T(8,128)(2,1)S(1)} %broadcast_in_dim.24), channel_id=1, replica_groups=mesh['zh'=4,'zl'=4,'y'=4,'core'=2,'feat'=4] {'zh'}, dimensions={0} | all-to-all | bytes 393216 | tf_op jit(solution)/shard_map/all_to_all | solution.py:161
  178.9 0.1 broadcast_in_dim.25
  179.0 14.0 %all_to_all.33 = bf16[8,192,128]{2,1,0:T(8,128)(2,1)S(1)} all-to-all(bf16[8,192,128]{2,1,0:T(8,128)(2,1)S(1)} %broadcast_in_dim.25), channel_id=1, replica_groups=mesh['zh'=4,'zl'=4,'y'=4,'core'=2,'feat'=4] {'y','core'}, dimensions={0} | all-to-all | bytes 786432 | tf_op jit(solution)/shard_map/all_to_all | solution.py:161
  193.1 0.8 slice.34
  193.9 0.7 pad_maximum_fusion.2
  194.6 0.7 convert_multiply_fusion.1
  (18 shorter events, 0.3 us)
Async XLA Ops:
  0.6 0.8 copy-start
  0.6 19.1 %copy-start.8 = (f32[16,32,512]{2,1,0:T(8,128)S(1)}, f32[16,32,512]{2,1,0:T(8,128)}, u32[]{:S(2)}) copy-start(f32[16,32,512]{2,1,0:T(8,128)} %param.14) | copy-start | bytes 3145732
  4.6 10.4 %all-to-all-start = ((bf16[4,256,128]{2,1,0:T(8,128)(2,1)}), bf16[4,256,128]{2,1,0:T(8,128)(2,1)S(1)}, u32[]{:S(2)}, u32[]{:S(2)}) async-start(bf16[4,256,128]{2,1,0:T(8,128)(2,1)} %pad_maximum_fusion.1), calls=%async_computation | async-start | bytes 524288 | tf_op jit(solution)/shard_map/all_to_all | solution.py:154
  15.7 14.7 %all-to-all-start.1 = ((bf16[4,256,128]{2,1,0:T(8,128)(2,1)}), bf16[4,256,128]{2,1,0:T(8,128)(2,1)}, u32[]{:S(2)}, u32[]{:S(2)}) async-start(bf16[4,256,128]{2,1,0:T(8,128)(2,1)} %broadcast_in_dim.20), calls=%async_computation.1 | async-start | bytes 524288 | tf_op jit(solution)/shard_map/all_to_all | solution.py:161
  32.4 48.5 %collective-permute-start.6 = (bf16[128,128]{1,0:T(8,128)(2,1)S(1)}, bf16[128,128]{1,0:T(8,128)(2,1)S(1)}, u32[]{:S(2)}, u32[]{:S(2)}) collective-permute-start(bf16[128,128]{1,0:T(8,128)(2,1)S(1)} %get-tuple-element.29), channel_id=1, source_target_pairs={{0,4},{4,8},{8,12},{12,16},{16,20},{20,24},{24,28},{28,32},{32,36}... | collective-permute-start | bytes 98312 | tf_op jit(solution)/shard_map/ppermute | solution.py:150
  37.6 1.2 copy-start.6
  38.8 66.4 %copy-start.2 = (bf16[512,256]{1,0:T(8,128)(2,1)S(1)}, bf16[512,256]{1,0:T(8,128)(2,1)}, u32[]{:S(2)}) copy-start(bf16[512,256]{1,0:T(8,128)(2,1)} %feats_ref.1) | copy-start | bytes 786436
  38.8 66.4 %copy-start.3 = (bf16[512,256]{1,0:T(8,128)(2,1)S(1)}, bf16[512,256]{1,0:T(8,128)(2,1)}, u32[]{:S(2)}) copy-start(bf16[512,256]{1,0:T(8,128)(2,1)} %rest_10_.1) | copy-start | bytes 786436
  38.8 66.4 %copy-start.4 = (bf16[256,128]{1,0:T(8,128)(2,1)S(1)}, bf16[256,128]{1,0:T(8,128)(2,1)}, u32[]{:S(2)}) copy-start(bf16[256,128]{1,0:T(8,128)(2,1)} %wdown_ref.1) | copy-start | bytes 196612
  38.8 66.4 %copy-start.5 = (s32[1,6,128]{2,0,1:T(1,128)S(1)}, s32[1,6,128]{2,0,1:T(1,128)}, u32[]{:S(2)}) copy-start(s32[1,6,128]{2,0,1:T(1,128)} %param.17) | copy-start | bytes 9220
  60.4 23.5 %collective-permute-start = (bf16[128,128]{1,0:T(8,128)(2,1)S(1)}, bf16[128,128]{1,0:T(8,128)(2,1)S(1)}, u32[]{:S(2)}, u32[]{:S(2)}) collective-permute-start(bf16[128,128]{1,0:T(8,128)(2,1)S(1)} %get-tuple-element.21), channel_id=1, source_target_pairs={{0,508},{4,0},{8,4},{12,8},{16,12},{20,16},{24,20},{28,24},{32,28}... | collective-permute-start | bytes 98312 | tf_op jit(solution)/shard_map/ppermute | solution.py:150
  65.5 20.2 %collective-permute-start.1 = (bf16[128,128]{1,0:T(8,128)(2,1)S(1)}, bf16[128,128]{1,0:T(8,128)(2,1)S(1)}, u32[]{:S(2)}, u32[]{:S(2)}) collective-permute-start(bf16[128,128]{1,0:T(8,128)(2,1)S(1)} %get-tuple-element.22), channel_id=1, source_target_pairs={{0,504},{4,508},{8,0},{12,4},{16,8},{20,12},{24,16},{28,20},{32,24... | collective-permute-start | bytes 98312 | tf_op jit(solution)/shard_map/ppermute | solution.py:150
  74.7 13.0 %collective-permute-start.2 = (bf16[128,128]{1,0:T(8,128)(2,1)S(1)}, bf16[128,128]{1,0:T(8,128)(2,1)S(1)}, u32[]{:S(2)}, u32[]{:S(2)}) collective-permute-start(bf16[128,128]{1,0:T(8,128)(2,1)S(1)} %get-tuple-element.23), channel_id=1, source_target_pairs={{0,500},{4,504},{8,508},{12,0},{16,4},{20,8},{24,12},{28,16},{32,2... | collective-permute-start | bytes 98312 | tf_op jit(solution)/shard_map/ppermute | solution.py:150
  79.0 10.7 %collective-permute-start.3 = (bf16[128,128]{1,0:T(8,128)(2,1)S(1)}, bf16[128,128]{1,0:T(8,128)(2,1)S(1)}, u32[]{:S(2)}, u32[]{:S(2)}) collective-permute-start(bf16[128,128]{1,0:T(8,128)(2,1)S(1)} %get-tuple-element.24), channel_id=1, source_target_pairs={{0,4},{4,8},{8,12},{12,16},{16,20},{20,24},{24,28},{28,32},{32,36}... | collective-permute-start | bytes 98312 | tf_op jit(solution)/shard_map/ppermute | solution.py:150
  80.9 11.4 %collective-permute-start.4 = (bf16[128,128]{1,0:T(8,128)(2,1)S(1)}, bf16[128,128]{1,0:T(8,128)(2,1)S(1)}, u32[]{:S(2)}, u32[]{:S(2)}) collective-permute-start(bf16[128,128]{1,0:T(8,128)(2,1)S(1)} %get-tuple-element.25), channel_id=1, source_target_pairs={{0,8},{4,12},{8,16},{12,20},{16,24},{20,28},{24,32},{28,36},{32,40... | collective-permute-start | bytes 98312 | tf_op jit(solution)/shard_map/ppermute | solution.py:150
  83.8 15.5 %collective-permute-start.5 = (bf16[128,128]{1,0:T(8,128)(2,1)S(1)}, bf16[128,128]{1,0:T(8,128)(2,1)S(1)}, u32[]{:S(2)}, u32[]{:S(2)}) collective-permute-start(bf16[128,128]{1,0:T(8,128)(2,1)S(1)} %get-tuple-element.26), channel_id=1, source_target_pairs={{0,12},{4,16},{8,20},{12,24},{16,28},{20,32},{24,36},{28,40},{32,4... | collective-permute-start | bytes 98312 | tf_op jit(solution)/shard_map/ppermute | solution.py:150
  85.8 20.9 %collective-permute-start.7 = (bf16[128,128]{1,0:T(8,128)(2,1)}, bf16[128,128]{1,0:T(8,128)(2,1)S(1)}, u32[]{:S(2)}, u32[]{:S(2)}) collective-permute-start(bf16[128,128]{1,0:T(8,128)(2,1)} %get-tuple-element.30), channel_id=1, source_target_pairs={{0,8},{4,12},{8,16},{12,20},{16,24},{20,28},{24,32},{28,36},{32,40... | collective-permute-start | bytes 98312 | tf_op jit(solution)/shard_map/ppermute | solution.py:150
  87.7 18.9 %collective-permute-start.8 = (bf16[128,128]{1,0:T(8,128)(2,1)}, bf16[128,128]{1,0:T(8,128)(2,1)S(1)}, u32[]{:S(2)}, u32[]{:S(2)}) collective-permute-start(bf16[128,128]{1,0:T(8,128)(2,1)} %get-tuple-element.31), channel_id=1, source_target_pairs={{0,12},{4,16},{8,20},{12,24},{16,28},{20,32},{24,36},{28,40},{32,4... | collective-permute-start | bytes 98312 | tf_op jit(solution)/shard_map/ppermute | solution.py:150
  89.6 17.0 %collective-permute-start.9 = (bf16[128,128]{1,0:T(8,128)(2,1)}, bf16[128,128]{1,0:T(8,128)(2,1)S(1)}, u32[]{:S(2)}, u32[]{:S(2)}) collective-permute-start(bf16[128,128]{1,0:T(8,128)(2,1)} %get-tuple-element.32), channel_id=1, source_target_pairs={{0,508},{4,0},{8,4},{12,8},{16,12},{20,16},{24,20},{28,24},{32,28}... | collective-permute-start | bytes 98312 | tf_op jit(solution)/shard_map/ppermute | solution.py:150
  92.3 14.3 %collective-permute-start.10 = (bf16[128,128]{1,0:T(8,128)(2,1)}, bf16[128,128]{1,0:T(8,128)(2,1)S(1)}, u32[]{:S(2)}, u32[]{:S(2)}) collective-permute-start(bf16[128,128]{1,0:T(8,128)(2,1)} %get-tuple-element.33), channel_id=1, source_target_pairs={{0,504},{4,508},{8,0},{12,4},{16,8},{20,12},{24,16},{28,20},{32,24... | collective-permute-start | bytes 98312 | tf_op jit(solution)/shard_map/ppermute | solution.py:150
  99.3 7.3 %collective-permute-start.11 = (bf16[128,128]{1,0:T(8,128)(2,1)}, bf16[128,128]{1,0:T(8,128)(2,1)S(1)}, u32[]{:S(2)}, u32[]{:S(2)}) collective-permute-start(bf16[128,128]{1,0:T(8,128)(2,1)} %get-tuple-element.34), channel_id=1, source_target_pairs={{0,500},{4,504},{8,508},{12,0},{16,4},{20,8},{24,12},{28,16},{32,2... | collective-permute-start | bytes 98312 | tf_op jit(solution)/shard_map/ppermute | solution.py:150
  106.7 2.2 %copy-start.1 = (bf16[16,32,512]{0,2,1:T(8,128)(2,1)S(1)}, bf16[16,32,512]{0,2,1:T(8,128)(2,1)}, u32[]{:S(2)}) copy-start(bf16[16,32,512]{0,2,1:T(8,128)(2,1)} %copy.36) | copy-start | bytes 1572868
  108.8 1.2 copy-start.7

commit v2 on v1

v2 whole, which is shorter than its diff:
```python
import math

import jax
import jax.numpy as jnp
from jax import lax
from jax.experimental import pallas as pl
from jax.experimental.pallas import tpu as pltpu
from jax.sharding import Mesh
from jax.sharding import PartitionSpec as P

BF = jnp.bfloat16
F32 = jnp.float32
NT = (((1,), (1,)), ((), ()))
TN = (((0,), (0,)), ((), ()))
DOM = ("zh", "zl", "y", "core")
LANES = 128
BACK_UNROLL = 8
FORE_UNROLL = 4
VMEM_BYTES = 40 << 20
GROUP = 16


def dot(a, b, dims=(((1,), (0,)), ((), ()))):
    return lax.dot_general(a, b, dims, preferred_element_type=F32)


def ones_where(cond):
    return jnp.where(cond, 1.0, 0.0).astype(BF)


def iota(shape, dim):
    return lax.broadcasted_iota(jnp.int32, shape, dim)


def silu_grad(value):
    sigma = jax.nn.sigmoid(value)
    return sigma * (1.0 + value * (1.0 - sigma))


def call(kernel, outs, scratch, flops, which, *args):
    moved_bytes = sum(a.size * a.dtype.itemsize for a in args)
    scalars = [pl.BlockSpec(memory_space=pltpu.SMEM)] if len(which) else []
    return pl.pallas_call(
        kernel,
        in_specs=scalars + [pl.BlockSpec(memory_space=pltpu.VMEM)] * len(args),
        out_shape=outs,
        scratch_shapes=scratch,
        compiler_params=pltpu.CompilerParams(vmem_limit_bytes=VMEM_BYTES),
        cost_estimate=pl.CostEstimate(flops=flops, bytes_accessed=moved_bytes, transcendentals=0),
    )(*([which] if len(which) else []), *args)


def down_kernel(pre_ref, send_ref, down_ref, *out_refs):
    pre = pre_ref[...].astype(F32)
    down = (pre * jax.nn.sigmoid(pre)).astype(BF)
    down_ref[...] = down
    slots = out_refs[0].shape[0]
    edges = down.shape[0]
    for j, out_ref in enumerate(out_refs):
        pick = ones_where(send_ref[j * slots : (j + 1) * slots, :] == iota((slots, edges), 1))
        out_ref[...] = dot(pick, down).astype(BF)


def chunks_swapped(tiles):
    tiles = list(tiles)
    chunk = iota(tiles[0].shape, 1) // GROUP
    for step in (4, 2, 1):
        low = (chunk & step) == 0
        for i in range(8):
            if i & step:
                continue
            a, b = tiles[i], tiles[i + step]
            tiles[i] = jnp.where(low, a, pltpu.roll(b, GROUP * step, 1))
            tiles[i + step] = jnp.where(low, pltpu.roll(a, LANES - GROUP * step, 1), b)
    return tiles


def prep_kernel(basis_ref, count_ref, by_basis_ref, by_trip_ref, live_ref):
    _, basis, _ = by_basis_ref.shape
    _, trips, _ = by_trip_ref.shape
    for t in range(count_ref.shape[1] // LANES):
        lanes = slice(t * LANES, (t + 1) * LANES)
        count = count_ref[:, lanes]
        tall = jnp.broadcast_to(count, (basis, LANES))
        for h in range(trips // 8):
            tiles = []
            for i in range(8 * h, 8 * h + 8):
                at = slice(i * basis, (i + 1) * basis)
                tiles.append(jnp.where(tall > i, basis_ref[at, lanes], 0.0))
                live_ref[at, :] = tiles[-1]
            for q, tile in enumerate(chunks_swapped(tiles)):
                by_basis_ref[8 * t + q, :, h * LANES : (h + 1) * LANES] = tile
        for o in range(basis // 8):
            octet = range(8 * o, 8 * o + 8)
            tiles = [live_ref[pl.ds(b, trips, stride=basis), :] for b in octet]
            for q, tile in enumerate(chunks_swapped(tiles)):
                by_trip_ref[8 * t + q, :, o * LANES : (o + 1) * LANES] = tile


def diagonal(rows):
    count, lanes = rows.shape
    same = iota((GROUP, lanes), 0) == iota((GROUP, lanes), 1) % GROUP
    parts = []
    for r in range(count):
        wide = jnp.broadcast_to(rows[r : r + 1, :], (GROUP, lanes))
        parts.append(jnp.where(same, wide, 0.0).astype(BF))
    return jnp.concatenate(parts, axis=0)


def back_kernel(which_ref, bar_ref, wbil_ref, w_ref, k_ref, own_ref, rem_a_ref, rem_b_ref, grad_ref, acc_ref):
    basis, edges, width = grad_ref.shape
    rows = k_ref.shape[2]
    slots = own_ref.shape[0]
    bar = bar_ref[...]
    for b in range(basis):
        grad_ref[b] = dot(bar, wbil_ref[b * width : (b + 1) * width, :], NT).astype(BF)
    acc_ref[...] = jnp.zeros_like(acc_ref)
    first = which_ref[0] * slots
    row = iota((3 * slots, rows), 0)
    block = row // slots
    jump = jnp.where(block == 0, 0, edges + (block - 1) * 4 * slots - block * slots)
    target = row + jump

    def body(g, carry):
        at = pl.ds(pl.multiple_of(g * GROUP, GROUP), GROUP)
        grad = grad_ref[:, at, :].reshape(basis * GROUP, width)
        d_rows = dot(diagonal(w_ref[g]), grad).astype(BF)
        pick = ones_where(k_ref[g] - first == target)
        acc_ref[...] += dot(pick, d_rows)
        return carry

    lax.fori_loop(0, edges // GROUP, body, 0, unroll=BACK_UNROLL)
    own_ref[...] = acc_ref[:slots, :].astype(BF)
    rem_a_ref[...] = acc_ref[slots : 2 * slots, :].astype(BF)
    rem_b_ref[...] = acc_ref[2 * slots :, :].astype(BF)


def fore_kernel(which_ref, down_ref, in_ref, w_ref, k_ref, wbil_ref, bar_ref, bil_ref, agg_ref, tab_ref, got_ref, sum_ref, all_ref):
    groups, rows, width = got_ref.shape
    basis = all_ref.shape[0]
    own, edges, _ = sum_ref.shape
    trips = k_ref.shape[1]
    tall = tab_ref.shape[0]
    highs = tab_ref.shape[1] // width
    slots = in_ref.shape[1] // 2
    parts = [down_ref[j * slots : (j + 1) * slots, :] for j in range(edges // slots)]
    parts += [in_ref[f, :slots, :] for f in range(4)] + [in_ref[f, slots:, :] for f in range(2)]
    per = tall // slots
    for j, part in enumerate(parts):
        h, p = j // per, j % per
        tab_ref[p * slots : (p + 1) * slots, h * width : (h + 1) * width] = part
    which = which_ref[0]

    def body(g, carry):
        at = pl.ds(pl.multiple_of(g * GROUP, GROUP), GROUP)
        k = k_ref[at, :]
        low, high = k & (tall - 1), k // tall
        lane = iota((GROUP, tall), 1)
        pick = jnp.concatenate([ones_where(low[:, i : i + 1] == lane) for i in range(trips)], axis=0)
        wide = dot(pick, tab_ref[...])
        kept = []
        for i in range(trips):
            part = wide[i * GROUP : (i + 1) * GROUP, :]
            mine = jnp.broadcast_to(high[:, i : i + 1], (GROUP, width))
            value = part[:, :width]
            for h in range(1, highs):
                value = jnp.where(mine == h, part[:, h * width : (h + 1) * width], value)
            kept.append(value.astype(BF))
        got = jnp.concatenate(kept, axis=0)
        got_ref[g] = got
        w = w_ref[g, pl.ds(pl.multiple_of(which * own, own), own), :]
        sum_ref[:, at, :] = dot(diagonal(w), got).astype(BF).reshape(own, GROUP, width)
        return carry

    lax.fori_loop(0, groups, body, 0, unroll=FORE_UNROLL)
    share = agg_ref.shape[0] // GROUP
    for q in range(share):
        g = which * share + q
        total = dot(diagonal(w_ref[g]), got_ref[g]).astype(BF)
        all_ref[:, q * GROUP : (q + 1) * GROUP, :] = total.reshape(basis, GROUP, width)
    agg = jnp.zeros(agg_ref.shape, F32)
    for b in range(0, basis, 2):
        pair = jnp.concatenate([all_ref[b], all_ref[b + 1]], axis=1)
        agg = agg + dot(pair, wbil_ref[b * width : (b + 2) * width, :])
    agg_ref[...] = agg.astype(BF)
    bar = bar_ref[...]
    for j in range(own):
        bil_ref[j * width : (j + 1) * width, :] = dot(sum_ref[j], bar, TN).astype(BF)


def last_kernel(got_ref, pre_ref, send_ref, wdown_ref, cot_ref, feats_ref, grad_ref, term_ref):
    edges, span = cot_ref.shape
    share = edges // got_ref.shape[0]
    width = got_ref.shape[2]
    feats = got_ref.shape[0]
    part = lambda j: [got_ref[f, j * share : (j + 1) * share, :] for f in range(feats)]
    blocks = part(1) + part(2)
    count = send_ref.shape[1] // share
    total = jnp.concatenate(part(0), axis=0).astype(F32)
    place = ones_where(send_ref[...] == iota((edges, count * share), 0))
    total = total + dot(place, jnp.concatenate(blocks[:count], axis=0))
    pre_bar = (total * silu_grad(pre_ref[...].astype(F32))).astype(BF)
    grad_ref[...] = (cot_ref[...].astype(F32) + dot(pre_bar, wdown_ref[...], NT)).astype(BF)
    term_ref[:span, :] = dot(feats_ref[...], pre_bar, TN).astype(BF)
    agg = jnp.concatenate(part(3), axis=0)
    for h in range(span // width):
        up = dot(agg, cot_ref[:, h * width : (h + 1) * width], TN)
        term_ref[span + h * width : span + (h + 1) * width, :] = up.astype(BF)


def moved(value, steps):
    domains, feats = lax.axis_size(DOM), lax.axis_size("feat")
    pairs = [
        (d * feats + f, (d + step) % domains * feats + f)
        for d in range(domains)
        for f, step in enumerate(steps[:feats])
        if step is not None
    ]
    return lax.ppermute(value, (*DOM, "feat"), pairs)


def scattered_sum(pieces, axis):
    arrived = lax.all_to_all(pieces, axis, 0, 0)
    return jnp.sum(arrived.astype(F32), axis=0).astype(BF)


def everywhere(value, axis):
    count = lax.axis_size(axis)
    copies = lax.optimization_barrier(jnp.broadcast_to(value[None], (count, *value.shape)))
    return lax.all_to_all(copies, axis, 0, 0)


def exchanged_sum(value, axis):
    return jnp.sum(everywhere(value, axis).astype(F32), axis=0).astype(BF)


def local(edge_feats, cotangent, w_down, w_up, w_bil, basis, trip_k, trip_count, send_rows):
    edges, span = edge_feats.shape
    width = w_down.shape[1]
    trips, basis_total, _ = basis.shape
    _, blocks, slots = send_rows.shape
    reach = blocks // 2
    offsets = [j + 1 if j < reach else reach - j - 1 for j in range(blocks)]
    feats = lax.axis_size("feat")
    groups = edges // GROUP
    own_basis = basis_total // feats
    low = lambda *shape: jax.ShapeDtypeStruct(shape, BF)
    feat = lax.axis_index("feat").astype(jnp.int32)
    which = feat.reshape(1)
    sends = offsets[:feats], (offsets[feats:] + [None] * feats)[:feats]
    backs = [[None if o is None else -o for o in steps] for steps in sends]

    part_pre = dot(edge_feats, w_down).astype(BF).reshape(feats, edges // feats, width)
    part_bar = dot(cotangent, w_up, NT).astype(BF).reshape(feats, edges // feats, width)
    both = scattered_sum(jnp.concatenate([part_pre, part_bar], axis=1), "feat")
    both = everywhere(both, "feat")
    pre = both[:, : edges // feats].reshape(edges, width)
    bar = both[:, edges // feats :].reshape(edges, width)

    by_basis, by_trip = call(
        prep_kernel,
        [
            jax.ShapeDtypeStruct((groups, basis_total, trips * GROUP), F32),
            jax.ShapeDtypeStruct((groups, trips, basis_total * GROUP), F32),
        ],
        [pltpu.VMEM((trips * basis_total, LANES), F32)],
        1 << 28,
        (),
        basis.reshape(trips * basis_total, edges),
        trip_count.reshape(1, edges),
    )
    k_rows = trip_k.T.reshape(trips, groups, GROUP).transpose(1, 0, 2).reshape(groups, 1, -1)

    second = jnp.minimum(feats + feat, blocks - 1)
    listed = jnp.concatenate([send_rows[0, feat], send_rows[0, second]]).reshape(-1, 1)
    down, out_a, out_b = call(
        down_kernel,
        [low(edges, width), low(slots, width), low(slots, width)],
        [],
        4 * slots * edges * width,
        (),
        pre,
        listed,
    )
    in_a, in_b = moved(out_a, sends[0]), moved(out_b, sends[1])

    table = edges + blocks * slots
    big = 2 * edges * trips * width * 2000
    own, rem_a, rem_b = call(
        back_kernel,
        [low(slots, width)] * 3,
        [
            pltpu.VMEM((basis_total, edges, width), BF),
            pltpu.VMEM((3 * slots, width), F32),
        ],
        big,
        which,
        bar,
        w_bil,
        by_trip,
        k_rows,
    )
    back_a, back_b = moved(rem_a, backs[0]), moved(rem_b, backs[1])

    incoming, own = lax.optimization_barrier((jnp.concatenate([in_a, in_b], axis=0), own))
    incoming = everywhere(incoming, "feat")
    tall = 2 * slots
    bil, agg = call(
        fore_kernel,
        [low(own_basis * width, width), low(edges // feats, width)],
        [
            pltpu.VMEM((tall, table // tall * width), BF),
            pltpu.VMEM((groups, trips * GROUP, width), BF),
            pltpu.VMEM((own_basis, edges, width), BF),
            pltpu.VMEM((basis_total, edges // feats, width), BF),
        ],
        big,
        which,
        down,
        incoming,
        by_basis,
        trip_k,
        w_bil,
        bar,
    )
    shared = everywhere(jnp.concatenate([own, back_a, back_b, agg], axis=0), "feat")
    input_grad, terms = call(
        last_kernel,
        [low(edges, span), low(2 * span, width)],
        [],
        2 * edges * width * (blocks * slots + 3 * span),
        (),
        shared,
        pre,
        send_rows.reshape(1, -1),
        w_down,
        cotangent,
        edge_feats,
    )

    near = ("y", "core")
    count = lax.axis_size(near)
    bil = bil.reshape(count, -1, width)
    terms = terms.reshape(count, -1, width)
    split = bil.shape[1]
    total = scattered_sum(jnp.concatenate([bil, terms], axis=1), near)
    total = exchanged_sum(total, "zl")
    total = exchanged_sum(total, "zh")
    total = everywhere(total, near)
    factor = 1.0 / math.sqrt(edges * lax.axis_size(DOM))
    bil = total[:, :split].reshape(-1, width).astype(F32) * factor
    terms = total[:, split:].reshape(-1, width).astype(F32) * factor
    up = jnp.concatenate([terms[span : span + width], terms[span + width :]], axis=1)
    return input_grad, terms[:span], up, bil


def solution(mesh):
    fine = Mesh(mesh.devices.reshape(4, 4, 4, 2, 4), (*DOM, "feat"))
    return jax.shard_map(
        local,
        mesh=fine,
        in_specs=(
            P(DOM, "feat"),
            P(DOM, "feat"),
            P("feat", None),
            P(None, "feat"),
            P(),
            P(None, None, DOM),
            P(DOM, None),
            P(DOM),
            P(DOM, None, None),
        ),
        out_specs=(P(DOM, "feat"), P("feat", None), P(None, "feat"), P("feat", None)),
        check_vma=False,
    )
```

time: 196 us -> 153 us (0.78)
  starting transfers between devices: 57.9 us -> 33.5 us
  Pallas kernels: 48.7 us -> 26.3 us
  blocking collectives: 57.9 us -> 71.6 us
  local copies, waits for them, and re-layouts: 21.5 us -> 9.45 us
  waiting for transfers between devices: 2.65 us -> 6.35 us
    ppermute x12 -> x4, starting transfers between devices: 49 us -> 20.2 us  [moved(): return lax.ppermute(value, (*DOM, 'feat'), pairs)]
    pallas_call x4 -> x5, Pallas kernels: 48.7 us -> 26.3 us  [call(): pl.pallas_call(kernel, in_specs=scalars + [pl.BlockSpec(memory_space=pltp...]
    all_to_all x3 -> x4, blocking collectives: 47.9 us -> 58.7 us  [everywhere(): return lax.all_to_all(copies, axis, 0, 0)]
    transpose x1 -> x0, local copies, waits for them, and re-layouts: 7.23 us -> none  [local(): w_back = weights.transpose(0, 2, 1)]
    all_to_all x1 -> x2, starting transfers between devices: 4.06 us -> 8.47 us  [everywhere(): return lax.all_to_all(copies, axis, 0, 0)]
    select_n x1 -> x0, local copies, waits for them, and re-layouts: 3.19 us -> none  [local(): weights = jnp.where(live[:, None, :], basis, 0.0).astype(BF)]
    all_to_all x1, waiting for transfers between devices: 2.62 us -> 5.53 us  [scattered_sum(): arrived = lax.all_to_all(pieces, axis, 0, 0)]
    all_to_all x1, blocking collectives: 10 us -> 12.9 us  [scattered_sum(): arrived = lax.all_to_all(pieces, axis, 0, 0)]
  transfers between devices with their start and end apart: 14 -> 7, of which waited for: 1 -> 2; matrix products, arithmetic and copies ran while one was open for 7% -> 0% of each run, Pallas kernels for 12% -> 16%
where the time goes in v2:
time: 153 us; the launch traced here: 152 us
  blocking collectives  71.6 us (47%)
  starting transfers between devices  33.5 us (22%)
  Pallas kernels  26.3 us (17%)
  local copies, waits for them, and re-layouts  9.45 us (6%)
  waiting for transfers between devices  6.35 us (4%)
  other arithmetic  2.46 us (2%)
    all_to_all x4, blocking collectives, everywhere(): return lax.all_to_all(copies, axis, 0, 0)  58.7 us
    pallas_call x5, Pallas kernels, call(): pl.pallas_call(kernel, in_specs=scalars + [pl.BlockSpec(memory_space=pltp...  26.3 us
    ppermute x4, starting transfers between devices, moved(): return lax.ppermute(value, (*DOM, 'feat'), pairs)  20.2 us
    all_to_all x1, blocking collectives, scattered_sum(): arrived = lax.all_to_all(pieces, axis, 0, 0)  12.9 us
    all_to_all x2, starting transfers between devices, everywhere(): return lax.all_to_all(copies, axis, 0, 0)  8.47 us
    unnamed x27, local copies, waits for them, and re-layouts  6.64 us
    all_to_all x1, waiting for transfers between devices, scattered_sum(): arrived = lax.all_to_all(pieces, axis, 0, 0)  5.53 us
    all_to_all x1, starting transfers between devices, scattered_sum(): arrived = lax.all_to_all(pieces, axis, 0, 0)  4.82 us
  transfers between devices with their start and end apart: 7, of which 2 were waited for; matrix products, arithmetic and copies ran while one was open for 0% of the time, Pallas kernels for 16%

profile of v2, /device:TPU:1, one launch (start us, length us, event | category | flops | bytes accessed | tf_op | source)
XLA Modules:
  0.0 152.0 jit_solution(10374328242369046165)
XLA Ops:
  0.6 0.0 copy-start
  0.6 0.0 copy-start.4
  0.7 0.0 copy-start.3
  0.7 0.8 copy-done
  1.5 1.2 convolution_convert_fusion
  2.7 0.0 copy-done.4
  2.7 0.0 copy-done.3
  2.7 0.2 convolution_convert_fusion.1
  2.9 0.7 pad_maximum_fusion.1
  3.6 4.8 %all-to-all-start = ((bf16[4,256,128]{2,1,0:T(8,128)(2,1)}), bf16[4,256,128]{2,1,0:T(8,128)(2,1)S(1)}, u32[]{:S(2)}, u32[]{:S(2)}) async-start(bf16[4,256,128]{2,1,0:T(8,128)(2,1)} %pad_maximum_fusion.1), calls=%async_computation | async-start | bytes 524288 | tf_op jit(solution)/shard_map/all_to_all | solution.py:223
  8.4 0.0 copy-start.1
  8.4 5.5 %all-to-all-done = bf16[4,256,128]{2,1,0:T(8,128)(2,1)S(1)} async-done(((bf16[4,256,128]{2,1,0:T(8,128)(2,1)}), bf16[4,256,128]{2,1,0:T(8,128)(2,1)S(1)}, u32[]{:S(2)}, u32[]{:S(2)}) %all-to-all-start) | async-done | bytes 262176 | tf_op jit(solution)/shard_map/all_to_all | solution.py:223
  14.0 0.7 broadcast_in_dim.12
  14.8 3.5 %all-to-all-start.1 = ((bf16[4,256,128]{2,1,0:T(8,128)(2,1)}), bf16[4,256,128]{2,1,0:T(8,128)(2,1)S(1)}, u32[]{:S(2)}, u32[]{:S(2)}) async-start(bf16[4,256,128]{2,1,0:T(8,128)(2,1)} %broadcast_in_dim.12), calls=%async_computation.1 | async-start | bytes 524288 | tf_op jit(solution)/shard_map/all_to_all | solution.py:230
  18.3 0.0 copy-done.5
  18.3 0.0 copy-start.12
  18.4 0.1 copy.19.send_ref
  18.5 0.6 copy-done.12
  19.1 0.1 reshape.72
  19.2 0.1 copy.20
  19.4 0.1 copy.21.k_ref
  19.4 0.0 copy-start.6
  19.5 0.0 copy-start.7
  19.5 0.0 copy-done.1
  19.5 0.7 copy-done.6
  20.1 4.1 %shard_map.121 = (f32[32,32,256]{2,1,0:T(8,128)S(1)}, f32[32,16,512]{2,1,0:T(8,128)S(1)}) custom-call(f32[512,512]{1,0:T(8,128)S(1)} %bitcast.28, s32[1,512]{1,0:T(1,128)S(1)} %bitcast.34), custom_call_target="tpu_custom_call" | custom-call | flops 268435456 | bytes 1050624 | tf_op jit(solution)/shard_map/pallas_call | solution.py:43
  24.2 0.0 copy-start.8
  24.2 1.0 copy-done.8
  25.2 0.0 copy-start.10
  25.2 1.0 copy-done.10
  26.2 0.0 all-to-all-done.1
  26.2 0.3 shard_map.120
  26.5 5.2 %collective-permute-start = (bf16[128,128]{1,0:T(8,128)(2,1)S(1)}, bf16[128,128]{1,0:T(8,128)(2,1)S(1)}, u32[]{:S(2)}, u32[]{:S(2)}) collective-permute-start(bf16[128,128]{1,0:T(8,128)(2,1)S(1)} %get-tuple-element.18), channel_id=1, source_target_pairs={{0,4},{1,9},{2,14},{3,511},{4,8},{5,13},{6,18},{7,3},{8,12},{9,17}... | collective-permute-start | bytes 98312 | tf_op jit(solution)/shard_map/ppermute | solution.py:219
  31.7 10.3 %collective-permute-start.1 = (bf16[128,128]{1,0:T(8,128)(2,1)S(1)}, bf16[128,128]{1,0:T(8,128)(2,1)S(1)}, u32[]{:S(2)}, u32[]{:S(2)}) collective-permute-start(bf16[128,128]{1,0:T(8,128)(2,1)S(1)} %get-tuple-element.19), channel_id=1, source_target_pairs={{0,504},{1,501},{4,508},{5,505},{8,0},{9,509},{12,4},{13,1},{16,8}... | collective-permute-start | bytes 98312 | tf_op jit(solution)/shard_map/ppermute | solution.py:219
  42.0 0.0 copy-done.7
  42.0 0.0 copy-start.11
  42.0 1.2 copy-done.11
  43.3 8.3 %shard_map.122 = (bf16[128,128]{1,0:T(8,128)(2,1)S(1)}, bf16[128,128]{1,0:T(8,128)(2,1)S(1)}, bf16[128,128]{1,0:T(8,128)(2,1)S(1)}) custom-call(s32[1]{0:T(128)} %bitcast.6.which_ref, bf16[512,128]{1,0:T(8,128)(2,1)S(1)} %bitcast.30, bf16[4096,128]{1,0:T(8,128)(2,1)S(1)} %copy-done.7, f32[32,16,512]{2,1,0:T(8,128)S(1)} %copy-done.11, ...), custom_call_target="tpu_custom_call" | custom-call | flops 4194304000 | bytes 2260992 | tf_op jit(solution)/shard_map/pallas_call | solution.py:43
  51.5 0.0 collective-permute-done
  51.6 0.0 collective-permute-done.1
  51.6 0.7 broadcast_in_dim.13
  52.3 4.9 %all-to-all-start.2 = ((bf16[4,256,128]{2,1,0:T(8,128)(2,1)}), bf16[4,256,128]{2,1,0:T(8,128)(2,1)S(1)}, u32[]{:S(2)}, u32[]{:S(2)}) async-start(bf16[4,256,128]{2,1,0:T(8,128)(2,1)} %broadcast_in_dim.13), calls=%async_computation.2 | async-start | bytes 524288 | tf_op jit(solution)/shard_map/all_to_all | solution.py:230
  57.2 0.1 copy.22.k_ref
  57.4 2.8 %collective-permute-start.2 = (bf16[128,128]{1,0:T(8,128)(2,1)S(1)}, bf16[128,128]{1,0:T(8,128)(2,1)S(1)}, u32[]{:S(2)}, u32[]{:S(2)}) collective-permute-start(bf16[128,128]{1,0:T(8,128)(2,1)S(1)} %get-tuple-element.23), channel_id=1, source_target_pairs={{0,508},{1,505},{2,502},{3,7},{4,0},{5,509},{6,506},{7,11},{8,4},{... | collective-permute-start | bytes 98312 | tf_op jit(solution)/shard_map/ppermute | solution.py:219
  60.2 1.9 %collective-permute-start.3 = (bf16[128,128]{1,0:T(8,128)(2,1)S(1)}, bf16[128,128]{1,0:T(8,128)(2,1)S(1)}, u32[]{:S(2)}, u32[]{:S(2)}) collective-permute-start(bf16[128,128]{1,0:T(8,128)(2,1)S(1)} %get-tuple-element.24), channel_id=1, source_target_pairs={{0,8},{1,13},{4,12},{5,17},{8,16},{9,21},{12,20},{13,25},{16,24},{... | collective-permute-start | bytes 98312 | tf_op jit(solution)/shard_map/ppermute | solution.py:219
  62.1 0.8 all-to-all-done.2.in_ref
  62.9 1.2 copy-done.9
  64.1 12.4 %shard_map.123 = (bf16[1024,128]{1,0:T(8,128)(2,1)S(1)}, bf16[128,128]{1,0:T(8,128)(2,1)S(1)}) custom-call(s32[1]{0:T(128)} %bitcast.6.which_ref, bf16[512,128]{1,0:T(8,128)(2,1)S(1)} %get-tuple-element.25.down_ref, bf16[4,256,128]{2,1,0:T(8,128)(2,1)S(1)} %all-to-all-done.2.in_ref, f32[32,32,256]{2,1,0:T(8,128)S(1)} %copy-done.9, ...), custom_call_target="tpu_custom_call" | custom-call | flops 4194304000 | bytes 2654208 | tf_op jit(solution)/shard_map/pallas_call | solution.py:43
  76.5 0.0 collective-permute-done.2
  76.5 0.0 collective-permute-done.3
  76.5 0.1 broadcast_in_dim.14
  76.6 0.0 copy-start.2
  76.6 11.7 %all_to_all.40.got_ref = bf16[4,512,128]{2,1,0:T(8,128)(2,1)S(1)} all-to-all(bf16[4,512,128]{2,1,0:T(8,128)(2,1)S(1)} %broadcast_in_dim.14), channel_id=1, replica_groups=mesh['zh'=4,'zl'=4,'y'=4,'core'=2,'feat'=4] {'feat'}, dimensions={0} | all-to-all | bytes 1048576 | tf_op jit(solution)/shard_map/all_to_all | solution.py:230
  88.3 0.0 copy-done.2
  88.3 1.3 shard_map.124
  89.6 12.9 %all_to_all.41 = bf16[8,192,128]{2,1,0:T(8,128)(2,1)S(1)} all-to-all(bf16[8,192,128]{2,1,0:T(8,128)(2,1)S(1)} %pad_maximum_fusion), channel_id=1, replica_groups=mesh['zh'=4,'zl'=4,'y'=4,'core'=2,'feat'=4] {'y','core'}, dimensions={0} | all-to-all | bytes 786432 | tf_op jit(solution)/shard_map/all_to_all | solution.py:223
  102.5 0.1 reduce_sum.49
  102.6 8.0 %all_to_all.42 = bf16[4,192,128]{2,1,0:T(8,128)(2,1)S(1)} all-to-all(bf16[4,192,128]{2,1,0:T(8,128)(2,1)S(1)} %broadcast_in_dim.15), channel_id=1, replica_groups=mesh['zh'=4,'zl'=4,'y'=4,'core'=2,'feat'=4] {'zl'}, dimensions={0} | all-to-all | bytes 393216 | tf_op jit(solution)/shard_map/all_to_all | solution.py:230
  110.7 25.0 %all_to_all.43 = bf16[4,192,128]{2,1,0:T(8,128)(2,1)S(1)} all-to-all(bf16[4,192,128]{2,1,0:T(8,128)(2,1)S(1)} %broadcast_in_dim.16), channel_id=1, replica_groups=mesh['zh'=4,'zl'=4,'y'=4,'core'=2,'feat'=4] {'zh'}, dimensions={0} | all-to-all | bytes 393216 | tf_op jit(solution)/shard_map/all_to_all | solution.py:230
  135.7 0.1 broadcast_in_dim.17
  135.8 14.0 %all_to_all.44 = bf16[8,192,128]{2,1,0:T(8,128)(2,1)S(1)} all-to-all(bf16[8,192,128]{2,1,0:T(8,128)(2,1)S(1)} %broadcast_in_dim.17), channel_id=1, replica_groups=mesh['zh'=4,'zl'=4,'y'=4,'core'=2,'feat'=4] {'y','core'}, dimensions={0} | all-to-all | bytes 786432 | tf_op jit(solution)/shard_map/all_to_all | solution.py:230
  149.8 0.7 slice.43
  150.5 0.7 pad_maximum_fusion.3
  151.2 0.8 convert_multiply_fusion
  (15 shorter events, 0.3 us)
Async XLA Ops:
  0.6 0.8 copy-start
  0.6 2.0 %copy-start.4 = (bf16[256,128]{1,0:T(8,128)(2,1)S(1)}, bf16[256,128]{1,0:T(8,128)(2,1)}, u32[]{:S(2)}) copy-start(bf16[256,128]{1,0:T(8,128)(2,1)} %wdown_ref.1) | copy-start | bytes 196612
  0.7 2.0 %copy-start.3 = (bf16[512,256]{1,0:T(8,128)(2,1)S(1)}, bf16[512,256]{1,0:T(8,128)(2,1)}, u32[]{:S(2)}) copy-start(bf16[512,256]{1,0:T(8,128)(2,1)} %feats_ref.1) | copy-start | bytes 786436
  3.6 10.4 %all-to-all-start = ((bf16[4,256,128]{2,1,0:T(8,128)(2,1)}), bf16[4,256,128]{2,1,0:T(8,128)(2,1)S(1)}, u32[]{:S(2)}, u32[]{:S(2)}) async-start(bf16[4,256,128]{2,1,0:T(8,128)(2,1)} %pad_maximum_fusion.1), calls=%async_computation | async-start | bytes 524288 | tf_op jit(solution)/shard_map/all_to_all | solution.py:223
  8.4 11.0 %copy-start.1 = (f32[16,32,512]{2,1,0:T(8,128)S(1)}, f32[16,32,512]{2,1,0:T(8,128)}, u32[]{:S(2)}) copy-start(f32[16,32,512]{2,1,0:T(8,128)} %param.14) | copy-start | bytes 3145732
  14.8 3.6 %copy-start.5 = (s32[1,6,128]{2,0,1:T(1,128)S(1)}, s32[1,6,128]{2,0,1:T(1,128)}, u32[]{:S(2)}) copy-start(s32[1,6,128]{2,0,1:T(1,128)} %param.17) | copy-start | bytes 9220
  14.8 11.4 %all-to-all-start.1 = ((bf16[4,256,128]{2,1,0:T(8,128)(2,1)}), bf16[4,256,128]{2,1,0:T(8,128)(2,1)S(1)}, u32[]{:S(2)}, u32[]{:S(2)}) async-start(bf16[4,256,128]{2,1,0:T(8,128)(2,1)} %broadcast_in_dim.12), calls=%async_computation.1 | async-start | bytes 524288 | tf_op jit(solution)/shard_map/all_to_all | solution.py:230
  18.3 0.8 copy-start.12
  19.4 0.7 copy-start.6
  19.5 22.6 %copy-start.7 = (bf16[4096,128]{1,0:T(8,128)(2,1)S(1)}, bf16[4096,128]{1,0:T(8,128)(2,1)}, u32[]{:S(2)}) copy-start(bf16[4096,128]{1,0:T(8,128)(2,1)} %wbil_ref.3) | copy-start | bytes 3145732
  24.2 1.0 copy-start.8
  25.2 1.0 copy-start.10
  26.5 25.1 %collective-permute-start = (bf16[128,128]{1,0:T(8,128)(2,1)S(1)}, bf16[128,128]{1,0:T(8,128)(2,1)S(1)}, u32[]{:S(2)}, u32[]{:S(2)}) collective-permute-start(bf16[128,128]{1,0:T(8,128)(2,1)S(1)} %get-tuple-element.18), channel_id=1, source_target_pairs={{0,4},{1,9},{2,14},{3,511},{4,8},{5,13},{6,18},{7,3},{8,12},{9,17}... | collective-permute-start | bytes 98312 | tf_op jit(solution)/shard_map/ppermute | solution.py:219
  31.7 19.9 %collective-permute-start.1 = (bf16[128,128]{1,0:T(8,128)(2,1)S(1)}, bf16[128,128]{1,0:T(8,128)(2,1)S(1)}, u32[]{:S(2)}, u32[]{:S(2)}) collective-permute-start(bf16[128,128]{1,0:T(8,128)(2,1)S(1)} %get-tuple-element.19), channel_id=1, source_target_pairs={{0,504},{1,501},{4,508},{5,505},{8,0},{9,509},{12,4},{13,1},{16,8}... | collective-permute-start | bytes 98312 | tf_op jit(solution)/shard_map/ppermute | solution.py:219
  42.0 1.2 copy-start.11
  52.3 10.6 %all-to-all-start.2 = ((bf16[4,256,128]{2,1,0:T(8,128)(2,1)}), bf16[4,256,128]{2,1,0:T(8,128)(2,1)S(1)}, u32[]{:S(2)}, u32[]{:S(2)}) async-start(bf16[4,256,128]{2,1,0:T(8,128)(2,1)} %broadcast_in_dim.13), calls=%async_computation.2 | async-start | bytes 524288 | tf_op jit(solution)/shard_map/all_to_all | solution.py:230
  57.4 19.1 %collective-permute-start.2 = (bf16[128,128]{1,0:T(8,128)(2,1)S(1)}, bf16[128,128]{1,0:T(8,128)(2,1)S(1)}, u32[]{:S(2)}, u32[]{:S(2)}) collective-permute-start(bf16[128,128]{1,0:T(8,128)(2,1)S(1)} %get-tuple-element.23), channel_id=1, source_target_pairs={{0,508},{1,505},{2,502},{3,7},{4,0},{5,509},{6,506},{7,11},{8,4},{... | collective-permute-start | bytes 98312 | tf_op jit(solution)/shard_map/ppermute | solution.py:219
  60.2 16.4 %collective-permute-start.3 = (bf16[128,128]{1,0:T(8,128)(2,1)S(1)}, bf16[128,128]{1,0:T(8,128)(2,1)S(1)}, u32[]{:S(2)}, u32[]{:S(2)}) collective-permute-start(bf16[128,128]{1,0:T(8,128)(2,1)S(1)} %get-tuple-element.24), channel_id=1, source_target_pairs={{0,8},{1,13},{4,12},{5,17},{8,16},{9,21},{12,20},{13,25},{16,24},{... | collective-permute-start | bytes 98312 | tf_op jit(solution)/shard_map/ppermute | solution.py:219
  62.9 1.2 copy-start.9
  76.6 11.7 %copy-start.2 = (bf16[512,256]{1,0:T(8,128)(2,1)S(1)}, bf16[512,256]{1,0:T(8,128)(2,1)}, u32[]{:S(2)}) copy-start(bf16[512,256]{1,0:T(8,128)(2,1)} %cot_ref.1) | copy-start | bytes 786436

commit v3 on v2

--- a/solution.py
+++ b/solution.py
@@ -1,3 +1,4 @@
+import functools
 import math
 
 import jax
@@ -15,8 +16,10 @@
 DOM = ("zh", "zl", "y", "core")
 LANES = 128
 BACK_UNROLL = 8
-FORE_UNROLL = 4
-VMEM_BYTES = 40 << 20
+GATHER_UNROLL = 2
+SUM_UNROLL = 4
+PAIR = 4
+VMEM_BYTES = 20 << 20
 GROUP = 16
 
 
@@ -37,25 +40,34 @@
     return sigma * (1.0 + value * (1.0 - sigma))
 
 
-def call(kernel, outs, scratch, flops, which, *args):
+def call(kernel, outs, scratch, flops, which, *args, late=()):
     moved_bytes = sum(a.size * a.dtype.itemsize for a in args)
     scalars = [pl.BlockSpec(memory_space=pltpu.SMEM)] if len(which) else []
     return pl.pallas_call(
         kernel,
-        in_specs=scalars + [pl.BlockSpec(memory_space=pltpu.VMEM)] * len(args),
+        in_specs=scalars
+        + [pl.BlockSpec(memory_space=pltpu.VMEM)] * len(args)
+        + [pl.BlockSpec(memory_space=pltpu.HBM)] * len(late),
         out_shape=outs,
-        scratch_shapes=scratch,
+        scratch_shapes=scratch
+        + [pltpu.VMEM(a.shape, a.dtype) for a in late]
+        + [pltpu.SemaphoreType.DMA] * len(late),
         compiler_params=pltpu.CompilerParams(vmem_limit_bytes=VMEM_BYTES),
         cost_estimate=pl.CostEstimate(flops=flops, bytes_accessed=moved_bytes, transcendentals=0),
-    )(*([which] if len(which) else []), *args)
-
-
-def down_kernel(pre_ref, send_ref, down_ref, *out_refs):
-    pre = pre_ref[...].astype(F32)
+    )(*([which] if len(which) else []), *args, *(pltpu.with_memory_space_constraint(a, pltpu.HBM) for a in late))
+
+
+def down_kernel(both_ref, send_ref, pre_ref, bar_ref, down_ref, *out_refs):
+    edges = pre_ref.shape[0]
+    pre, bar = both_ref[0, :edges, :].astype(F32), both_ref[0, edges:, :].astype(F32)
+    for f in range(1, both_ref.shape[0]):
+        pre = pre + both_ref[f, :edges, :].astype(F32)
+        bar = bar + both_ref[f, edges:, :].astype(F32)
+    pre_ref[...] = pre
+    bar_ref[...] = bar.astype(BF)
     down = (pre * jax.nn.sigmoid(pre)).astype(BF)
     down_ref[...] = down
     slots = out_refs[0].shape[0]
-    edges = down.shape[0]
     for j, out_ref in enumerate(out_refs):
         pick = ones_where(send_ref[j * slots : (j + 1) * slots, :] == iota((slots, edges), 1))
         out_ref[...] = dot(pick, down).astype(BF)
@@ -107,12 +119,39 @@
     return jnp.concatenate(parts, axis=0)
 
 
-def back_kernel(which_ref, bar_ref, wbil_ref, w_ref, k_ref, own_ref, rem_a_ref, rem_b_ref, grad_ref, acc_ref):
+def back_kernel(
+    which_ref,
+    bar_ref,
+    k_ref,
+    w_far,
+    wbil_far,
+    own_ref,
+    rem_a_ref,
+    rem_b_ref,
+    grad_ref,
+    acc_ref,
+    part_sems,
+    w_ref,
+    wbil_ref,
+    w_sem,
+    _,
+):
     basis, edges, width = grad_ref.shape
     rows = k_ref.shape[2]
     slots = own_ref.shape[0]
+    fetch = pltpu.make_async_copy(w_far, w_ref, w_sem)
+    parts = part_sems.shape[0]
+    some = wbil_ref.shape[0] // parts
+    fetch_parts = []
+    for p in range(parts):
+        at = pl.ds(p * some, some)
+        fetch_parts.append(pltpu.make_async_copy(wbil_far.at[at], wbil_ref.at[at], part_sems.at[p]))
+        fetch_parts[p].start()
+    fetch.start()
     bar = bar_ref[...]
     for b in range(basis):
+        if b % (basis // parts) == 0:
+            fetch_parts[b // (basis // parts)].wait()
         grad_ref[b] = dot(bar, wbil_ref[b * width : (b + 1) * width, :], NT).astype(BF)
     acc_ref[...] = jnp.zeros_like(acc_ref)
     first = which_ref[0] * slots
@@ -120,12 +159,14 @@
     block = row // slots
     jump = jnp.where(block == 0, 0, edges + (block - 1) * 4 * slots - block * slots)
     target = row + jump
+    fetch.wait()
 
     def body(g, carry):
         at = pl.ds(pl.multiple_of(g * GROUP, GROUP), GROUP)
         grad = grad_ref[:, at, :].reshape(basis * GROUP, width)
         d_rows = dot(diagonal(w_ref[g]), grad).astype(BF)
-        pick = ones_where(k_ref[g] - first == target)
+        k = jnp.broadcast_to(k_ref[g] - first, target.shape).astype(jnp.int16)
+        pick = jnp.where(k == target.astype(jnp.int16), jnp.ones((), BF), jnp.zeros((), BF))
         acc_ref[...] += dot(pick, d_rows)
         return carry
 
@@ -135,63 +176,88 @@
     rem_b_ref[...] = acc_ref[2 * slots :, :].astype(BF)
 
 
-def fore_kernel(which_ref, down_ref, in_ref, w_ref, k_ref, wbil_ref, bar_ref, bil_ref, agg_ref, tab_ref, got_ref, sum_ref, all_ref):
+def fore_kernel(
+    which_ref,
+    down_ref,
+    in_ref,
+    k_ref,
+    bar_ref,
+    w_far,
+    wbil_far,
+    cot_far,
+    term_ref,
+    tab_ref,
+    got_ref,
+    sum_ref,
+    w_ref,
+    wbil_ref,
+    cot_ref,
+    w_sem,
+    wbil_sem,
+    cot_sem,
+):
+    fetch_w = pltpu.make_async_copy(w_far, w_ref, w_sem)
+    fetch_wbil = pltpu.make_async_copy(wbil_far, wbil_ref, wbil_sem)
+    fetch_cot = pltpu.make_async_copy(cot_far, cot_ref, cot_sem)
+    fetch_w.start()
+    fetch_wbil.start()
+    fetch_cot.start()
     groups, rows, width = got_ref.shape
-    basis = all_ref.shape[0]
-    own, edges, _ = sum_ref.shape
+    basis, edges, _ = sum_ref.shape
     trips = k_ref.shape[1]
     tall = tab_ref.shape[0]
     highs = tab_ref.shape[1] // width
     slots = in_ref.shape[1] // 2
     parts = [down_ref[j * slots : (j + 1) * slots, :] for j in range(edges // slots)]
     parts += [in_ref[f, :slots, :] for f in range(4)] + [in_ref[f, slots:, :] for f in range(2)]
-    per = tall // slots
+    highs, tall = 1, tab_ref.shape[0]
     for j, part in enumerate(parts):
-        h, p = j // per, j % per
-        tab_ref[p * slots : (p + 1) * slots, h * width : (h + 1) * width] = part
-    which = which_ref[0]
-
-    def body(g, carry):
+        tab_ref[j * slots : (j + 1) * slots, :] = part
+
+    def gather(n, carry):
+        lane = iota((GROUP, tall * highs), 1).astype(jnp.int16)
+        for j in range(PAIR):
+            g = n * PAIR + j
+            at = pl.ds(pl.multiple_of(g * GROUP, GROUP), GROUP)
+            k = k_ref[at, :].astype(jnp.int16)
+            picks = [
+                jnp.where(k[:, i : i + 1] == lane, jnp.ones((), BF), jnp.zeros((), BF))
+                for i in range(trips)
+            ]
+            got_ref[g] = dot(jnp.concatenate(picks, axis=0), tab_ref[...]).astype(BF)
+        return carry
+
+    lax.fori_loop(0, groups // PAIR, gather, 0, unroll=GATHER_UNROLL)
+
+    fetch_w.wait()
+
+    def add_up(g, carry):
         at = pl.ds(pl.multiple_of(g * GROUP, GROUP), GROUP)
-        k = k_ref[at, :]
-        low, high = k & (tall - 1), k // tall
-        lane = iota((GROUP, tall), 1)
-        pick = jnp.concatenate([ones_where(low[:, i : i + 1] == lane) for i in range(trips)], axis=0)
-        wide = dot(pick, tab_ref[...])
-        kept = []
-        for i in range(trips):
-            part = wide[i * GROUP : (i + 1) * GROUP, :]
-            mine = jnp.broadcast_to(high[:, i : i + 1], (GROUP, width))
-            value = part[:, :width]
-            for h in range(1, highs):
-                value = jnp.where(mine == h, part[:, h * width : (h + 1) * width], value)
-            kept.append(value.astype(BF))
-        got = jnp.concatenate(kept, axis=0)
-        got_ref[g] = got
-        w = w_ref[g, pl.ds(pl.multiple_of(which * own, own), own), :]
-        sum_ref[:, at, :] = dot(diagonal(w), got).astype(BF).reshape(own, GROUP, width)
+        total = dot(diagonal(w_ref[g]), got_ref[g]).astype(BF)
+        sum_ref[:, at, :] = total.reshape(basis, GROUP, width)
         return carry
 
-    lax.fori_loop(0, groups, body, 0, unroll=FORE_UNROLL)
-    share = agg_ref.shape[0] // GROUP
-    for q in range(share):
-        g = which * share + q
-        total = dot(diagonal(w_ref[g]), got_ref[g]).astype(BF)
-        all_ref[:, q * GROUP : (q + 1) * GROUP, :] = total.reshape(basis, GROUP, width)
-    agg = jnp.zeros(agg_ref.shape, F32)
+    lax.fori_loop(0, groups, add_up, 0, unroll=SUM_UNROLL)
+    fetch_wbil.wait()
+    fetch_cot.wait()
+    agg = jnp.zeros((edges, width), F32)
     for b in range(0, basis, 2):
-        pair = jnp.concatenate([all_ref[b], all_ref[b + 1]], axis=1)
+        pair = jnp.concatenate([sum_ref[b], sum_ref[b + 1]], axis=1)
         agg = agg + dot(pair, wbil_ref[b * width : (b + 2) * width, :])
-    agg_ref[...] = agg.astype(BF)
+    agg = agg.astype(BF)
     bar = bar_ref[...]
+    own = term_ref.shape[0] // width - cot_ref.shape[1] // width
     for j in range(own):
-        bil_ref[j * width : (j + 1) * width, :] = dot(sum_ref[j], bar, TN).astype(BF)
+        part = dot(sum_ref[which_ref[0] * own + j], bar, TN)
+        term_ref[j * width : (j + 1) * width, :] = part.astype(BF)
+    for h in range(cot_ref.shape[1] // width):
+        up = dot(agg, cot_ref[:, h * width : (h + 1) * width], TN)
+        term_ref[(own + h) * width : (own + h + 1) * width, :] = up.astype(BF)
 
 
 def last_kernel(got_ref, pre_ref, send_ref, wdown_ref, cot_ref, feats_ref, grad_ref, term_ref):
     edges, span = cot_ref.shape
     share = edges // got_ref.shape[0]
-    width = got_ref.shape[2]
     feats = got_ref.shape[0]
     part = lambda j: [got_ref[f, j * share : (j + 1) * share, :] for f in range(feats)]
     blocks = part(1) + part(2)
@@ -199,13 +265,22 @@
     total = jnp.concatenate(part(0), axis=0).astype(F32)
     place = ones_where(send_ref[...] == iota((edges, count * share), 0))
     total = total + dot(place, jnp.concatenate(blocks[:count], axis=0))
-    pre_bar = (total * silu_grad(pre_ref[...].astype(F32))).astype(BF)
+    pre_bar = (total * silu_grad(pre_ref[...])).astype(BF)
     grad_ref[...] = (cot_ref[...].astype(F32) + dot(pre_bar, wdown_ref[...], NT)).astype(BF)
-    term_ref[:span, :] = dot(feats_ref[...], pre_bar, TN).astype(BF)
-    agg = jnp.concatenate(part(3), axis=0)
-    for h in range(span // width):
-        up = dot(agg, cot_ref[:, h * width : (h + 1) * width], TN)
-        term_ref[span + h * width : span + (h + 1) * width, :] = up.astype(BF)
+    term_ref[...] = dot(feats_ref[...], pre_bar, TN).astype(BF)
+
+
+def out_kernel(factor, total_ref, down_ref, up_ref, bil_ref):
+    pieces, rows, width = total_ref.shape
+    late = down_ref.shape[0] // pieces
+    early = rows - late
+    full = total_ref[...].astype(F32) * factor
+    down_ref[...] = full[:, early:, :].reshape(down_ref.shape)
+    flat = full[:, :early, :].reshape(pieces * early, width)
+    own = bil_ref.shape[0]
+    bil_ref[...] = flat[:own, :]
+    for h in range(up_ref.shape[1] // width):
+        up_ref[:, h * width : (h + 1) * width] = flat[own + h * width : own + (h + 1) * width, :]
 
 
 def moved(value, steps):
@@ -250,12 +325,9 @@
     sends = offsets[:feats], (offsets[feats:] + [None] * feats)[:feats]
     backs = [[None if o is None else -o for o in steps] for steps in sends]
 
-    part_pre = dot(edge_feats, w_down).astype(BF).reshape(feats, edges // feats, width)
-    part_bar = dot(cotangent, w_up, NT).astype(BF).reshape(feats, edges // feats, width)
-    both = scattered_sum(jnp.concatenate([part_pre, part_bar], axis=1), "feat")
-    both = everywhere(both, "feat")
-    pre = both[:, : edges // feats].reshape(edges, width)
-    bar = both[:, edges // feats :].reshape(edges, width)
+    part_pre = dot(edge_feats, w_down).astype(BF)
+    part_bar = dot(cotangent, w_up, NT).astype(BF)
+    both = everywhere(jnp.concatenate([part_pre, part_bar], axis=0), "feat")
 
     by_basis, by_trip = call(
         prep_kernel,
@@ -273,13 +345,15 @@
 
     second = jnp.minimum(feats + feat, blocks - 1)
     listed = jnp.concatenate([send_rows[0, feat], send_rows[0, second]]).reshape(-1, 1)
-    down, out_a, out_b = call(
+    pre, bar, down, out_a, out_b = call(
         down_kernel,
-        [low(edges, width), low(slots, width), low(slots, width)],
+        [jax.ShapeDtypeStruct((edges, width), F32)]
+        + [low(edges, width)] * 2
+        + [low(slots, width)] * 2,
         [],
         4 * slots * edges * width,
         (),
-        pre,
+        both,
         listed,
     )
     in_a, in_b = moved(out_a, sends[0]), moved(out_b, sends[1])
@@ -292,41 +366,39 @@
         [
             pltpu.VMEM((basis_total, edges, width), BF),
             pltpu.VMEM((3 * slots, width), F32),
+            pltpu.SemaphoreType.DMA((4,)),
         ],
         big,
         which,
         bar,
-        w_bil,
-        by_trip,
         k_rows,
+        late=(by_trip, w_bil),
     )
     back_a, back_b = moved(rem_a, backs[0]), moved(rem_b, backs[1])
 
     incoming, own = lax.optimization_barrier((jnp.concatenate([in_a, in_b], axis=0), own))
     incoming = everywhere(incoming, "feat")
     tall = 2 * slots
-    bil, agg = call(
+    shared = everywhere(jnp.concatenate([own, back_a, back_b], axis=0), "feat")
+    early = call(
         fore_kernel,
-        [low(own_basis * width, width), low(edges // feats, width)],
+        low(own_basis * width + span, width),
         [
-            pltpu.VMEM((tall, table // tall * width), BF),
+            pltpu.VMEM((table, width), BF),
             pltpu.VMEM((groups, trips * GROUP, width), BF),
-            pltpu.VMEM((own_basis, edges, width), BF),
-            pltpu.VMEM((basis_total, edges // feats, width), BF),
+            pltpu.VMEM((basis_total, edges, width), BF),
         ],
         big,
         which,
         down,
         incoming,
-        by_basis,
         trip_k,
-        w_bil,
         bar,
-    )
-    shared = everywhere(jnp.concatenate([own, back_a, back_b, agg], axis=0), "feat")
-    input_grad, terms = call(
+        late=(by_basis, w_bil, cotangent),
+    )
+    input_grad, late = call(
         last_kernel,
-        [low(edges, span), low(2 * span, width)],
+        [low(edges, span), low(span, width)],
         [],
         2 * edges * width * (blocks * slots + 3 * span),
         (),
@@ -340,18 +412,25 @@
 
     near = ("y", "core")
     count = lax.axis_size(near)
-    bil = bil.reshape(count, -1, width)
-    terms = terms.reshape(count, -1, width)
-    split = bil.shape[1]
-    total = scattered_sum(jnp.concatenate([bil, terms], axis=1), near)
+    pieces = [early.reshape(count, -1, width), late.reshape(count, -1, width)]
+    total = scattered_sum(jnp.concatenate(pieces, axis=1), near)
     total = exchanged_sum(total, "zl")
     total = exchanged_sum(total, "zh")
     total = everywhere(total, near)
     factor = 1.0 / math.sqrt(edges * lax.axis_size(DOM))
-    bil = total[:, :split].reshape(-1, width).astype(F32) * factor
-    terms = total[:, split:].reshape(-1, width).astype(F32) * factor
-    up = jnp.concatenate([terms[span : span + width], terms[span + width :]], axis=1)
-    return input_grad, terms[:span], up, bil
+    down_grad, up_grad, bil_grad = call(
+        functools.partial(out_kernel, factor),
+        [
+            jax.ShapeDtypeStruct((span, width), F32),
+            jax.ShapeDtypeStruct((width, span), F32),
+            jax.ShapeDtypeStruct((own_basis * width, width), F32),
+        ],
+        [],
+        1 << 20,
+        (),
+        total,
+    )
+    return input_grad, down_grad, up_grad, bil_grad
 
 
 def solution(mesh):

time: 153 us -> 143 us (0.935)
  blocking collectives: 71.6 us -> 59.5 us
  starting transfers between devices: 33.5 us -> 38.6 us
  other arithmetic: 2.46 us -> 0.19 us
  Pallas kernels: 26.3 us -> 28.4 us
    all_to_all x4 -> x3, blocking collectives: 58.7 us -> 47.3 us  [everywhere(): return lax.all_to_all(copies, axis, 0, 0)]
    ppermute x4, starting transfers between devices: 20.2 us -> 25.9 us  [moved(): return lax.ppermute(value, (*DOM, 'feat'), pairs)]
    all_to_all x1 -> x0, waiting for transfers between devices: 5.53 us -> none  [scattered_sum(): arrived = lax.all_to_all(pieces, axis, 0, 0)]
    all_to_all x1 -> x0, starting transfers between devices: 4.82 us -> none  [scattered_sum(): arrived = lax.all_to_all(pieces, axis, 0, 0)]
    all_to_all x2 -> x3, starting transfers between devices: 8.47 us -> 12.7 us  [everywhere(): return lax.all_to_all(copies, axis, 0, 0)]
    ppermute x4, waiting for transfers between devices: 0.01 us -> 3.9 us  [moved(): return lax.ppermute(value, (*DOM, 'feat'), pairs)]
    pallas_call x5 -> x6, Pallas kernels: 26.3 us -> 28.4 us  [call(): pl.pallas_call(kernel, in_specs=scalars + [pl.BlockSpec(memory_space=pltp...]
    unnamed x27 -> x21, local copies, waits for them, and re-layouts: 6.64 us -> 4.86 us
  transfers between devices with their start and end apart: 7 -> 7, of which waited for: 2 -> 2; matrix products, arithmetic and copies ran while one was open for 0% -> 1% of each run, Pallas kernels for 16% -> 18%
where the time goes in v3:
time: 143 us; the launch traced here: 142 us
  blocking collectives  59.5 us (42%)
  starting transfers between devices  38.6 us (27%)
  Pallas kernels  28.4 us (20%)
  local copies, waits for them, and re-layouts  8.1 us (6%)
  waiting for transfers between devices  5.12 us (4%)
    all_to_all x3, blocking collectives, everywhere(): return lax.all_to_all(copies, axis, 0, 0)  47.3 us
    pallas_call x6, Pallas kernels, call(): pl.pallas_call(kernel, in_specs=scalars + [pl.BlockSpec(memory_space=pltp...  28.4 us
    ppermute x4, starting transfers between devices, moved(): return lax.ppermute(value, (*DOM, 'feat'), pairs)  25.9 us
    all_to_all x3, starting transfers between devices, everywhere(): return lax.all_to_all(copies, axis, 0, 0)  12.7 us
    all_to_all x1, blocking collectives, scattered_sum(): arrived = lax.all_to_all(pieces, axis, 0, 0)  12.2 us
    unnamed x21, local copies, waits for them, and re-layouts  4.86 us
    ppermute x4, waiting for transfers between devices, moved(): return lax.ppermute(value, (*DOM, 'feat'), pairs)  3.9 us
  transfers between devices with their start and end apart: 7, of which 2 were waited for; matrix products, arithmetic and copies ran while one was open for 1% of the time, Pallas kernels for 18%

profile of v3, /device:TPU:1, one launch (start us, length us, event | category | flops | bytes accessed | tf_op | source)
XLA Modules:
  0.0 142.2 jit_solution(17835134788897312157)
XLA Ops:
  0.6 0.0 copy-start
  0.6 0.0 copy-start.3
  0.7 0.0 copy-start.4
  0.7 0.8 copy-done
  1.5 1.2 convolution_convert_fusion
  2.7 0.0 copy-done.3
  2.7 0.0 copy-done.4
  2.7 0.2 convolution_convert_fusion.1
  2.9 1.1 broadcast_in_dim.12
  4.1 0.0 copy-start.1
  4.1 5.0 %all-to-all-start = ((bf16[4,1024,128]{2,1,0:T(8,128)(2,1)}), bf16[4,1024,128]{2,1,0:T(8,128)(2,1)S(1)}, u32[]{:S(2)}, u32[]{:S(2)}) async-start(bf16[4,1024,128]{2,1,0:T(8,128)(2,1)} %broadcast_in_dim.12), calls=%async_computation | async-start | bytes 2097152 | tf_op jit(solution)/shard_map/all_to_all | solution.py:305
  9.0 0.0 copy-start.5
  9.0 0.7 copy-done.5
  9.7 0.0 copy-start.9
  9.7 0.1 copy.19.send_ref
  9.9 0.6 copy-done.9
  10.5 0.1 reshape.43
  10.6 0.1 copy.20
  10.7 0.1 copy.21.k_ref
  10.8 0.0 copy-start.6
  10.8 0.0 copy-done.1
  10.8 0.7 copy-done.6
  11.5 4.1 %shard_map.121 = (f32[32,32,256]{2,1,0:T(8,128)S(1)}, f32[32,16,512]{2,1,0:T(8,128)S(1)}) custom-call(f32[512,512]{1,0:T(8,128)S(1)} %bitcast.18, s32[1,512]{1,0:T(1,128)S(1)} %bitcast.22), custom_call_target="tpu_custom_call" | custom-call | flops 268435456 | bytes 1050624 | tf_op jit(solution)/shard_map/pallas_call | solution.py:46
  15.6 0.0 copy-start.7
  15.6 1.0 copy-done.7
  16.6 0.0 copy-start.8
  16.6 1.0 copy-done.8
  17.5 1.2 all-to-all-done.both_ref
  18.8 0.4 shard_map.120
  19.2 18.1 %collective-permute-start.1 = (bf16[128,128]{1,0:T(8,128)(2,1)S(1)}, bf16[128,128]{1,0:T(8,128)(2,1)S(1)}, u32[]{:S(2)}, u32[]{:S(2)}) collective-permute-start(bf16[128,128]{1,0:T(8,128)(2,1)S(1)} %get-tuple-element.22), channel_id=1, source_target_pairs={{0,504},{1,501},{4,508},{5,505},{8,0},{9,509},{12,4},{13,1},{16,8}... | collective-permute-start | bytes 98312 | tf_op jit(solution)/shard_map/ppermute | solution.py:294
  37.2 1.9 %collective-permute-start = (bf16[128,128]{1,0:T(8,128)(2,1)S(1)}, bf16[128,128]{1,0:T(8,128)(2,1)S(1)}, u32[]{:S(2)}, u32[]{:S(2)}) collective-permute-start(bf16[128,128]{1,0:T(8,128)(2,1)S(1)} %get-tuple-element.21), channel_id=1, source_target_pairs={{0,4},{1,9},{2,14},{3,511},{4,8},{5,13},{6,18},{7,3},{8,12},{9,17}... | collective-permute-start | bytes 98312 | tf_op jit(solution)/shard_map/ppermute | solution.py:294
  39.2 9.8 %shard_map.122 = (bf16[128,128]{1,0:T(8,128)(2,1)S(1)}, bf16[128,128]{1,0:T(8,128)(2,1)S(1)}, bf16[128,128]{1,0:T(8,128)(2,1)S(1)}) custom-call(s32[1]{0:T(128)} %bitcast.3.which_ref, bf16[512,128]{1,0:T(8,128)(2,1)S(1)} %get-tuple-element.23.bar_ref, s32[32,1,256]{2,1,0:T(1,128)S(1)} %copy.21.k_ref, f32[32,16,512]{2,1,0:T(8,128)} %copy-done.8, ...), custom_call_target="tpu_custom_call" | custom-call | flops 4194304000 | bytes 163840 | tf_op jit(solution)/shard_map/pallas_call | solution.py:46
  48.9 0.0 collective-permute-done.1
  49.0 0.0 collective-permute-done
  49.0 0.7 broadcast_in_dim.14
  49.7 3.4 %all-to-all-start.2 = ((bf16[4,256,128]{2,1,0:T(8,128)(2,1)}), bf16[4,256,128]{2,1,0:T(8,128)(2,1)S(1)}, u32[]{:S(2)}, u32[]{:S(2)}) async-start(bf16[4,256,128]{2,1,0:T(8,128)(2,1)} %broadcast_in_dim.14), calls=%async_computation.2 | async-start | bytes 524288 | tf_op jit(solution)/shard_map/all_to_all | solution.py:305
  53.1 1.9 %collective-permute-start.3 = (bf16[128,128]{1,0:T(8,128)(2,1)S(1)}, bf16[128,128]{1,0:T(8,128)(2,1)S(1)}, u32[]{:S(2)}, u32[]{:S(2)}) collective-permute-start(bf16[128,128]{1,0:T(8,128)(2,1)S(1)} %get-tuple-element.28), channel_id=1, source_target_pairs={{0,8},{1,13},{4,12},{5,17},{8,16},{9,21},{12,20},{13,25},{16,24},{... | collective-permute-start | bytes 98312 | tf_op jit(solution)/shard_map/ppermute | solution.py:294
  55.1 4.0 %collective-permute-start.2 = (bf16[128,128]{1,0:T(8,128)(2,1)S(1)}, bf16[128,128]{1,0:T(8,128)(2,1)S(1)}, u32[]{:S(2)}, u32[]{:S(2)}) collective-permute-start(bf16[128,128]{1,0:T(8,128)(2,1)S(1)} %get-tuple-element.27), channel_id=1, source_target_pairs={{0,508},{1,505},{2,502},{3,7},{4,0},{5,509},{6,506},{7,11},{8,4},{... | collective-permute-start | bytes 98312 | tf_op jit(solution)/shard_map/ppermute | solution.py:294
  59.1 0.1 copy.22.k_ref
  59.2 3.9 %collective-permute-done.3 = bf16[128,128]{1,0:T(8,128)(2,1)S(1)} collective-permute-done((bf16[128,128]{1,0:T(8,128)(2,1)S(1)}, bf16[128,128]{1,0:T(8,128)(2,1)S(1)}, u32[]{:S(2)}, u32[]{:S(2)}) %collective-permute-start.3) | collective-permute-done | bytes 32800 | tf_op jit(solution)/shard_map/ppermute | solution.py:294
  63.1 0.0 collective-permute-done.2
  63.1 0.8 broadcast_in_dim.13
  63.9 0.0 all-to-all-done.2.in_ref
  63.9 4.3 %all-to-all-start.1 = ((bf16[4,384,128]{2,1,0:T(8,128)(2,1)}), bf16[4,384,128]{2,1,0:T(8,128)(2,1)S(1)}, u32[]{:S(2)}, u32[]{:S(2)}) async-start(bf16[4,384,128]{2,1,0:T(8,128)(2,1)} %broadcast_in_dim.13), calls=%async_computation.1 | async-start | bytes 786432 | tf_op jit(solution)/shard_map/all_to_all | solution.py:305
  68.2 0.0 copy-start.2
  68.2 11.9 %shard_map.124 = bf16[1280,128]{1,0:T(8,128)(2,1)S(1)} custom-call(s32[1]{0:T(128)} %bitcast.3.which_ref, bf16[512,128]{1,0:T(8,128)(2,1)S(1)} %get-tuple-element.31.down_ref, bf16[4,256,128]{2,1,0:T(8,128)(2,1)S(1)} %all-to-all-done.2.in_ref, s32[512,16]{1,0:T(8,128)S(1)} %copy.22.k_ref, bf16[512,128]{1,0:T(8,128)(2,1)S(1)} %get-tuple-element.23.bar_ref, ...), custom_call_target="tpu_custom_call" | custom-call | flops 4194304000 | bytes 557056 | tf_op jit(solution)/shard_map/pallas_call | solution.py:46
  80.2 0.0 all-to-all-done.1.got_ref
  80.2 0.0 copy-done.2
  80.2 1.3 shard_map.123
  81.5 12.2 %all_to_all.35 = bf16[8,192,128]{2,1,0:T(8,128)(2,1)S(1)} all-to-all(bf16[8,192,128]{2,1,0:T(8,128)(2,1)S(1)} %pad_maximum_fusion), channel_id=1, replica_groups=mesh['zh'=4,'zl'=4,'y'=4,'core'=2,'feat'=4] {'y','core'}, dimensions={0} | all-to-all | bytes 786432 | tf_op jit(solution)/shard_map/all_to_all | solution.py:298
  93.7 0.1 reduce_sum.36
  93.8 8.0 %all_to_all.36 = bf16[4,192,128]{2,1,0:T(8,128)(2,1)S(1)} all-to-all(bf16[4,192,128]{2,1,0:T(8,128)(2,1)S(1)} %broadcast_in_dim.15), channel_id=1, replica_groups=mesh['zh'=4,'zl'=4,'y'=4,'core'=2,'feat'=4] {'zl'}, dimensions={0} | all-to-all | bytes 393216 | tf_op jit(solution)/shard_map/all_to_all | solution.py:305
  101.9 25.2 %all_to_all.37 = bf16[4,192,128]{2,1,0:T(8,128)(2,1)S(1)} all-to-all(bf16[4,192,128]{2,1,0:T(8,128)(2,1)S(1)} %broadcast_in_dim.16), channel_id=1, replica_groups=mesh['zh'=4,'zl'=4,'y'=4,'core'=2,'feat'=4] {'zh'}, dimensions={0} | all-to-all | bytes 393216 | tf_op jit(solution)/shard_map/all_to_all | solution.py:305
  127.2 0.1 broadcast_in_dim.17
  127.2 14.0 %all_to_all.38.total_ref = bf16[8,192,128]{2,1,0:T(8,128)(2,1)S(1)} all-to-all(bf16[8,192,128]{2,1,0:T(8,128)(2,1)S(1)} %broadcast_in_dim.17), channel_id=1, replica_groups=mesh['zh'=4,'zl'=4,'y'=4,'core'=2,'feat'=4] {'y','core'}, dimensions={0} | all-to-all | bytes 786432 | tf_op jit(solution)/shard_map/all_to_all | solution.py:305
  141.3 0.9 shard_map.125
  (10 shorter events, 0.2 us)
Async XLA Ops:
  0.6 0.8 copy-start
  0.6 2.0 %copy-start.3 = (bf16[512,256]{1,0:T(8,128)(2,1)S(1)}, bf16[512,256]{1,0:T(8,128)(2,1)}, u32[]{:S(2)}) copy-start(bf16[512,256]{1,0:T(8,128)(2,1)} %feats_ref.1) | copy-start | bytes 786436
  0.7 2.0 %copy-start.4 = (bf16[256,128]{1,0:T(8,128)(2,1)S(1)}, bf16[256,128]{1,0:T(8,128)(2,1)}, u32[]{:S(2)}) copy-start(bf16[256,128]{1,0:T(8,128)(2,1)} %wdown_ref.1) | copy-start | bytes 196612
  4.1 6.8 %copy-start.1 = (f32[16,32,512]{2,1,0:T(8,128)S(1)}, f32[16,32,512]{2,1,0:T(8,128)}, u32[]{:S(2)}) copy-start(f32[16,32,512]{2,1,0:T(8,128)} %param.14) | copy-start | bytes 3145732
  4.1 14.7 %all-to-all-start = ((bf16[4,1024,128]{2,1,0:T(8,128)(2,1)}), bf16[4,1024,128]{2,1,0:T(8,128)(2,1)S(1)}, u32[]{:S(2)}, u32[]{:S(2)}) async-start(bf16[4,1024,128]{2,1,0:T(8,128)(2,1)} %broadcast_in_dim.12), calls=%async_computation | async-start | bytes 2097152 | tf_op jit(solution)/shard_map/all_to_all | solution.py:305
  9.0 0.7 copy-start.5
  9.7 0.8 copy-start.9
  10.8 0.7 copy-start.6
  15.6 1.0 copy-start.7
  16.6 1.0 copy-start.8
  19.2 29.8 %collective-permute-start.1 = (bf16[128,128]{1,0:T(8,128)(2,1)S(1)}, bf16[128,128]{1,0:T(8,128)(2,1)S(1)}, u32[]{:S(2)}, u32[]{:S(2)}) collective-permute-start(bf16[128,128]{1,0:T(8,128)(2,1)S(1)} %get-tuple-element.22), channel_id=1, source_target_pairs={{0,504},{1,501},{4,508},{5,505},{8,0},{9,509},{12,4},{13,1},{16,8}... | collective-permute-start | bytes 98312 | tf_op jit(solution)/shard_map/ppermute | solution.py:294
  37.2 11.7 %collective-permute-start = (bf16[128,128]{1,0:T(8,128)(2,1)S(1)}, bf16[128,128]{1,0:T(8,128)(2,1)S(1)}, u32[]{:S(2)}, u32[]{:S(2)}) collective-permute-start(bf16[128,128]{1,0:T(8,128)(2,1)S(1)} %get-tuple-element.21), channel_id=1, source_target_pairs={{0,4},{1,9},{2,14},{3,511},{4,8},{5,13},{6,18},{7,3},{8,12},{9,17}... | collective-permute-start | bytes 98312 | tf_op jit(solution)/shard_map/ppermute | solution.py:294
  49.7 14.2 %all-to-all-start.2 = ((bf16[4,256,128]{2,1,0:T(8,128)(2,1)}), bf16[4,256,128]{2,1,0:T(8,128)(2,1)S(1)}, u32[]{:S(2)}, u32[]{:S(2)}) async-start(bf16[4,256,128]{2,1,0:T(8,128)(2,1)} %broadcast_in_dim.14), calls=%async_computation.2 | async-start | bytes 524288 | tf_op jit(solution)/shard_map/all_to_all | solution.py:305
  53.1 10.0 %collective-permute-start.3 = (bf16[128,128]{1,0:T(8,128)(2,1)S(1)}, bf16[128,128]{1,0:T(8,128)(2,1)S(1)}, u32[]{:S(2)}, u32[]{:S(2)}) collective-permute-start(bf16[128,128]{1,0:T(8,128)(2,1)S(1)} %get-tuple-element.28), channel_id=1, source_target_pairs={{0,8},{1,13},{4,12},{5,17},{8,16},{9,21},{12,20},{13,25},{16,24},{... | collective-permute-start | bytes 98312 | tf_op jit(solution)/shard_map/ppermute | solution.py:294
  55.1 8.0 %collective-permute-start.2 = (bf16[128,128]{1,0:T(8,128)(2,1)S(1)}, bf16[128,128]{1,0:T(8,128)(2,1)S(1)}, u32[]{:S(2)}, u32[]{:S(2)}) collective-permute-start(bf16[128,128]{1,0:T(8,128)(2,1)S(1)} %get-tuple-element.27), channel_id=1, source_target_pairs={{0,508},{1,505},{2,502},{3,7},{4,0},{5,509},{6,506},{7,11},{8,4},{... | collective-permute-start | bytes 98312 | tf_op jit(solution)/shard_map/ppermute | solution.py:294
  63.9 16.3 %all-to-all-start.1 = ((bf16[4,384,128]{2,1,0:T(8,128)(2,1)}), bf16[4,384,128]{2,1,0:T(8,128)(2,1)S(1)}, u32[]{:S(2)}, u32[]{:S(2)}) async-start(bf16[4,384,128]{2,1,0:T(8,128)(2,1)} %broadcast_in_dim.13), calls=%async_computation.1 | async-start | bytes 786432 | tf_op jit(solution)/shard_map/all_to_all | solution.py:305
  68.2 12.0 %copy-start.2 = (bf16[512,256]{1,0:T(8,128)(2,1)S(1)}, bf16[512,256]{1,0:T(8,128)(2,1)}, u32[]{:S(2)}) copy-start(bf16[512,256]{1,0:T(8,128)(2,1)} %cot_far.1) | copy-start | bytes 786436

commit v4 on v3

--- a/solution.py
+++ b/solution.py
@@ -202,7 +202,7 @@
     fetch_w.start()
     fetch_wbil.start()
     fetch_cot.start()
-    groups, rows, width = got_ref.shape
+    groups, _, width = got_ref.shape
     basis, edges, _ = sum_ref.shape
     trips = k_ref.shape[1]
     tall = tab_ref.shape[0]
@@ -256,7 +256,7 @@
 
 
 def last_kernel(got_ref, pre_ref, send_ref, wdown_ref, cot_ref, feats_ref, grad_ref, term_ref):
-    edges, span = cot_ref.shape
+    edges, _ = cot_ref.shape
     share = edges // got_ref.shape[0]
     feats = got_ref.shape[0]
     part = lambda j: [got_ref[f, j * share : (j + 1) * share, :] for f in range(feats)]
@@ -309,7 +309,7 @@
     return jnp.sum(everywhere(value, axis).astype(F32), axis=0).astype(BF)
 
 
-def local(edge_feats, cotangent, w_down, w_up, w_bil, basis, trip_k, trip_count, send_rows):
+def steps(edge_feats, cotangent, w_down, w_up, w_bil, basis, trip_k, trip_count, send_rows):
     edges, span = edge_feats.shape
     width = w_down.shape[1]
     trips, basis_total, _ = basis.shape
@@ -374,11 +374,11 @@
         k_rows,
         late=(by_trip, w_bil),
     )
-    back_a, back_b = moved(rem_a, backs[0]), moved(rem_b, backs[1])
+    back_a = moved(rem_a, backs[0])
+    back_b = moved(rem_b, backs[1])
 
     incoming, own = lax.optimization_barrier((jnp.concatenate([in_a, in_b], axis=0), own))
     incoming = everywhere(incoming, "feat")
-    tall = 2 * slots
     shared = everywhere(jnp.concatenate([own, back_a, back_b], axis=0), "feat")
     early = call(
         fore_kernel,
@@ -410,11 +410,10 @@
         edge_feats,
     )
 
-    near = ("y", "core")
+    near = ("zl", "y", "core")
     count = lax.axis_size(near)
     pieces = [early.reshape(count, -1, width), late.reshape(count, -1, width)]
     total = scattered_sum(jnp.concatenate(pieces, axis=1), near)
-    total = exchanged_sum(total, "zl")
     total = exchanged_sum(total, "zh")
     total = everywhere(total, near)
     factor = 1.0 / math.sqrt(edges * lax.axis_size(DOM))
@@ -436,7 +435,7 @@
 def solution(mesh):
     fine = Mesh(mesh.devices.reshape(4, 4, 4, 2, 4), (*DOM, "feat"))
     return jax.shard_map(
-        local,
+        steps,
         mesh=fine,
         in_specs=(
             P(DOM, "feat"),

time: 143 us -> 143 us (level)
    all_to_all x1, blocking collectives: 12.2 us -> 18.3 us  [scattered_sum(): arrived = lax.all_to_all(pieces, axis, 0, 0)]
    all_to_all x3 -> x2, blocking collectives: 47.3 us -> 41.3 us  [everywhere(): return lax.all_to_all(copies, axis, 0, 0)]
where the time goes in v4:
time: 143 us; the launch traced here: 142 us
  blocking collectives  59.5 us (42%)
  starting transfers between devices  38.6 us (27%)
  Pallas kernels  28.4 us (20%)
  local copies, waits for them, and re-layouts  8.06 us (6%)
  waiting for transfers between devices  5.1 us (4%)
    all_to_all x2, blocking collectives, everywhere(): return lax.all_to_all(copies, axis, 0, 0)  41.3 us
    pallas_call x6, Pallas kernels, call(): pl.pallas_call(kernel, in_specs=scalars + [pl.BlockSpec(memory_space=pltp...  28.4 us
    ppermute x4, starting transfers between devices, moved(): return lax.ppermute(value, (*DOM, 'feat'), pairs)  25.9 us
    all_to_all x1, blocking collectives, scattered_sum(): arrived = lax.all_to_all(pieces, axis, 0, 0)  18.3 us
    all_to_all x3, starting transfers between devices, everywhere(): return lax.all_to_all(copies, axis, 0, 0)  12.7 us
    unnamed x21, local copies, waits for them, and re-layouts  4.89 us
    ppermute x4, waiting for transfers between devices, moved(): return lax.ppermute(value, (*DOM, 'feat'), pairs)  3.9 us
  transfers between devices with their start and end apart: 7, of which 2 were waited for; matrix products, arithmetic and copies ran while one was open for 1% of the time, Pallas kernels for 18%

profile of v4, /device:TPU:1, one launch (start us, length us, event | category | flops | bytes accessed | tf_op | source)
XLA Modules:
  0.0 142.1 jit_solution(3929433344006029310)
XLA Ops:
  0.6 0.0 copy-start
  0.6 0.0 copy-start.3
  0.7 0.0 copy-start.4
  0.7 0.8 copy-done
  1.5 1.2 convolution_convert_fusion
  2.7 0.0 copy-done.3
  2.7 0.0 copy-done.4
  2.7 0.2 convolution_convert_fusion.1
  2.9 1.1 broadcast_in_dim.10
  4.0 0.0 copy-start.1
  4.0 5.0 %all-to-all-start = ((bf16[4,1024,128]{2,1,0:T(8,128)(2,1)}), bf16[4,1024,128]{2,1,0:T(8,128)(2,1)S(1)}, u32[]{:S(2)}, u32[]{:S(2)}) async-start(bf16[4,1024,128]{2,1,0:T(8,128)(2,1)} %broadcast_in_dim.10), calls=%async_computation | async-start | bytes 2097152 | tf_op jit(solution)/shard_map/all_to_all | solution.py:305
  9.0 0.0 copy-start.5
  9.0 0.7 copy-done.5
  9.7 0.0 copy-start.9
  9.7 0.1 copy.19.send_ref
  9.8 0.6 copy-done.9
  10.5 0.1 reshape.42
  10.6 0.1 copy.20
  10.7 0.1 copy.21.k_ref
  10.8 0.0 copy-start.6
  10.8 0.0 copy-done.1
  10.8 0.7 copy-done.6
  11.5 4.1 %shard_map.121 = (f32[32,32,256]{2,1,0:T(8,128)S(1)}, f32[32,16,512]{2,1,0:T(8,128)S(1)}) custom-call(f32[512,512]{1,0:T(8,128)S(1)} %bitcast.18, s32[1,512]{1,0:T(1,128)S(1)} %bitcast.22), custom_call_target="tpu_custom_call" | custom-call | flops 268435456 | bytes 1050624 | tf_op jit(solution)/shard_map/pallas_call | solution.py:46
  15.6 0.0 copy-start.7
  15.6 1.0 copy-done.7
  16.6 0.0 copy-start.8
  16.6 1.0 copy-done.8
  17.5 1.2 all-to-all-done.both_ref
  18.7 0.4 shard_map.120
  19.1 18.1 %collective-permute-start.1 = (bf16[128,128]{1,0:T(8,128)(2,1)S(1)}, bf16[128,128]{1,0:T(8,128)(2,1)S(1)}, u32[]{:S(2)}, u32[]{:S(2)}) collective-permute-start(bf16[128,128]{1,0:T(8,128)(2,1)S(1)} %get-tuple-element.22), channel_id=1, source_target_pairs={{0,504},{1,501},{4,508},{5,505},{8,0},{9,509},{12,4},{13,1},{16,8}... | collective-permute-start | bytes 98312 | tf_op jit(solution)/shard_map/ppermute | solution.py:294
  37.2 1.9 %collective-permute-start = (bf16[128,128]{1,0:T(8,128)(2,1)S(1)}, bf16[128,128]{1,0:T(8,128)(2,1)S(1)}, u32[]{:S(2)}, u32[]{:S(2)}) collective-permute-start(bf16[128,128]{1,0:T(8,128)(2,1)S(1)} %get-tuple-element.21), channel_id=1, source_target_pairs={{0,4},{1,9},{2,14},{3,511},{4,8},{5,13},{6,18},{7,3},{8,12},{9,17}... | collective-permute-start | bytes 98312 | tf_op jit(solution)/shard_map/ppermute | solution.py:294
  39.1 9.8 %shard_map.122 = (bf16[128,128]{1,0:T(8,128)(2,1)S(1)}, bf16[128,128]{1,0:T(8,128)(2,1)S(1)}, bf16[128,128]{1,0:T(8,128)(2,1)S(1)}) custom-call(s32[1]{0:T(128)} %bitcast.3.which_ref, bf16[512,128]{1,0:T(8,128)(2,1)S(1)} %get-tuple-element.23.bar_ref, s32[32,1,256]{2,1,0:T(1,128)S(1)} %copy.21.k_ref, f32[32,16,512]{2,1,0:T(8,128)} %copy-done.8, ...), custom_call_target="tpu_custom_call" | custom-call | flops 4194304000 | bytes 163840 | tf_op jit(solution)/shard_map/pallas_call | solution.py:46
  48.9 0.0 collective-permute-done.1
  48.9 0.0 collective-permute-done
  49.0 0.7 broadcast_in_dim.12
  49.7 3.4 %all-to-all-start.2 = ((bf16[4,256,128]{2,1,0:T(8,128)(2,1)}), bf16[4,256,128]{2,1,0:T(8,128)(2,1)S(1)}, u32[]{:S(2)}, u32[]{:S(2)}) async-start(bf16[4,256,128]{2,1,0:T(8,128)(2,1)} %broadcast_in_dim.12), calls=%async_computation.2 | async-start | bytes 524288 | tf_op jit(solution)/shard_map/all_to_all | solution.py:305
  53.1 1.9 %collective-permute-start.3 = (bf16[128,128]{1,0:T(8,128)(2,1)S(1)}, bf16[128,128]{1,0:T(8,128)(2,1)S(1)}, u32[]{:S(2)}, u32[]{:S(2)}) collective-permute-start(bf16[128,128]{1,0:T(8,128)(2,1)S(1)} %get-tuple-element.28), channel_id=1, source_target_pairs={{0,8},{1,13},{4,12},{5,17},{8,16},{9,21},{12,20},{13,25},{16,24},{... | collective-permute-start | bytes 98312 | tf_op jit(solution)/shard_map/ppermute | solution.py:294
  55.0 4.0 %collective-permute-start.2 = (bf16[128,128]{1,0:T(8,128)(2,1)S(1)}, bf16[128,128]{1,0:T(8,128)(2,1)S(1)}, u32[]{:S(2)}, u32[]{:S(2)}) collective-permute-start(bf16[128,128]{1,0:T(8,128)(2,1)S(1)} %get-tuple-element.27), channel_id=1, source_target_pairs={{0,508},{1,505},{2,502},{3,7},{4,0},{5,509},{6,506},{7,11},{8,4},{... | collective-permute-start | bytes 98312 | tf_op jit(solution)/shard_map/ppermute | solution.py:294
  59.1 0.1 copy.22.k_ref
  59.2 3.9 %collective-permute-done.3 = bf16[128,128]{1,0:T(8,128)(2,1)S(1)} collective-permute-done((bf16[128,128]{1,0:T(8,128)(2,1)S(1)}, bf16[128,128]{1,0:T(8,128)(2,1)S(1)}, u32[]{:S(2)}, u32[]{:S(2)}) %collective-permute-start.3) | collective-permute-done | bytes 32800 | tf_op jit(solution)/shard_map/ppermute | solution.py:294
  63.1 0.0 collective-permute-done.2
  63.1 0.8 broadcast_in_dim.11
  63.9 0.0 all-to-all-done.2.in_ref
  63.9 4.3 %all-to-all-start.1 = ((bf16[4,384,128]{2,1,0:T(8,128)(2,1)}), bf16[4,384,128]{2,1,0:T(8,128)(2,1)S(1)}, u32[]{:S(2)}, u32[]{:S(2)}) async-start(bf16[4,384,128]{2,1,0:T(8,128)(2,1)} %broadcast_in_dim.11), calls=%async_computation.1 | async-start | bytes 786432 | tf_op jit(solution)/shard_map/all_to_all | solution.py:305
  68.2 0.0 copy-start.2
  68.2 11.9 %shard_map.124 = bf16[1280,128]{1,0:T(8,128)(2,1)S(1)} custom-call(s32[1]{0:T(128)} %bitcast.3.which_ref, bf16[512,128]{1,0:T(8,128)(2,1)S(1)} %get-tuple-element.31.down_ref, bf16[4,256,128]{2,1,0:T(8,128)(2,1)S(1)} %all-to-all-done.2.in_ref, s32[512,16]{1,0:T(8,128)S(1)} %copy.22.k_ref, bf16[512,128]{1,0:T(8,128)(2,1)S(1)} %get-tuple-element.23.bar_ref, ...), custom_call_target="tpu_custom_call" | custom-call | flops 4194304000 | bytes 557056 | tf_op jit(solution)/shard_map/pallas_call | solution.py:46
  80.2 0.0 all-to-all-done.1.got_ref
  80.2 0.0 copy-done.2
  80.2 1.3 shard_map.123
  81.5 18.3 %all_to_all.30 = bf16[32,48,128]{2,1,0:T(8,128)(2,1)S(1)} all-to-all(bf16[32,48,128]{2,1,0:T(8,128)(2,1)S(1)} %pad_maximum_fusion), channel_id=1, replica_groups=mesh['zh'=4,'zl'=4,'y'=4,'core'=2,'feat'=4] {'zl','y','core'}, dimensions={0} | all-to-all | bytes 786432 | tf_op jit(solution)/shard_map/all_to_all | solution.py:298
  99.8 0.1 reduce_sum.24
  99.9 22.2 %all_to_all.31 = bf16[4,48,128]{2,1,0:T(8,128)(2,1)S(1)} all-to-all(bf16[4,48,128]{2,1,0:T(8,128)(2,1)S(1)} %broadcast_in_dim.13), channel_id=1, replica_groups=mesh['zh'=4,'zl'=4,'y'=4,'core'=2,'feat'=4] {'zh'}, dimensions={0} | all-to-all | bytes 98304 | tf_op jit(solution)/shard_map/all_to_all | solution.py:305
  122.1 0.1 broadcast_in_dim.14
  122.1 19.1 %all_to_all.32.total_ref = bf16[32,48,128]{2,1,0:T(8,128)(2,1)S(1)} all-to-all(bf16[32,48,128]{2,1,0:T(8,128)(2,1)S(1)} %broadcast_in_dim.14), channel_id=1, replica_groups=mesh['zh'=4,'zl'=4,'y'=4,'core'=2,'feat'=4] {'zl','y','core'}, dimensions={0} | all-to-all | bytes 786432 | tf_op jit(solution)/shard_map/all_to_all | solution.py:305
  141.2 0.9 shard_map.125
  (8 shorter events, 0.1 us)
Async XLA Ops:
  0.6 0.8 copy-start
  0.6 2.0 %copy-start.3 = (bf16[512,256]{1,0:T(8,128)(2,1)S(1)}, bf16[512,256]{1,0:T(8,128)(2,1)}, u32[]{:S(2)}) copy-start(bf16[512,256]{1,0:T(8,128)(2,1)} %feats_ref.1) | copy-start | bytes 786436
  0.7 2.0 %copy-start.4 = (bf16[256,128]{1,0:T(8,128)(2,1)S(1)}, bf16[256,128]{1,0:T(8,128)(2,1)}, u32[]{:S(2)}) copy-start(bf16[256,128]{1,0:T(8,128)(2,1)} %wdown_ref.1) | copy-start | bytes 196612
  4.0 6.8 %copy-start.1 = (f32[16,32,512]{2,1,0:T(8,128)S(1)}, f32[16,32,512]{2,1,0:T(8,128)}, u32[]{:S(2)}) copy-start(f32[16,32,512]{2,1,0:T(8,128)} %param.14) | copy-start | bytes 3145732
  4.0 14.7 %all-to-all-start = ((bf16[4,1024,128]{2,1,0:T(8,128)(2,1)}), bf16[4,1024,128]{2,1,0:T(8,128)(2,1)S(1)}, u32[]{:S(2)}, u32[]{:S(2)}) async-start(bf16[4,1024,128]{2,1,0:T(8,128)(2,1)} %broadcast_in_dim.10), calls=%async_computation | async-start | bytes 2097152 | tf_op jit(solution)/shard_map/all_to_all | solution.py:305
  9.0 0.7 copy-start.5
  9.7 0.8 copy-start.9
  10.8 0.7 copy-start.6
  15.6 1.0 copy-start.7
  16.6 1.0 copy-start.8
  19.1 29.8 %collective-permute-start.1 = (bf16[128,128]{1,0:T(8,128)(2,1)S(1)}, bf16[128,128]{1,0:T(8,128)(2,1)S(1)}, u32[]{:S(2)}, u32[]{:S(2)}) collective-permute-start(bf16[128,128]{1,0:T(8,128)(2,1)S(1)} %get-tuple-element.22), channel_id=1, source_target_pairs={{0,504},{1,501},{4,508},{5,505},{8,0},{9,509},{12,4},{13,1},{16,8}... | collective-permute-start | bytes 98312 | tf_op jit(solution)/shard_map/ppermute | solution.py:294
  37.2 11.7 %collective-permute-start = (bf16[128,128]{1,0:T(8,128)(2,1)S(1)}, bf16[128,128]{1,0:T(8,128)(2,1)S(1)}, u32[]{:S(2)}, u32[]{:S(2)}) collective-permute-start(bf16[128,128]{1,0:T(8,128)(2,1)S(1)} %get-tuple-element.21), channel_id=1, source_target_pairs={{0,4},{1,9},{2,14},{3,511},{4,8},{5,13},{6,18},{7,3},{8,12},{9,17}... | collective-permute-start | bytes 98312 | tf_op jit(solution)/shard_map/ppermute | solution.py:294
  49.7 14.2 %all-to-all-start.2 = ((bf16[4,256,128]{2,1,0:T(8,128)(2,1)}), bf16[4,256,128]{2,1,0:T(8,128)(2,1)S(1)}, u32[]{:S(2)}, u32[]{:S(2)}) async-start(bf16[4,256,128]{2,1,0:T(8,128)(2,1)} %broadcast_in_dim.12), calls=%async_computation.2 | async-start | bytes 524288 | tf_op jit(solution)/shard_map/all_to_all | solution.py:305
  53.1 10.0 %collective-permute-start.3 = (bf16[128,128]{1,0:T(8,128)(2,1)S(1)}, bf16[128,128]{1,0:T(8,128)(2,1)S(1)}, u32[]{:S(2)}, u32[]{:S(2)}) collective-permute-start(bf16[128,128]{1,0:T(8,128)(2,1)S(1)} %get-tuple-element.28), channel_id=1, source_target_pairs={{0,8},{1,13},{4,12},{5,17},{8,16},{9,21},{12,20},{13,25},{16,24},{... | collective-permute-start | bytes 98312 | tf_op jit(solution)/shard_map/ppermute | solution.py:294
  55.0 8.0 %collective-permute-start.2 = (bf16[128,128]{1,0:T(8,128)(2,1)S(1)}, bf16[128,128]{1,0:T(8,128)(2,1)S(1)}, u32[]{:S(2)}, u32[]{:S(2)}) collective-permute-start(bf16[128,128]{1,0:T(8,128)(2,1)S(1)} %get-tuple-element.27), channel_id=1, source_target_pairs={{0,508},{1,505},{2,502},{3,7},{4,0},{5,509},{6,506},{7,11},{8,4},{... | collective-permute-start | bytes 98312 | tf_op jit(solution)/shard_map/ppermute | solution.py:294
  63.9 16.3 %all-to-all-start.1 = ((bf16[4,384,128]{2,1,0:T(8,128)(2,1)}), bf16[4,384,128]{2,1,0:T(8,128)(2,1)S(1)}, u32[]{:S(2)}, u32[]{:S(2)}) async-start(bf16[4,384,128]{2,1,0:T(8,128)(2,1)} %broadcast_in_dim.11), calls=%async_computation.1 | async-start | bytes 786432 | tf_op jit(solution)/shard_map/all_to_all | solution.py:305
  68.2 12.0 %copy-start.2 = (bf16[512,256]{1,0:T(8,128)(2,1)S(1)}, bf16[512,256]{1,0:T(8,128)(2,1)}, u32[]{:S(2)}) copy-start(bf16[512,256]{1,0:T(8,128)(2,1)} %cot_far.1) | copy-start | bytes 786436

commit v5 on v3

--- a/solution.py
+++ b/solution.py
@@ -16,9 +16,8 @@
 DOM = ("zh", "zl", "y", "core")
 LANES = 128
 BACK_UNROLL = 8
-GATHER_UNROLL = 2
-SUM_UNROLL = 4
-PAIR = 4
+GATHER_UNROLL = 4
+SUM_UNROLL = 8
 VMEM_BYTES = 20 << 20
 GROUP = 16
 
@@ -29,6 +28,11 @@
 
 def ones_where(cond):
     return jnp.where(cond, 1.0, 0.0).astype(BF)
+
+
+def ones_at(row, targets):
+    rows = jnp.broadcast_to(row, targets.shape).astype(jnp.int16)
+    return jnp.where(rows == targets.astype(jnp.int16), jnp.ones((), BF), jnp.zeros((), BF))
 
 
 def iota(shape, dim):
@@ -40,7 +44,7 @@
     return sigma * (1.0 + value * (1.0 - sigma))
 
 
-def call(kernel, outs, scratch, flops, which, *args, late=()):
+def call(kernel, outs, scratch, flops, which, *args, late=(), **more):
     moved_bytes = sum(a.size * a.dtype.itemsize for a in args)
     scalars = [pl.BlockSpec(memory_space=pltpu.SMEM)] if len(which) else []
     return pl.pallas_call(
@@ -49,12 +53,26 @@
         + [pl.BlockSpec(memory_space=pltpu.VMEM)] * len(args)
         + [pl.BlockSpec(memory_space=pltpu.HBM)] * len(late),
         out_shape=outs,
+        **more,
         scratch_shapes=scratch
         + [pltpu.VMEM(a.shape, a.dtype) for a in late]
         + [pltpu.SemaphoreType.DMA] * len(late),
         compiler_params=pltpu.CompilerParams(vmem_limit_bytes=VMEM_BYTES),
         cost_estimate=pl.CostEstimate(flops=flops, bytes_accessed=moved_bytes, transcendentals=0),
     )(*([which] if len(which) else []), *args, *(pltpu.with_memory_space_constraint(a, pltpu.HBM) for a in late))
+
+
+def first_kernel(feats_ref, wdown_ref, cot_ref, wup_ref, out_far, both_ref, sems):
+    edges = feats_ref.shape[0]
+    both_ref[:edges, :] = dot(feats_ref[...], wdown_ref[...]).astype(BF)
+    both_ref[edges:, :] = dot(cot_ref[...], wup_ref[...], NT).astype(BF)
+    copies = [
+        pltpu.make_async_copy(both_ref, out_far.at[f], sems.at[f]) for f in range(out_far.shape[0])
+    ]
+    for copy in copies:
+        copy.start()
+    for copy in copies:
+        copy.wait()
 
 
 def down_kernel(both_ref, send_ref, pre_ref, bar_ref, down_ref, *out_refs):
@@ -87,9 +105,9 @@
     return tiles
 
 
-def prep_kernel(basis_ref, count_ref, by_basis_ref, by_trip_ref, live_ref):
-    _, basis, _ = by_basis_ref.shape
-    _, trips, _ = by_trip_ref.shape
+def prep_kernel(basis_ref, count_ref, by_basis_ref):
+    _, basis, lanes = by_basis_ref.shape
+    trips = lanes // GROUP
     for t in range(count_ref.shape[1] // LANES):
         lanes = slice(t * LANES, (t + 1) * LANES)
         count = count_ref[:, lanes]
@@ -99,14 +117,8 @@
             for i in range(8 * h, 8 * h + 8):
                 at = slice(i * basis, (i + 1) * basis)
                 tiles.append(jnp.where(tall > i, basis_ref[at, lanes], 0.0))
-                live_ref[at, :] = tiles[-1]
             for q, tile in enumerate(chunks_swapped(tiles)):
                 by_basis_ref[8 * t + q, :, h * LANES : (h + 1) * LANES] = tile
-        for o in range(basis // 8):
-            octet = range(8 * o, 8 * o + 8)
-            tiles = [live_ref[pl.ds(b, trips, stride=basis), :] for b in octet]
-            for q, tile in enumerate(chunks_swapped(tiles)):
-                by_trip_ref[8 * t + q, :, o * LANES : (o + 1) * LANES] = tile
 
 
 def diagonal(rows):
@@ -140,18 +152,16 @@
     rows = k_ref.shape[2]
     slots = own_ref.shape[0]
     fetch = pltpu.make_async_copy(w_far, w_ref, w_sem)
-    parts = part_sems.shape[0]
-    some = wbil_ref.shape[0] // parts
+    soon = 4
     fetch_parts = []
-    for p in range(parts):
-        at = pl.ds(p * some, some)
+    for p, at in enumerate((pl.ds(0, soon * width), pl.ds(soon * width, (basis - soon) * width))):
         fetch_parts.append(pltpu.make_async_copy(wbil_far.at[at], wbil_ref.at[at], part_sems.at[p]))
         fetch_parts[p].start()
     fetch.start()
     bar = bar_ref[...]
     for b in range(basis):
-        if b % (basis // parts) == 0:
-            fetch_parts[b // (basis // parts)].wait()
+        if b in (0, soon):
+            fetch_parts[b // soon].wait()
         grad_ref[b] = dot(bar, wbil_ref[b * width : (b + 1) * width, :], NT).astype(BF)
     acc_ref[...] = jnp.zeros_like(acc_ref)
     first = which_ref[0] * slots
@@ -164,16 +174,13 @@
     def body(g, carry):
         at = pl.ds(pl.multiple_of(g * GROUP, GROUP), GROUP)
         grad = grad_ref[:, at, :].reshape(basis * GROUP, width)
-        d_rows = dot(diagonal(w_ref[g]), grad).astype(BF)
-        k = jnp.broadcast_to(k_ref[g] - first, target.shape).astype(jnp.int16)
-        pick = jnp.where(k == target.astype(jnp.int16), jnp.ones((), BF), jnp.zeros((), BF))
-        acc_ref[...] += dot(pick, d_rows)
+        d_rows = dot(grad, diagonal(w_ref[g]), TN).astype(BF)
+        acc_ref[...] += dot(d_rows, ones_at(k_ref[g] - first, target), NT)
         return carry
 
     lax.fori_loop(0, edges // GROUP, body, 0, unroll=BACK_UNROLL)
-    own_ref[...] = acc_ref[:slots, :].astype(BF)
-    rem_a_ref[...] = acc_ref[slots : 2 * slots, :].astype(BF)
-    rem_b_ref[...] = acc_ref[2 * slots :, :].astype(BF)
+    for j, ref in enumerate((own_ref, rem_a_ref, rem_b_ref)):
+        ref[...] = acc_ref[:, j * slots : (j + 1) * slots].T.astype(BF)
 
 
 def fore_kernel(
@@ -202,48 +209,36 @@
     fetch_w.start()
     fetch_wbil.start()
     fetch_cot.start()
-    groups, rows, width = got_ref.shape
+    groups, width, rows = got_ref.shape
     basis, edges, _ = sum_ref.shape
-    trips = k_ref.shape[1]
-    tall = tab_ref.shape[0]
-    highs = tab_ref.shape[1] // width
+    table = tab_ref.shape[1]
     slots = in_ref.shape[1] // 2
     parts = [down_ref[j * slots : (j + 1) * slots, :] for j in range(edges // slots)]
     parts += [in_ref[f, :slots, :] for f in range(4)] + [in_ref[f, slots:, :] for f in range(2)]
-    highs, tall = 1, tab_ref.shape[0]
     for j, part in enumerate(parts):
-        tab_ref[j * slots : (j + 1) * slots, :] = part
-
-    def gather(n, carry):
-        lane = iota((GROUP, tall * highs), 1).astype(jnp.int16)
-        for j in range(PAIR):
-            g = n * PAIR + j
-            at = pl.ds(pl.multiple_of(g * GROUP, GROUP), GROUP)
-            k = k_ref[at, :].astype(jnp.int16)
-            picks = [
-                jnp.where(k[:, i : i + 1] == lane, jnp.ones((), BF), jnp.zeros((), BF))
-                for i in range(trips)
-            ]
-            got_ref[g] = dot(jnp.concatenate(picks, axis=0), tab_ref[...]).astype(BF)
+        tab_ref[:, j * slots : (j + 1) * slots] = part.astype(F32).T.astype(BF)
+
+    def gather(g, carry):
+        pick = ones_at(k_ref[g], iota((table, rows), 0))
+        got_ref[g] = dot(tab_ref[...], pick).astype(BF)
         return carry
 
-    lax.fori_loop(0, groups // PAIR, gather, 0, unroll=GATHER_UNROLL)
-
+    lax.fori_loop(0, groups, gather, 0, unroll=GATHER_UNROLL)
     fetch_w.wait()
 
     def add_up(g, carry):
         at = pl.ds(pl.multiple_of(g * GROUP, GROUP), GROUP)
-        total = dot(diagonal(w_ref[g]), got_ref[g]).astype(BF)
+        total = dot(diagonal(w_ref[g]), got_ref[g], NT).astype(BF)
         sum_ref[:, at, :] = total.reshape(basis, GROUP, width)
         return carry
 
     lax.fori_loop(0, groups, add_up, 0, unroll=SUM_UNROLL)
     fetch_wbil.wait()
     fetch_cot.wait()
-    agg = jnp.zeros((edges, width), F32)
+    agg = jnp.zeros((width, edges), F32)
     for b in range(0, basis, 2):
         pair = jnp.concatenate([sum_ref[b], sum_ref[b + 1]], axis=1)
-        agg = agg + dot(pair, wbil_ref[b * width : (b + 2) * width, :])
+        agg = agg + dot(wbil_ref[:, b * width : (b + 2) * width], pair, NT)
     agg = agg.astype(BF)
     bar = bar_ref[...]
     own = term_ref.shape[0] // width - cot_ref.shape[1] // width
@@ -251,7 +246,7 @@
         part = dot(sum_ref[which_ref[0] * own + j], bar, TN)
         term_ref[j * width : (j + 1) * width, :] = part.astype(BF)
     for h in range(cot_ref.shape[1] // width):
-        up = dot(agg, cot_ref[:, h * width : (h + 1) * width], TN)
+        up = dot(agg, cot_ref[:, h * width : (h + 1) * width])
         term_ref[(own + h) * width : (own + h + 1) * width, :] = up.astype(BF)
 
 
@@ -325,17 +320,24 @@
     sends = offsets[:feats], (offsets[feats:] + [None] * feats)[:feats]
     backs = [[None if o is None else -o for o in steps] for steps in sends]
 
-    part_pre = dot(edge_feats, w_down).astype(BF)
-    part_bar = dot(cotangent, w_up, NT).astype(BF)
-    both = everywhere(jnp.concatenate([part_pre, part_bar], axis=0), "feat")
-
-    by_basis, by_trip = call(
+    both = call(
+        first_kernel,
+        low(feats, 2 * edges, width),
+        [pltpu.VMEM((2 * edges, width), BF), pltpu.SemaphoreType.DMA((feats,))],
+        4 * edges * span * width,
+        (),
+        edge_feats,
+        w_down,
+        cotangent,
+        w_up,
+        out_specs=pl.BlockSpec(memory_space=pltpu.HBM),
+    )
+    both = lax.all_to_all(both, "feat", 0, 0)
+
+    by_basis = call(
         prep_kernel,
-        [
-            jax.ShapeDtypeStruct((groups, basis_total, trips * GROUP), F32),
-            jax.ShapeDtypeStruct((groups, trips, basis_total * GROUP), F32),
-        ],
-        [pltpu.VMEM((trips * basis_total, LANES), F32)],
+        jax.ShapeDtypeStruct((groups, basis_total, trips * GROUP), F32),
+        [],
         1 << 28,
         (),
         basis.reshape(trips * basis_total, edges),
@@ -365,36 +367,35 @@
         [low(slots, width)] * 3,
         [
             pltpu.VMEM((basis_total, edges, width), BF),
-            pltpu.VMEM((3 * slots, width), F32),
-            pltpu.SemaphoreType.DMA((4,)),
+            pltpu.VMEM((width, 3 * slots), F32),
+            pltpu.SemaphoreType.DMA((2,)),
         ],
         big,
         which,
         bar,
         k_rows,
-        late=(by_trip, w_bil),
+        late=(by_basis, w_bil),
     )
     back_a, back_b = moved(rem_a, backs[0]), moved(rem_b, backs[1])
 
     incoming, own = lax.optimization_barrier((jnp.concatenate([in_a, in_b], axis=0), own))
     incoming = everywhere(incoming, "feat")
-    tall = 2 * slots
     shared = everywhere(jnp.concatenate([own, back_a, back_b], axis=0), "feat")
     early = call(
         fore_kernel,
         low(own_basis * width + span, width),
         [
-            pltpu.VMEM((table, width), BF),
-            pltpu.VMEM((groups, trips * GROUP, width), BF),
+            pltpu.VMEM((width, table), BF),
+            pltpu.VMEM((groups, width, trips * GROUP), BF),
             pltpu.VMEM((basis_total, edges, width), BF),
         ],
         big,
         which,
         down,
         incoming,
-        trip_k,
+        k_rows,
         bar,
-        late=(by_basis, w_bil, cotangent),
+        late=(by_basis, w_bil.T, cotangent),
     )
     input_grad, late = call(
         last_kernel,
@@ -410,11 +411,10 @@
         edge_feats,
     )
 
-    near = ("y", "core")
+    near = ("zl", "y", "core")
     count = lax.axis_size(near)
     pieces = [early.reshape(count, -1, width), late.reshape(count, -1, width)]
     total = scattered_sum(jnp.concatenate(pieces, axis=1), near)
-    total = exchanged_sum(total, "zl")
     total = exchanged_sum(total, "zh")
     total = everywhere(total, near)
     factor = 1.0 / math.sqrt(edges * lax.axis_size(DOM))

time: 143 us -> 142 us (level)
  Pallas kernels: 28.4 us -> 24.4 us
  waiting for transfers between devices: 5.12 us -> 7.35 us
  local copies, waits for them, and re-layouts: 8.1 us -> 9.96 us
    all_to_all x3 -> x2, blocking collectives: 47.3 us -> 41.3 us  [everywhere(): return lax.all_to_all(copies, axis, 0, 0)]
    all_to_all x1, blocking collectives: 12.2 us -> 17.9 us  [scattered_sum(): arrived = lax.all_to_all(pieces, axis, 0, 0)]
    all_to_all x0 -> x1, starting transfers between devices: none -> 4.97 us  [local(): both = lax.all_to_all(both, 'feat', 0, 0)]
    all_to_all x0 -> x1, waiting for transfers between devices: none -> 4.68 us  [local(): both = lax.all_to_all(both, 'feat', 0, 0)]
    all_to_all x3 -> x2, starting transfers between devices: 12.7 us -> 8.09 us  [everywhere(): return lax.all_to_all(copies, axis, 0, 0)]
    pallas_call x6 -> x7, Pallas kernels: 28.4 us -> 24.4 us  [call(): pl.pallas_call(kernel, in_specs=scalars + [pl.BlockSpec(memory_space=pltp...]
    unnamed x21 -> x27, local copies, waits for them, and re-layouts: 4.86 us -> 7.91 us
  transfers between devices with their start and end apart: 7 -> 7, of which waited for: 2 -> 2; matrix products, arithmetic and copies ran while one was open for 1% -> 2% of each run, Pallas kernels for 18% -> 15%
where the time goes in v5:
time: 142 us; the launch traced here: 141 us
  blocking collectives  59.2 us (42%)
  starting transfers between devices  39 us (27%)
  Pallas kernels  24.4 us (17%)
  local copies, waits for them, and re-layouts  9.96 us (7%)
  waiting for transfers between devices  7.35 us (5%)
    all_to_all x2, blocking collectives, everywhere(): return lax.all_to_all(copies, axis, 0, 0)  41.3 us
    ppermute x4, starting transfers between devices, moved(): return lax.ppermute(value, (*DOM, 'feat'), pairs)  25.9 us
    pallas_call x7, Pallas kernels, call(): pl.pallas_call(kernel, in_specs=scalars + [pl.BlockSpec(memory_space=pltp...  24.4 us
    all_to_all x1, blocking collectives, scattered_sum(): arrived = lax.all_to_all(pieces, axis, 0, 0)  17.9 us
    all_to_all x2, starting transfers between devices, everywhere(): return lax.all_to_all(copies, axis, 0, 0)  8.09 us
    unnamed x27, local copies, waits for them, and re-layouts  7.91 us
    all_to_all x1, starting transfers between devices, local(): both = lax.all_to_all(both, 'feat', 0, 0)  4.97 us
    all_to_all x1, waiting for transfers between devices, local(): both = lax.all_to_all(both, 'feat', 0, 0)  4.68 us
  transfers between devices with their start and end apart: 7, of which 2 were waited for; matrix products, arithmetic and copies ran while one was open for 2% of the time, Pallas kernels for 15%

profile of v5, /device:TPU:1, one launch (start us, length us, event | category | flops | bytes accessed | tf_op | source)
XLA Modules:
  0.0 140.9 jit_solution(13494225616699735727)
XLA Ops:
  0.6 0.0 copy-start.2
  0.6 0.9 copy-done.2
  1.6 0.0 copy-start.4
  1.6 0.9 copy-done.4
  2.5 0.0 copy-start.6
  2.5 0.8 copy-done.6
  3.4 0.0 copy-start.8
  3.4 0.8 copy-done.8
  4.2 1.3 shard_map.120
  5.5 0.0 copy-start
  5.5 5.0 %all-to-all-start = ((bf16[4,1024,128]{2,1,0:T(8,128)(2,1)}), bf16[4,1024,128]{2,1,0:T(8,128)(2,1)S(1)}, u32[]{:S(2)}, u32[]{:S(2)}) async-start(bf16[4,1024,128]{2,1,0:T(8,128)(2,1)} %shard_map.120), calls=%async_computation | async-start | bytes 2097152 | tf_op jit(solution)/shard_map/all_to_all | solution.py:335
  10.5 0.0 copy-start.9
  10.5 0.7 copy-done.9
  11.2 0.0 copy-start.12
  11.2 0.1 copy.20.send_ref
  11.4 0.6 copy-done.12
  12.0 0.1 reshape.41
  12.1 0.1 copy.21
  12.2 0.1 copy.22.k_ref
  12.3 0.0 copy-start.10
  12.3 0.0 copy-done
  12.3 0.7 copy-done.10
  13.0 1.6 %shard_map.122.w_far = f32[32,32,256]{2,1,0:T(8,128)S(1)} custom-call(f32[512,512]{1,0:T(8,128)S(1)} %bitcast.15, s32[1,512]{1,0:T(1,128)S(1)} %bitcast.19), custom_call_target="tpu_custom_call" | custom-call | flops 268435456 | bytes 1050624 | tf_op jit(solution)/shard_map/pallas_call | solution.py:50
  14.6 0.0 copy-start.1
  14.6 1.0 copy-done.1
  15.6 4.7 %all-to-all-done.both_ref = bf16[4,1024,128]{2,1,0:T(8,128)(2,1)S(1)} async-done(((bf16[4,1024,128]{2,1,0:T(8,128)(2,1)}), bf16[4,1024,128]{2,1,0:T(8,128)(2,1)S(1)}, u32[]{:S(2)}, u32[]{:S(2)}) %all-to-all-start) | async-done | bytes 1048608 | tf_op jit(solution)/shard_map/all_to_all | solution.py:335
  20.3 0.4 shard_map.121
  20.6 18.1 %collective-permute-start.1 = (bf16[128,128]{1,0:T(8,128)(2,1)S(1)}, bf16[128,128]{1,0:T(8,128)(2,1)S(1)}, u32[]{:S(2)}, u32[]{:S(2)}) collective-permute-start(bf16[128,128]{1,0:T(8,128)(2,1)S(1)} %get-tuple-element.20), channel_id=1, source_target_pairs={{0,504},{1,501},{4,508},{5,505},{8,0},{9,509},{12,4},{13,1},{16,8}... | collective-permute-start | bytes 98312 | tf_op jit(solution)/shard_map/ppermute | solution.py:289
  38.7 1.9 %collective-permute-start = (bf16[128,128]{1,0:T(8,128)(2,1)S(1)}, bf16[128,128]{1,0:T(8,128)(2,1)S(1)}, u32[]{:S(2)}, u32[]{:S(2)}) collective-permute-start(bf16[128,128]{1,0:T(8,128)(2,1)S(1)} %get-tuple-element.19), channel_id=1, source_target_pairs={{0,4},{1,9},{2,14},{3,511},{4,8},{5,13},{6,18},{7,3},{8,12},{9,17}... | collective-permute-start | bytes 98312 | tf_op jit(solution)/shard_map/ppermute | solution.py:289
  40.7 0.0 copy-start.11
  40.7 9.8 %shard_map.123 = (bf16[128,128]{1,0:T(8,128)(2,1)S(1)}, bf16[128,128]{1,0:T(8,128)(2,1)S(1)}, bf16[128,128]{1,0:T(8,128)(2,1)S(1)}) custom-call(s32[1]{0:T(128)} %bitcast.3.which_ref, bf16[512,128]{1,0:T(8,128)(2,1)S(1)} %get-tuple-element.21.bar_ref, s32[32,1,256]{2,1,0:T(1,128)S(1)} %copy.22.k_ref, f32[32,32,256]{2,1,0:T(8,128)} %copy-done.1, ...), custom_call_target="tpu_custom_call" | custom-call | flops 4194304000 | bytes 163840 | tf_op jit(solution)/shard_map/pallas_call | solution.py:50
  50.4 0.0 collective-permute-done.1
  50.4 0.0 collective-permute-done
  50.5 0.7 broadcast_in_dim.9
  51.2 3.4 %all-to-all-start.2 = ((bf16[4,256,128]{2,1,0:T(8,128)(2,1)}), bf16[4,256,128]{2,1,0:T(8,128)(2,1)S(1)}, u32[]{:S(2)}, u32[]{:S(2)}) async-start(bf16[4,256,128]{2,1,0:T(8,128)(2,1)} %broadcast_in_dim.9), calls=%async_computation.2 | async-start | bytes 524288 | tf_op jit(solution)/shard_map/all_to_all | solution.py:300
  54.6 1.9 %collective-permute-start.3 = (bf16[128,128]{1,0:T(8,128)(2,1)S(1)}, bf16[128,128]{1,0:T(8,128)(2,1)S(1)}, u32[]{:S(2)}, u32[]{:S(2)}) collective-permute-start(bf16[128,128]{1,0:T(8,128)(2,1)S(1)} %get-tuple-element.25), channel_id=1, source_target_pairs={{0,8},{1,13},{4,12},{5,17},{8,16},{9,21},{12,20},{13,25},{16,24},{... | collective-permute-start | bytes 98312 | tf_op jit(solution)/shard_map/ppermute | solution.py:289
  56.5 4.0 %collective-permute-start.2 = (bf16[128,128]{1,0:T(8,128)(2,1)S(1)}, bf16[128,128]{1,0:T(8,128)(2,1)S(1)}, u32[]{:S(2)}, u32[]{:S(2)}) collective-permute-start(bf16[128,128]{1,0:T(8,128)(2,1)S(1)} %get-tuple-element.24), channel_id=1, source_target_pairs={{0,508},{1,505},{2,502},{3,7},{4,0},{5,509},{6,506},{7,11},{8,4},{... | collective-permute-start | bytes 98312 | tf_op jit(solution)/shard_map/ppermute | solution.py:289
  60.6 0.0 copy-done.11
  60.6 1.3 copy.23
  61.9 2.7 %collective-permute-done.3 = bf16[128,128]{1,0:T(8,128)(2,1)S(1)} collective-permute-done((bf16[128,128]{1,0:T(8,128)(2,1)S(1)}, bf16[128,128]{1,0:T(8,128)(2,1)S(1)}, u32[]{:S(2)}, u32[]{:S(2)}) %collective-permute-start.3) | collective-permute-done | bytes 32800 | tf_op jit(solution)/shard_map/ppermute | solution.py:289
  64.6 0.0 collective-permute-done.2
  64.6 0.8 broadcast_in_dim.8
  65.4 0.0 all-to-all-done.2.in_ref
  65.4 4.7 %all-to-all-start.1 = ((bf16[4,384,128]{2,1,0:T(8,128)(2,1)}), bf16[4,384,128]{2,1,0:T(8,128)(2,1)S(1)}, u32[]{:S(2)}, u32[]{:S(2)}) async-start(bf16[4,384,128]{2,1,0:T(8,128)(2,1)} %broadcast_in_dim.8), calls=%async_computation.1 | async-start | bytes 786432 | tf_op jit(solution)/shard_map/all_to_all | solution.py:300
  70.1 0.0 copy-start.3
  70.1 0.0 copy-start.5
  70.1 0.0 copy-start.7
  70.1 9.3 %shard_map.125 = bf16[1280,128]{1,0:T(8,128)(2,1)S(1)} custom-call(s32[1]{0:T(128)} %bitcast.3.which_ref, bf16[512,128]{1,0:T(8,128)(2,1)S(1)} %get-tuple-element.28.down_ref, bf16[4,256,128]{2,1,0:T(8,128)(2,1)S(1)} %all-to-all-done.2.in_ref, s32[32,1,256]{2,1,0:T(1,128)S(1)} %copy.22.k_ref, bf16[512,128]{1,0:T(8,128)(2,1)S(1)} %get-tuple-element.21.bar_ref, ...), custom_call_target="tpu_custom_call" | custom-call | flops 4194304000 | bytes 557056 | tf_op jit(solution)/shard_map/pallas_call | solution.py:50
  79.4 0.0 all-to-all-done.1.got_ref
  79.4 0.0 copy-done.3
  79.4 0.0 copy-done.5
  79.4 0.0 copy-done.7
  79.4 1.3 shard_map.124
  80.7 17.9 %all_to_all.30 = bf16[32,48,128]{2,1,0:T(8,128)(2,1)S(1)} all-to-all(bf16[32,48,128]{2,1,0:T(8,128)(2,1)S(1)} %pad_maximum_fusion), channel_id=1, replica_groups=mesh['zh'=4,'zl'=4,'y'=4,'core'=2,'feat'=4] {'zl','y','core'}, dimensions={0} | all-to-all | bytes 786432 | tf_op jit(solution)/shard_map/all_to_all | solution.py:293
  98.6 0.1 reduce_sum.24
  98.7 22.2 %all_to_all.31 = bf16[4,48,128]{2,1,0:T(8,128)(2,1)S(1)} all-to-all(bf16[4,48,128]{2,1,0:T(8,128)(2,1)S(1)} %broadcast_in_dim.10), channel_id=1, replica_groups=mesh['zh'=4,'zl'=4,'y'=4,'core'=2,'feat'=4] {'zh'}, dimensions={0} | all-to-all | bytes 98304 | tf_op jit(solution)/shard_map/all_to_all | solution.py:300
  120.9 0.1 broadcast_in_dim.11
  121.0 19.1 %all_to_all.32.total_ref = bf16[32,48,128]{2,1,0:T(8,128)(2,1)S(1)} all-to-all(bf16[32,48,128]{2,1,0:T(8,128)(2,1)S(1)} %broadcast_in_dim.11), channel_id=1, replica_groups=mesh['zh'=4,'zl'=4,'y'=4,'core'=2,'feat'=4] {'zl','y','core'}, dimensions={0} | all-to-all | bytes 786432 | tf_op jit(solution)/shard_map/all_to_all | solution.py:300
  140.0 0.9 shard_map.126
  (7 shorter events, 0.1 us)
Async XLA Ops:
  0.6 1.0 copy-start.2
  1.6 0.9 copy-start.4
  2.5 0.8 copy-start.6
  3.4 0.8 copy-start.8
  5.5 6.8 %copy-start = (f32[16,32,512]{2,1,0:T(8,128)S(1)}, f32[16,32,512]{2,1,0:T(8,128)}, u32[]{:S(2)}) copy-start(f32[16,32,512]{2,1,0:T(8,128)} %param.14) | copy-start | bytes 3145732
  5.5 14.7 %all-to-all-start = ((bf16[4,1024,128]{2,1,0:T(8,128)(2,1)}), bf16[4,1024,128]{2,1,0:T(8,128)(2,1)S(1)}, u32[]{:S(2)}, u32[]{:S(2)}) async-start(bf16[4,1024,128]{2,1,0:T(8,128)(2,1)} %shard_map.120), calls=%async_computation | async-start | bytes 2097152 | tf_op jit(solution)/shard_map/all_to_all | solution.py:335
  10.5 0.7 copy-start.9
  11.2 0.8 copy-start.12
  12.3 0.7 copy-start.10
  14.6 1.0 copy-start.1
  20.6 29.8 %collective-permute-start.1 = (bf16[128,128]{1,0:T(8,128)(2,1)S(1)}, bf16[128,128]{1,0:T(8,128)(2,1)S(1)}, u32[]{:S(2)}, u32[]{:S(2)}) collective-permute-start(bf16[128,128]{1,0:T(8,128)(2,1)S(1)} %get-tuple-element.20), channel_id=1, source_target_pairs={{0,504},{1,501},{4,508},{5,505},{8,0},{9,509},{12,4},{13,1},{16,8}... | collective-permute-start | bytes 98312 | tf_op jit(solution)/shard_map/ppermute | solution.py:289
  38.7 11.7 %collective-permute-start = (bf16[128,128]{1,0:T(8,128)(2,1)S(1)}, bf16[128,128]{1,0:T(8,128)(2,1)S(1)}, u32[]{:S(2)}, u32[]{:S(2)}) collective-permute-start(bf16[128,128]{1,0:T(8,128)(2,1)S(1)} %get-tuple-element.19), channel_id=1, source_target_pairs={{0,4},{1,9},{2,14},{3,511},{4,8},{5,13},{6,18},{7,3},{8,12},{9,17}... | collective-permute-start | bytes 98312 | tf_op jit(solution)/shard_map/ppermute | solution.py:289
  40.7 19.9 %copy-start.11 = (bf16[4096,128]{1,0:T(8,128)(2,1)S(1)}, bf16[4096,128]{1,0:T(8,128)(2,1)}, u32[]{:S(2)}) copy-start(bf16[4096,128]{1,0:T(8,128)(2,1)} %wbil_far.1) | copy-start | bytes 3145732
  51.2 14.2 %all-to-all-start.2 = ((bf16[4,256,128]{2,1,0:T(8,128)(2,1)}), bf16[4,256,128]{2,1,0:T(8,128)(2,1)S(1)}, u32[]{:S(2)}, u32[]{:S(2)}) async-start(bf16[4,256,128]{2,1,0:T(8,128)(2,1)} %broadcast_in_dim.9), calls=%async_computation.2 | async-start | bytes 524288 | tf_op jit(solution)/shard_map/all_to_all | solution.py:300
  54.6 10.0 %collective-permute-start.3 = (bf16[128,128]{1,0:T(8,128)(2,1)S(1)}, bf16[128,128]{1,0:T(8,128)(2,1)S(1)}, u32[]{:S(2)}, u32[]{:S(2)}) collective-permute-start(bf16[128,128]{1,0:T(8,128)(2,1)S(1)} %get-tuple-element.25), channel_id=1, source_target_pairs={{0,8},{1,13},{4,12},{5,17},{8,16},{9,21},{12,20},{13,25},{16,24},{... | collective-permute-start | bytes 98312 | tf_op jit(solution)/shard_map/ppermute | solution.py:289
  56.5 8.0 %collective-permute-start.2 = (bf16[128,128]{1,0:T(8,128)(2,1)S(1)}, bf16[128,128]{1,0:T(8,128)(2,1)S(1)}, u32[]{:S(2)}, u32[]{:S(2)}) collective-permute-start(bf16[128,128]{1,0:T(8,128)(2,1)S(1)} %get-tuple-element.24), channel_id=1, source_target_pairs={{0,508},{1,505},{2,502},{3,7},{4,0},{5,509},{6,506},{7,11},{8,4},{... | collective-permute-start | bytes 98312 | tf_op jit(solution)/shard_map/ppermute | solution.py:289
  65.4 14.0 %all-to-all-start.1 = ((bf16[4,384,128]{2,1,0:T(8,128)(2,1)}), bf16[4,384,128]{2,1,0:T(8,128)(2,1)S(1)}, u32[]{:S(2)}, u32[]{:S(2)}) async-start(bf16[4,384,128]{2,1,0:T(8,128)(2,1)} %broadcast_in_dim.8), calls=%async_computation.1 | async-start | bytes 786432 | tf_op jit(solution)/shard_map/all_to_all | solution.py:300
  70.1 9.3 %copy-start.3 = (bf16[512,256]{1,0:T(8,128)(2,1)S(1)}, bf16[512,256]{1,0:T(8,128)(2,1)}, u32[]{:S(2)}) copy-start(bf16[512,256]{1,0:T(8,128)(2,1)} %feats_ref.3) | copy-start | bytes 786436
  70.1 9.3 %copy-start.5 = (bf16[512,256]{1,0:T(8,128)(2,1)S(1)}, bf16[512,256]{1,0:T(8,128)(2,1)}, u32[]{:S(2)}) copy-start(bf16[512,256]{1,0:T(8,128)(2,1)} %cot_far.1) | copy-start | bytes 786436
  70.1 9.3 %copy-start.7 = (bf16[256,128]{1,0:T(8,128)(2,1)S(1)}, bf16[256,128]{1,0:T(8,128)(2,1)}, u32[]{:S(2)}) copy-start(bf16[256,128]{1,0:T(8,128)(2,1)} %wdown_ref.3) | copy-start | bytes 196612

commit v6 on v5

--- a/solution.py
+++ b/solution.py
@@ -22,7 +22,10 @@
 GROUP = 16
 
 
-def dot(a, b, dims=(((1,), (0,)), ((), ()))):
+PLAIN = (((1,), (0,)), ((), ()))
+
+
+def dot(a, b, dims=PLAIN):
     return lax.dot_general(a, b, dims, preferred_element_type=F32)
 
 
@@ -62,27 +65,40 @@
     )(*([which] if len(which) else []), *args, *(pltpu.with_memory_space_constraint(a, pltpu.HBM) for a in late))
 
 
-def first_kernel(feats_ref, wdown_ref, cot_ref, wup_ref, out_far, both_ref, sems):
-    edges = feats_ref.shape[0]
-    both_ref[:edges, :] = dot(feats_ref[...], wdown_ref[...]).astype(BF)
-    both_ref[edges:, :] = dot(cot_ref[...], wup_ref[...], NT).astype(BF)
-    copies = [
-        pltpu.make_async_copy(both_ref, out_far.at[f], sems.at[f]) for f in range(out_far.shape[0])
-    ]
-    for copy in copies:
-        copy.start()
+def first_kernel(feats_far, wdown_far, cot_far, wup_far, out_far, both_ref, sems, *fetched):
+    refs, in_sems = fetched[:4], fetched[4:]
+    fars = feats_far, wdown_far, cot_far, wup_far
+    fetches = [pltpu.make_async_copy(*trio) for trio in zip(fars, refs, in_sems)]
+    for fetch in fetches:
+        fetch.start()
+    count, rows, _ = out_far.shape
+    half = rows // 2
+    copies = []
+    for h, dims in enumerate((PLAIN, NT)):
+        fetches[2 * h].wait()
+        fetches[2 * h + 1].wait()
+        part = pl.ds(h * half, half)
+        both_ref[part, :] = dot(refs[2 * h][...], refs[2 * h + 1][...], dims).astype(BF)
+        for f in range(count):
+            far = out_far.at[f, part]
+            copies.append(pltpu.make_async_copy(both_ref.at[part], far, sems.at[h, f]))
+            copies[-1].start()
     for copy in copies:
         copy.wait()
 
 
-def down_kernel(both_ref, send_ref, pre_ref, bar_ref, down_ref, *out_refs):
+def summed_over(parts_ref, rows):
+    total = parts_ref[0, rows, :].astype(F32)
+    for f in range(1, parts_ref.shape[0]):
+        total = total + parts_ref[f, rows, :].astype(F32)
+    return total
+
+
+def down_kernel(parts_ref, send_ref, pre_ref, bar_ref, down_ref, *out_refs):
     edges = pre_ref.shape[0]
-    pre, bar = both_ref[0, :edges, :].astype(F32), both_ref[0, edges:, :].astype(F32)
-    for f in range(1, both_ref.shape[0]):
-        pre = pre + both_ref[f, :edges, :].astype(F32)
-        bar = bar + both_ref[f, edges:, :].astype(F32)
+    pre = summed_over(parts_ref, pl.ds(0, edges))
     pre_ref[...] = pre
-    bar_ref[...] = bar.astype(BF)
+    bar_ref[...] = summed_over(parts_ref, pl.ds(edges, edges)).astype(BF)
     down = (pre * jax.nn.sigmoid(pre)).astype(BF)
     down_ref[...] = down
     slots = out_refs[0].shape[0]
@@ -105,9 +121,9 @@
     return tiles
 
 
-def prep_kernel(basis_ref, count_ref, by_basis_ref):
-    _, basis, lanes = by_basis_ref.shape
-    trips = lanes // GROUP
+def prep_kernel(basis_ref, count_ref, wbil_ref, by_basis_ref, by_trip_ref, turned_ref, live_ref):
+    _, basis, _ = by_basis_ref.shape
+    _, trips, _ = by_trip_ref.shape
     for t in range(count_ref.shape[1] // LANES):
         lanes = slice(t * LANES, (t + 1) * LANES)
         count = count_ref[:, lanes]
@@ -117,8 +133,17 @@
             for i in range(8 * h, 8 * h + 8):
                 at = slice(i * basis, (i + 1) * basis)
                 tiles.append(jnp.where(tall > i, basis_ref[at, lanes], 0.0))
+                live_ref[at, :] = tiles[-1]
             for q, tile in enumerate(chunks_swapped(tiles)):
                 by_basis_ref[8 * t + q, :, h * LANES : (h + 1) * LANES] = tile
+        for o in range(basis // 8):
+            octet = range(8 * o, 8 * o + 8)
+            tiles = [live_ref[pl.ds(b, trips, stride=basis), :] for b in octet]
+            for q, tile in enumerate(chunks_swapped(tiles)):
+                by_trip_ref[8 * t + q, :, o * LANES : (o + 1) * LANES] = tile
+    for b in range(basis):
+        block = slice(b * LANES, (b + 1) * LANES)
+        turned_ref[:, block] = wbil_ref[block, :].astype(F32).T.astype(BF)
 
 
 def diagonal(rows):
@@ -135,7 +160,7 @@
     which_ref,
     bar_ref,
     k_ref,
-    w_far,
+    w_ref,
     wbil_far,
     own_ref,
     rem_a_ref,
@@ -143,21 +168,17 @@
     grad_ref,
     acc_ref,
     part_sems,
-    w_ref,
     wbil_ref,
-    w_sem,
     _,
 ):
     basis, edges, width = grad_ref.shape
     rows = k_ref.shape[2]
     slots = own_ref.shape[0]
-    fetch = pltpu.make_async_copy(w_far, w_ref, w_sem)
     soon = 4
     fetch_parts = []
     for p, at in enumerate((pl.ds(0, soon * width), pl.ds(soon * width, (basis - soon) * width))):
         fetch_parts.append(pltpu.make_async_copy(wbil_far.at[at], wbil_ref.at[at], part_sems.at[p]))
         fetch_parts[p].start()
-    fetch.start()
     bar = bar_ref[...]
     for b in range(basis):
         if b in (0, soon):
@@ -169,18 +190,17 @@
     block = row // slots
     jump = jnp.where(block == 0, 0, edges + (block - 1) * 4 * slots - block * slots)
     target = row + jump
-    fetch.wait()
 
     def body(g, carry):
         at = pl.ds(pl.multiple_of(g * GROUP, GROUP), GROUP)
         grad = grad_ref[:, at, :].reshape(basis * GROUP, width)
-        d_rows = dot(grad, diagonal(w_ref[g]), TN).astype(BF)
-        acc_ref[...] += dot(d_rows, ones_at(k_ref[g] - first, target), NT)
+        d_rows = dot(diagonal(w_ref[g]), grad).astype(BF)
+        acc_ref[...] += dot(ones_at(k_ref[g] - first, target), d_rows)
         return carry
 
     lax.fori_loop(0, edges // GROUP, body, 0, unroll=BACK_UNROLL)
     for j, ref in enumerate((own_ref, rem_a_ref, rem_b_ref)):
-        ref[...] = acc_ref[:, j * slots : (j + 1) * slots].T.astype(BF)
+        ref[...] = acc_ref[j * slots : (j + 1) * slots, :].astype(BF)
 
 
 def fore_kernel(
@@ -323,25 +343,27 @@
     both = call(
         first_kernel,
         low(feats, 2 * edges, width),
-        [pltpu.VMEM((2 * edges, width), BF), pltpu.SemaphoreType.DMA((feats,))],
+        [pltpu.VMEM((2 * edges, width), BF), pltpu.SemaphoreType.DMA((2, feats))],
         4 * edges * span * width,
         (),
-        edge_feats,
-        w_down,
-        cotangent,
-        w_up,
+        late=(edge_feats, w_down, cotangent, w_up),
         out_specs=pl.BlockSpec(memory_space=pltpu.HBM),
     )
     both = lax.all_to_all(both, "feat", 0, 0)
 
-    by_basis = call(
+    by_basis, by_trip, turned = call(
         prep_kernel,
-        jax.ShapeDtypeStruct((groups, basis_total, trips * GROUP), F32),
-        [],
+        [
+            jax.ShapeDtypeStruct((groups, basis_total, trips * GROUP), F32),
+            jax.ShapeDtypeStruct((groups, trips, basis_total * GROUP), F32),
+            low(width, basis_total * width),
+        ],
+        [pltpu.VMEM((trips * basis_total, LANES), F32)],
         1 << 28,
         (),
         basis.reshape(trips * basis_total, edges),
         trip_count.reshape(1, edges),
+        w_bil,
     )
     k_rows = trip_k.T.reshape(trips, groups, GROUP).transpose(1, 0, 2).reshape(groups, 1, -1)
 
@@ -349,9 +371,13 @@
     listed = jnp.concatenate([send_rows[0, feat], send_rows[0, second]]).reshape(-1, 1)
     pre, bar, down, out_a, out_b = call(
         down_kernel,
-        [jax.ShapeDtypeStruct((edges, width), F32)]
-        + [low(edges, width)] * 2
-        + [low(slots, width)] * 2,
+        [
+            jax.ShapeDtypeStruct((edges, width), F32),
+            low(edges, width),
+            low(edges, width),
+            low(slots, width),
+            low(slots, width),
+        ],
         [],
         4 * slots * edges * width,
         (),
@@ -367,14 +393,15 @@
         [low(slots, width)] * 3,
         [
             pltpu.VMEM((basis_total, edges, width), BF),
-            pltpu.VMEM((width, 3 * slots), F32),
+            pltpu.VMEM((3 * slots, width), F32),
             pltpu.SemaphoreType.DMA((2,)),
         ],
         big,
         which,
         bar,
         k_rows,
-        late=(by_basis, w_bil),
+        by_trip,
+        late=(w_bil,),
     )
     back_a, back_b = moved(rem_a, backs[0]), moved(rem_b, backs[1])
 
@@ -395,7 +422,7 @@
         incoming,
         k_rows,
         bar,
-        late=(by_basis, w_bil.T, cotangent),
+        late=(by_basis, turned, cotangent),
     )
     input_grad, late = call(
         last_kernel,
@@ -434,7 +461,7 @@
 
 
 def solution(mesh):
-    fine = Mesh(mesh.devices.reshape(4, 4, 4, 2, 4), (*DOM, "feat"))
+    fine = Mesh(mesh.devices.reshape(8, 2, 4, 2, 4), (*DOM, "feat"))
     return jax.shard_map(
         local,
         mesh=fine,

time: 142 us -> 131 us (0.923)
  blocking collectives: 59.2 us -> 49.4 us
  Pallas kernels: 24.4 us -> 28.2 us
  starting transfers between devices: 39 us -> 37.1 us
    all_to_all x1, blocking collectives: 17.9 us -> 12.2 us  [scattered_sum(): arrived = lax.all_to_all(pieces, axis, 0, 0)]
    all_to_all x1, waiting for transfers between devices: 4.68 us -> 0.01 us  [local(): both = lax.all_to_all(both, 'feat', 0, 0)]
    all_to_all x2, blocking collectives: 41.3 us -> 37.2 us  [everywhere(): return lax.all_to_all(copies, axis, 0, 0)]
    pallas_call x7, Pallas kernels: 24.4 us -> 28.2 us  [call(): pl.pallas_call(kernel, in_specs=scalars + [pl.BlockSpec(memory_space=pltp...]
    ppermute x4, waiting for transfers between devices: 2.67 us -> 6.05 us  [moved(): return lax.ppermute(value, (*DOM, 'feat'), pairs)]
    unnamed x27 -> x24, local copies, waits for them, and re-layouts: 7.91 us -> 4.92 us
    ppermute x4, starting transfers between devices: 25.9 us -> 24.1 us  [moved(): return lax.ppermute(value, (*DOM, 'feat'), pairs)]
  transfers between devices with their start and end apart: 7 -> 7, of which waited for: 2 -> 1; matrix products, arithmetic and copies ran while one was open for 2% -> 2% of each run, Pallas kernels for 15% -> 18%
where the time goes in v6:
time: 131 us; the launch traced here: 130 us
  blocking collectives  49.4 us (38%)
  starting transfers between devices  37.1 us (28%)
  Pallas kernels  28.2 us (22%)
  local copies, waits for them, and re-layouts  8.64 us (7%)
  waiting for transfers between devices  6.06 us (5%)
    all_to_all x2, blocking collectives, everywhere(): return lax.all_to_all(copies, axis, 0, 0)  37.2 us
    pallas_call x7, Pallas kernels, call(): pl.pallas_call(kernel, in_specs=scalars + [pl.BlockSpec(memory_space=pltp...  28.2 us
    ppermute x4, starting transfers between devices, moved(): return lax.ppermute(value, (*DOM, 'feat'), pairs)  24.1 us
    all_to_all x1, blocking collectives, scattered_sum(): arrived = lax.all_to_all(pieces, axis, 0, 0)  12.2 us
    all_to_all x2, starting transfers between devices, everywhere(): return lax.all_to_all(copies, axis, 0, 0)  8.05 us
    ppermute x4, waiting for transfers between devices, moved(): return lax.ppermute(value, (*DOM, 'feat'), pairs)  6.05 us
    all_to_all x1, starting transfers between devices, local(): both = lax.all_to_all(both, 'feat', 0, 0)  4.98 us
    unnamed x24, local copies, waits for them, and re-layouts  4.92 us
  transfers between devices with their start and end apart: 7, of which 1 were waited for; matrix products, arithmetic and copies ran while one was open for 2% of the time, Pallas kernels for 18%

profile of v6, /device:TPU:1, one launch (start us, length us, event | category | flops | bytes accessed | tf_op | source)
XLA Modules:
  0.0 130.4 jit_solution(8614191488979016062)
XLA Ops:
  0.6 2.4 %shard_map.120 = bf16[4,1024,128]{2,1,0:T(8,128)(2,1)} custom-call(bf16[512,256]{1,0:T(8,128)(2,1)} %feats_ref.1, bf16[256,128]{1,0:T(8,128)(2,1)} %wdown_ref.1, bf16[512,256]{1,0:T(8,128)(2,1)} %cot_far.3, bf16[128,256]{1,0:T(8,128)(2,1)} %wup_far.1), custom_call_target="tpu_custom_call" | custom-call | flops 67108864 | tf_op jit(solution)/shard_map/pallas_call | solution.py:53
  3.1 0.0 copy-start
  3.1 0.0 copy-start.1
  3.1 5.0 %all-to-all-start = ((bf16[4,1024,128]{2,1,0:T(8,128)(2,1)}), bf16[4,1024,128]{2,1,0:T(8,128)(2,1)S(1)}, u32[]{:S(2)}, u32[]{:S(2)}) async-start(bf16[4,1024,128]{2,1,0:T(8,128)(2,1)} %shard_map.120), calls=%async_computation | async-start | bytes 2097152 | tf_op jit(solution)/shard_map/all_to_all | solution.py:352
  8.1 0.0 copy-start.5
  8.1 0.7 copy-done.5
  8.8 0.0 copy-start.11
  8.8 0.1 copy.18.send_ref
  8.9 0.6 copy-done.11
  9.5 0.8 reshape.41
  10.4 1.1 copy.19
  11.4 0.1 copy.20.k_ref
  11.5 0.0 copy-start.6
  11.5 0.0 copy-done
  11.5 0.0 copy-done.1
  11.5 0.7 copy-done.6
  12.2 4.5 %shard_map.122 = (f32[32,32,256]{2,1,0:T(8,128)S(1)}, f32[32,16,512]{2,1,0:T(8,128)S(1)}, bf16[128,4096]{1,0:T(8,128)(2,1)S(1)}) custom-call(f32[512,512]{1,0:T(8,128)S(1)} %bitcast.14, s32[1,512]{1,0:T(1,128)S(1)} %bitcast.18, bf16[4096,128]{1,0:T(8,128)(2,1)S(1)} %copy-done.1), custom_call_target="tpu_custom_call" | custom-call | flops 268435456 | bytes 2099200 | tf_op jit(solution)/shard_map/pallas_call | solution.py:53
  16.7 0.0 copy-start.7
  16.7 1.0 copy-done.7
  17.7 0.0 copy-start.8
  17.7 1.0 copy-done.8
  18.7 0.0 copy-start.9
  18.7 1.0 copy-done.9
  19.7 0.0 all-to-all-done.parts_ref
  19.7 0.0 copy-start.10
  19.7 0.4 shard_map.121
  20.1 7.5 %collective-permute-start = (bf16[128,128]{1,0:T(8,128)(2,1)S(1)}, bf16[128,128]{1,0:T(8,128)(2,1)S(1)}, u32[]{:S(2)}, u32[]{:S(2)}) collective-permute-start(bf16[128,128]{1,0:T(8,128)(2,1)S(1)} %get-tuple-element.22), channel_id=1, source_target_pairs={{0,4},{1,9},{2,14},{3,511},{4,8},{5,13},{6,18},{7,3},{8,12},{9,17}... | collective-permute-start | bytes 98312 | tf_op jit(solution)/shard_map/ppermute | solution.py:309
  27.6 10.6 %collective-permute-start.1 = (bf16[128,128]{1,0:T(8,128)(2,1)S(1)}, bf16[128,128]{1,0:T(8,128)(2,1)S(1)}, u32[]{:S(2)}, u32[]{:S(2)}) collective-permute-start(bf16[128,128]{1,0:T(8,128)(2,1)S(1)} %get-tuple-element.23), channel_id=1, source_target_pairs={{0,504},{1,501},{4,508},{5,505},{8,0},{9,509},{12,4},{13,1},{16,8}... | collective-permute-start | bytes 98312 | tf_op jit(solution)/shard_map/ppermute | solution.py:309
  38.2 0.0 copy-done.10
  38.2 9.4 %shard_map.123 = (bf16[128,128]{1,0:T(8,128)(2,1)S(1)}, bf16[128,128]{1,0:T(8,128)(2,1)S(1)}, bf16[128,128]{1,0:T(8,128)(2,1)S(1)}) custom-call(s32[1]{0:T(128)} %bitcast.3.which_ref, bf16[512,128]{1,0:T(8,128)(2,1)S(1)} %get-tuple-element.24.bar_ref, s32[32,1,256]{2,1,0:T(1,128)S(1)} %copy.20.k_ref, f32[32,16,512]{2,1,0:T(8,128)S(1)} %copy-done.10, ...), custom_call_target="tpu_custom_call" | custom-call | flops 4194304000 | bytes 1212416 | tf_op jit(solution)/shard_map/pallas_call | solution.py:53
  47.7 0.0 collective-permute-done
  47.7 0.0 collective-permute-done.1
  47.7 0.7 broadcast_in_dim.9
  48.4 3.4 %all-to-all-start.2 = ((bf16[4,256,128]{2,1,0:T(8,128)(2,1)}), bf16[4,256,128]{2,1,0:T(8,128)(2,1)S(1)}, u32[]{:S(2)}, u32[]{:S(2)}) async-start(bf16[4,256,128]{2,1,0:T(8,128)(2,1)} %broadcast_in_dim.9), calls=%async_computation.2 | async-start | bytes 524288 | tf_op jit(solution)/shard_map/all_to_all | solution.py:320
  51.9 4.0 %collective-permute-start.2 = (bf16[128,128]{1,0:T(8,128)(2,1)S(1)}, bf16[128,128]{1,0:T(8,128)(2,1)S(1)}, u32[]{:S(2)}, u32[]{:S(2)}) collective-permute-start(bf16[128,128]{1,0:T(8,128)(2,1)S(1)} %get-tuple-element.28), channel_id=1, source_target_pairs={{0,508},{1,505},{2,502},{3,7},{4,0},{5,509},{6,506},{7,11},{8,4},{... | collective-permute-start | bytes 98312 | tf_op jit(solution)/shard_map/ppermute | solution.py:309
  55.9 1.9 %collective-permute-start.3 = (bf16[128,128]{1,0:T(8,128)(2,1)S(1)}, bf16[128,128]{1,0:T(8,128)(2,1)S(1)}, u32[]{:S(2)}, u32[]{:S(2)}) collective-permute-start(bf16[128,128]{1,0:T(8,128)(2,1)S(1)} %get-tuple-element.29), channel_id=1, source_target_pairs={{0,8},{1,13},{4,12},{5,17},{8,16},{9,21},{12,20},{13,25},{16,24},{... | collective-permute-start | bytes 98312 | tf_op jit(solution)/shard_map/ppermute | solution.py:309
  57.8 0.0 collective-permute-done.2
  57.8 6.0 %collective-permute-done.3 = bf16[128,128]{1,0:T(8,128)(2,1)S(1)} collective-permute-done((bf16[128,128]{1,0:T(8,128)(2,1)S(1)}, bf16[128,128]{1,0:T(8,128)(2,1)S(1)}, u32[]{:S(2)}, u32[]{:S(2)}) %collective-permute-start.3) | collective-permute-done | bytes 32800 | tf_op jit(solution)/shard_map/ppermute | solution.py:309
  63.8 0.8 broadcast_in_dim.8
  64.6 0.0 all-to-all-done.2.in_ref
  64.6 4.6 %all-to-all-start.1 = ((bf16[4,384,128]{2,1,0:T(8,128)(2,1)}), bf16[4,384,128]{2,1,0:T(8,128)(2,1)S(1)}, u32[]{:S(2)}, u32[]{:S(2)}) async-start(bf16[4,384,128]{2,1,0:T(8,128)(2,1)} %broadcast_in_dim.8), calls=%async_computation.1 | async-start | bytes 786432 | tf_op jit(solution)/shard_map/all_to_all | solution.py:320
  69.3 0.0 copy-start.2
  69.3 0.0 copy-start.3
  69.3 0.0 copy-start.4
  69.3 9.3 %shard_map.125 = bf16[1280,128]{1,0:T(8,128)(2,1)S(1)} custom-call(s32[1]{0:T(128)} %bitcast.3.which_ref, bf16[512,128]{1,0:T(8,128)(2,1)S(1)} %get-tuple-element.32.down_ref, bf16[4,256,128]{2,1,0:T(8,128)(2,1)S(1)} %all-to-all-done.2.in_ref, s32[32,1,256]{2,1,0:T(1,128)S(1)} %copy.20.k_ref, bf16[512,128]{1,0:T(8,128)(2,1)S(1)} %get-tuple-element.24.bar_ref, ...), custom_call_target="tpu_custom_call" | custom-call | flops 4194304000 | bytes 557056 | tf_op jit(solution)/shard_map/pallas_call | solution.py:53
  78.6 0.0 all-to-all-done.1.got_ref
  78.6 0.0 copy-done.2
  78.6 0.0 copy-done.3
  78.6 0.0 copy-done.4
  78.6 1.3 shard_map.124
  79.9 12.2 %all_to_all.30 = bf16[16,96,128]{2,1,0:T(8,128)(2,1)S(1)} all-to-all(bf16[16,96,128]{2,1,0:T(8,128)(2,1)S(1)} %pad_maximum_fusion), channel_id=1, replica_groups=mesh['zh'=8,'zl'=2,'y'=4,'core'=2,'feat'=4] {'zl','y','core'}, dimensions={0} | all-to-all | bytes 786432 | tf_op jit(solution)/shard_map/all_to_all | solution.py:313
  92.1 0.1 reduce_sum.24
  92.2 22.7 %all_to_all.31 = bf16[8,96,128]{2,1,0:T(8,128)(2,1)S(1)} all-to-all(bf16[8,96,128]{2,1,0:T(8,128)(2,1)S(1)} %broadcast_in_dim.10), channel_id=1, replica_groups=mesh['zh'=8,'zl'=2,'y'=4,'core'=2,'feat'=4] {'zh'}, dimensions={0} | all-to-all | bytes 393216 | tf_op jit(solution)/shard_map/all_to_all | solution.py:320
  114.9 0.1 broadcast_in_dim.11
  115.0 14.5 %all_to_all.32.total_ref = bf16[16,96,128]{2,1,0:T(8,128)(2,1)S(1)} all-to-all(bf16[16,96,128]{2,1,0:T(8,128)(2,1)S(1)} %broadcast_in_dim.11), channel_id=1, replica_groups=mesh['zh'=8,'zl'=2,'y'=4,'core'=2,'feat'=4] {'zl','y','core'}, dimensions={0} | all-to-all | bytes 786432 | tf_op jit(solution)/shard_map/all_to_all | solution.py:320
  129.5 0.9 shard_map.126
  (7 shorter events, 0.1 us)
Async XLA Ops:
  3.1 8.5 %copy-start = (f32[16,32,512]{2,1,0:T(8,128)S(1)}, f32[16,32,512]{2,1,0:T(8,128)}, u32[]{:S(2)}) copy-start(f32[16,32,512]{2,1,0:T(8,128)} %param.14) | copy-start | bytes 3145732
  3.1 8.5 %copy-start.1 = (bf16[4096,128]{1,0:T(8,128)(2,1)S(1)}, bf16[4096,128]{1,0:T(8,128)(2,1)}, u32[]{:S(2)}) copy-start(bf16[4096,128]{1,0:T(8,128)(2,1)} %wbil_far.1) | copy-start | bytes 3145732
  3.1 16.6 %all-to-all-start = ((bf16[4,1024,128]{2,1,0:T(8,128)(2,1)}), bf16[4,1024,128]{2,1,0:T(8,128)(2,1)S(1)}, u32[]{:S(2)}, u32[]{:S(2)}) async-start(bf16[4,1024,128]{2,1,0:T(8,128)(2,1)} %shard_map.120), calls=%async_computation | async-start | bytes 2097152 | tf_op jit(solution)/shard_map/all_to_all | solution.py:352
  8.1 0.7 copy-start.5
  8.8 0.8 copy-start.11
  11.5 0.7 copy-start.6
  16.7 1.0 copy-start.7
  17.7 1.0 copy-start.8
  18.7 1.0 copy-start.9
  19.7 18.6 %copy-start.10 = (f32[32,16,512]{2,1,0:T(8,128)S(1)}, f32[32,16,512]{2,1,0:T(8,128)}, u32[]{:S(2)}) copy-start(f32[32,16,512]{2,1,0:T(8,128)} %copy-done.9) | copy-start | bytes 3145732
  20.1 27.6 %collective-permute-start = (bf16[128,128]{1,0:T(8,128)(2,1)S(1)}, bf16[128,128]{1,0:T(8,128)(2,1)S(1)}, u32[]{:S(2)}, u32[]{:S(2)}) collective-permute-start(bf16[128,128]{1,0:T(8,128)(2,1)S(1)} %get-tuple-element.22), channel_id=1, source_target_pairs={{0,4},{1,9},{2,14},{3,511},{4,8},{5,13},{6,18},{7,3},{8,12},{9,17}... | collective-permute-start | bytes 98312 | tf_op jit(solution)/shard_map/ppermute | solution.py:309
  27.6 20.1 %collective-permute-start.1 = (bf16[128,128]{1,0:T(8,128)(2,1)S(1)}, bf16[128,128]{1,0:T(8,128)(2,1)S(1)}, u32[]{:S(2)}, u32[]{:S(2)}) collective-permute-start(bf16[128,128]{1,0:T(8,128)(2,1)S(1)} %get-tuple-element.23), channel_id=1, source_target_pairs={{0,504},{1,501},{4,508},{5,505},{8,0},{9,509},{12,4},{13,1},{16,8}... | collective-permute-start | bytes 98312 | tf_op jit(solution)/shard_map/ppermute | solution.py:309
  48.4 16.2 %all-to-all-start.2 = ((bf16[4,256,128]{2,1,0:T(8,128)(2,1)}), bf16[4,256,128]{2,1,0:T(8,128)(2,1)S(1)}, u32[]{:S(2)}, u32[]{:S(2)}) async-start(bf16[4,256,128]{2,1,0:T(8,128)(2,1)} %broadcast_in_dim.9), calls=%async_computation.2 | async-start | bytes 524288 | tf_op jit(solution)/shard_map/all_to_all | solution.py:320
  51.9 5.9 %collective-permute-start.2 = (bf16[128,128]{1,0:T(8,128)(2,1)S(1)}, bf16[128,128]{1,0:T(8,128)(2,1)S(1)}, u32[]{:S(2)}, u32[]{:S(2)}) collective-permute-start(bf16[128,128]{1,0:T(8,128)(2,1)S(1)} %get-tuple-element.28), channel_id=1, source_target_pairs={{0,508},{1,505},{2,502},{3,7},{4,0},{5,509},{6,506},{7,11},{8,4},{... | collective-permute-start | bytes 98312 | tf_op jit(solution)/shard_map/ppermute | solution.py:309
  55.9 8.0 %collective-permute-start.3 = (bf16[128,128]{1,0:T(8,128)(2,1)S(1)}, bf16[128,128]{1,0:T(8,128)(2,1)S(1)}, u32[]{:S(2)}, u32[]{:S(2)}) collective-permute-start(bf16[128,128]{1,0:T(8,128)(2,1)S(1)} %get-tuple-element.29), channel_id=1, source_target_pairs={{0,8},{1,13},{4,12},{5,17},{8,16},{9,21},{12,20},{13,25},{16,24},{... | collective-permute-start | bytes 98312 | tf_op jit(solution)/shard_map/ppermute | solution.py:309
  64.6 13.9 %all-to-all-start.1 = ((bf16[4,384,128]{2,1,0:T(8,128)(2,1)}), bf16[4,384,128]{2,1,0:T(8,128)(2,1)S(1)}, u32[]{:S(2)}, u32[]{:S(2)}) async-start(bf16[4,384,128]{2,1,0:T(8,128)(2,1)} %broadcast_in_dim.8), calls=%async_computation.1 | async-start | bytes 786432 | tf_op jit(solution)/shard_map/all_to_all | solution.py:320
  69.3 9.3 %copy-start.2 = (bf16[512,256]{1,0:T(8,128)(2,1)S(1)}, bf16[512,256]{1,0:T(8,128)(2,1)}, u32[]{:S(2)}) copy-start(bf16[512,256]{1,0:T(8,128)(2,1)} %feats_ref.1) | copy-start | bytes 786436
  69.3 9.3 %copy-start.3 = (bf16[512,256]{1,0:T(8,128)(2,1)S(1)}, bf16[512,256]{1,0:T(8,128)(2,1)}, u32[]{:S(2)}) copy-start(bf16[512,256]{1,0:T(8,128)(2,1)} %cot_far.3) | copy-start | bytes 786436
  69.3 9.3 %copy-start.4 = (bf16[256,128]{1,0:T(8,128)(2,1)S(1)}, bf16[256,128]{1,0:T(8,128)(2,1)}, u32[]{:S(2)}) copy-start(bf16[256,128]{1,0:T(8,128)(2,1)} %wdown_ref.1) | copy-start | bytes 196612

commit v7 on v6

--- a/solution.py
+++ b/solution.py
@@ -16,8 +16,9 @@
 DOM = ("zh", "zl", "y", "core")
 LANES = 128
 BACK_UNROLL = 8
+CHUNKS = (0, 4, 8, 16)
+STAGES = 8
 GATHER_UNROLL = 4
-SUM_UNROLL = 8
 VMEM_BYTES = 20 << 20
 GROUP = 16
 
@@ -160,7 +161,7 @@
     which_ref,
     bar_ref,
     k_ref,
-    w_ref,
+    w_far,
     wbil_far,
     own_ref,
     rem_a_ref,
@@ -168,21 +169,25 @@
     grad_ref,
     acc_ref,
     part_sems,
+    w_ref,
     wbil_ref,
+    w_sem,
     _,
 ):
     basis, edges, width = grad_ref.shape
     rows = k_ref.shape[2]
     slots = own_ref.shape[0]
-    soon = 4
-    fetch_parts = []
-    for p, at in enumerate((pl.ds(0, soon * width), pl.ds(soon * width, (basis - soon) * width))):
-        fetch_parts.append(pltpu.make_async_copy(wbil_far.at[at], wbil_ref.at[at], part_sems.at[p]))
-        fetch_parts[p].start()
+    fetches = {}
+    for p, (b, stop) in enumerate(zip(CHUNKS, (*CHUNKS[1:], basis))):
+        at = pl.ds(b * width, (stop - b) * width)
+        fetches[b] = pltpu.make_async_copy(wbil_far.at[at], wbil_ref.at[at], part_sems.at[p])
+        fetches[b].start()
+    fetch_w = pltpu.make_async_copy(w_far, w_ref, w_sem)
+    fetch_w.start()
     bar = bar_ref[...]
     for b in range(basis):
-        if b in (0, soon):
-            fetch_parts[b // soon].wait()
+        if b in fetches:
+            fetches[b].wait()
         grad_ref[b] = dot(bar, wbil_ref[b * width : (b + 1) * width, :], NT).astype(BF)
     acc_ref[...] = jnp.zeros_like(acc_ref)
     first = which_ref[0] * slots
@@ -190,6 +195,7 @@
     block = row // slots
     jump = jnp.where(block == 0, 0, edges + (block - 1) * 4 * slots - block * slots)
     target = row + jump
+    fetch_w.wait()
 
     def body(g, carry):
         at = pl.ds(pl.multiple_of(g * GROUP, GROUP), GROUP)
@@ -203,34 +209,9 @@
         ref[...] = acc_ref[j * slots : (j + 1) * slots, :].astype(BF)
 
 
-def fore_kernel(
-    which_ref,
-    down_ref,
-    in_ref,
-    k_ref,
-    bar_ref,
-    w_far,
-    wbil_far,
-    cot_far,
-    term_ref,
-    tab_ref,
-    got_ref,
-    sum_ref,
-    w_ref,
-    wbil_ref,
-    cot_ref,
-    w_sem,
-    wbil_sem,
-    cot_sem,
-):
-    fetch_w = pltpu.make_async_copy(w_far, w_ref, w_sem)
-    fetch_wbil = pltpu.make_async_copy(wbil_far, wbil_ref, wbil_sem)
-    fetch_cot = pltpu.make_async_copy(cot_far, cot_ref, cot_sem)
-    fetch_w.start()
-    fetch_wbil.start()
-    fetch_cot.start()
-    groups, width, rows = got_ref.shape
-    basis, edges, _ = sum_ref.shape
+def gather_kernel(down_ref, in_ref, k_ref, got_far, tab_ref, got_ref, sems):
+    groups, _, rows = got_ref.shape
+    edges = down_ref.shape[0]
     table = tab_ref.shape[1]
     slots = in_ref.shape[1] // 2
     parts = [down_ref[j * slots : (j + 1) * slots, :] for j in range(edges // slots)]
@@ -243,16 +224,61 @@
         got_ref[g] = dot(tab_ref[...], pick).astype(BF)
         return carry
 
-    lax.fori_loop(0, groups, gather, 0, unroll=GATHER_UNROLL)
-    fetch_w.wait()
-
-    def add_up(g, carry):
-        at = pl.ds(pl.multiple_of(g * GROUP, GROUP), GROUP)
+    some = groups // sems.shape[0]
+    copies = []
+    for p in range(sems.shape[0]):
+        lax.fori_loop(p * some, (p + 1) * some, gather, 0, unroll=GATHER_UNROLL)
+        at = pl.ds(p * some, some)
+        copies.append(pltpu.make_async_copy(got_ref.at[at], got_far.at[at], sems.at[p]))
+        copies[p].start()
+    for copy in copies:
+        copy.wait()
+
+
+def fore_kernel(
+    which_ref,
+    bar_ref,
+    w_far,
+    got_far,
+    wbil_far,
+    cot_far,
+    term_ref,
+    sum_ref,
+    sems,
+    w_ref,
+    got_ref,
+    wbil_ref,
+    cot_ref,
+    _,
+    __,
+    wbil_sem,
+    cot_sem,
+):
+    groups, width, _ = got_ref.shape
+    basis, edges, _ = sum_ref.shape
+    stages = sems.shape[1]
+    some = groups // stages
+    staged = []
+    for p in range(stages):
+        at = pl.ds(p * some, some)
+        staged.append(
+            (
+                pltpu.make_async_copy(w_far.at[at], w_ref.at[at], sems.at[0, p]),
+                pltpu.make_async_copy(got_far.at[at], got_ref.at[at], sems.at[1, p]),
+            )
+        )
+        for copy in staged[p]:
+            copy.start()
+    fetch_wbil = pltpu.make_async_copy(wbil_far, wbil_ref, wbil_sem)
+    fetch_cot = pltpu.make_async_copy(cot_far, cot_ref, cot_sem)
+    fetch_wbil.start()
+    fetch_cot.start()
+    for g in range(groups):
+        if g % some == 0:
+            for copy in staged[g // some]:
+                copy.wait()
         total = dot(diagonal(w_ref[g]), got_ref[g], NT).astype(BF)
-        sum_ref[:, at, :] = total.reshape(basis, GROUP, width)
-        return carry
-
-    lax.fori_loop(0, groups, add_up, 0, unroll=SUM_UNROLL)
+        sum_ref[:, g * GROUP : (g + 1) * GROUP, :] = total.reshape(basis, GROUP, width)
     fetch_wbil.wait()
     fetch_cot.wait()
     agg = jnp.zeros((width, edges), F32)
@@ -271,7 +297,7 @@
 
 
 def last_kernel(got_ref, pre_ref, send_ref, wdown_ref, cot_ref, feats_ref, grad_ref, term_ref):
-    edges, span = cot_ref.shape
+    edges, _ = cot_ref.shape
     share = edges // got_ref.shape[0]
     feats = got_ref.shape[0]
     part = lambda j: [got_ref[f, j * share : (j + 1) * share, :] for f in range(feats)]
@@ -324,7 +350,7 @@
     return jnp.sum(everywhere(value, axis).astype(F32), axis=0).astype(BF)
 
 
-def local(edge_feats, cotangent, w_down, w_up, w_bil, basis, trip_k, trip_count, send_rows):
+def steps(edge_feats, cotangent, w_down, w_up, w_bil, basis, trip_k, trip_count, send_rows):
     edges, span = edge_feats.shape
     width = w_down.shape[1]
     trips, basis_total, _ = basis.shape
@@ -394,35 +420,43 @@
         [
             pltpu.VMEM((basis_total, edges, width), BF),
             pltpu.VMEM((3 * slots, width), F32),
-            pltpu.SemaphoreType.DMA((2,)),
+            pltpu.SemaphoreType.DMA((len(CHUNKS),)),
         ],
         big,
         which,
         bar,
         k_rows,
-        by_trip,
-        late=(w_bil,),
-    )
-    back_a, back_b = moved(rem_a, backs[0]), moved(rem_b, backs[1])
+        late=(by_trip, w_bil),
+    )
+    back_a = moved(rem_a, backs[0])
+    back_b = moved(rem_b, backs[1])
 
     incoming, own = lax.optimization_barrier((jnp.concatenate([in_a, in_b], axis=0), own))
     incoming = everywhere(incoming, "feat")
     shared = everywhere(jnp.concatenate([own, back_a, back_b], axis=0), "feat")
+    got = call(
+        gather_kernel,
+        pltpu.HBM((groups, width, trips * GROUP), BF),
+        [
+            pltpu.VMEM((width, table), BF),
+            pltpu.VMEM((groups, width, trips * GROUP), BF),
+            pltpu.SemaphoreType.DMA((4,)),
+        ],
+        big // 2,
+        (),
+        down,
+        incoming,
+        k_rows,
+        out_specs=pl.BlockSpec(memory_space=pltpu.HBM),
+    )
     early = call(
         fore_kernel,
         low(own_basis * width + span, width),
-        [
-            pltpu.VMEM((width, table), BF),
-            pltpu.VMEM((groups, width, trips * GROUP), BF),
-            pltpu.VMEM((basis_total, edges, width), BF),
-        ],
+        [pltpu.VMEM((basis_total, edges, width), BF), pltpu.SemaphoreType.DMA((2, STAGES))],
         big,
         which,
-        down,
-        incoming,
-        k_rows,
         bar,
-        late=(by_basis, turned, cotangent),
+        late=(by_basis, got, turned, cotangent),
     )
     input_grad, late = call(
         last_kernel,
@@ -463,7 +497,7 @@
 def solution(mesh):
     fine = Mesh(mesh.devices.reshape(8, 2, 4, 2, 4), (*DOM, "feat"))
     return jax.shard_map(
-        local,
+        steps,
         mesh=fine,
         in_specs=(
             P(DOM, "feat"),

time: 131 us -> 134 us (1.023)
  Pallas kernels: 28.2 us -> 31.1 us
  local copies, waits for them, and re-layouts: 8.64 us -> 6.69 us
  starting transfers between devices: 37.1 us -> 38.8 us
    pallas_call x7 -> x8, Pallas kernels: 28.2 us -> 31.1 us  [call(): pl.pallas_call(kernel, in_specs=scalars + [pl.BlockSpec(memory_space=pltp...]
    unnamed x24 -> x22, local copies, waits for them, and re-layouts: 4.92 us -> 2.96 us
    ppermute x4, starting transfers between devices: 24.1 us -> 25.9 us  [moved(): return lax.ppermute(value, (*DOM, 'feat'), pairs)]
  transfers between devices with their start and end apart: 7 -> 7, of which waited for: 1 -> 2; matrix products, arithmetic and copies ran while one was open for 2% -> 2% of each run, Pallas kernels for 18% -> 19%
where the time goes in v7:
time: 134 us; the launch traced here: 133 us
  blocking collectives  49.5 us (37%)
  starting transfers between devices  38.8 us (29%)
  Pallas kernels  31.1 us (23%)
  local copies, waits for them, and re-layouts  6.69 us (5%)
  waiting for transfers between devices  6.16 us (5%)
    all_to_all x2, blocking collectives, everywhere(): return lax.all_to_all(copies, axis, 0, 0)  37.2 us
    pallas_call x8, Pallas kernels, call(): pl.pallas_call(kernel, in_specs=scalars + [pl.BlockSpec(memory_space=pltp...  31.1 us
    ppermute x4, starting transfers between devices, moved(): return lax.ppermute(value, (*DOM, 'feat'), pairs)  25.9 us
    all_to_all x1, blocking collectives, scattered_sum(): arrived = lax.all_to_all(pieces, axis, 0, 0)  12.4 us
    all_to_all x2, starting transfers between devices, everywhere(): return lax.all_to_all(copies, axis, 0, 0)  8.07 us
    ppermute x4, waiting for transfers between devices, moved(): return lax.ppermute(value, (*DOM, 'feat'), pairs)  6.05 us
    all_to_all x1, starting transfers between devices, steps(): both = lax.all_to_all(both, 'feat', 0, 0)  4.84 us
    unnamed x22, local copies, waits for them, and re-layouts  2.96 us
  transfers between devices with their start and end apart: 7, of which 2 were waited for; matrix products, arithmetic and copies ran while one was open for 2% of the time, Pallas kernels for 19%

profile of v7, /device:TPU:1, one launch (start us, length us, event | category | flops | bytes accessed | tf_op | source)
XLA Modules:
  0.0 133.4 jit_solution(8553623324598116955)
XLA Ops:
  0.6 0.0 copy-start.5
  0.6 0.0 copy-start.10
  0.7 0.0 copy-start.1
  0.7 0.0 copy-start.6
  0.7 0.0 copy-start
  0.7 2.6 %shard_map.120 = bf16[4,1024,128]{2,1,0:T(8,128)(2,1)} custom-call(bf16[512,256]{1,0:T(8,128)(2,1)} %feats_ref.1, bf16[256,128]{1,0:T(8,128)(2,1)} %wdown_ref.1, bf16[512,256]{1,0:T(8,128)(2,1)} %cot_far.3, bf16[128,256]{1,0:T(8,128)(2,1)} %wup_far.1), custom_call_target="tpu_custom_call" | custom-call | flops 67108864 | tf_op jit(solution)/shard_map/pallas_call | solution.py:54
  3.3 4.8 %all-to-all-start = ((bf16[4,1024,128]{2,1,0:T(8,128)(2,1)}), bf16[4,1024,128]{2,1,0:T(8,128)(2,1)S(1)}, u32[]{:S(2)}, u32[]{:S(2)}) async-start(bf16[4,1024,128]{2,1,0:T(8,128)(2,1)} %shard_map.120), calls=%async_computation | async-start | bytes 2097152 | tf_op jit(solution)/shard_map/all_to_all | solution.py:378
  8.1 0.0 copy-done.5
  8.1 0.1 copy.18.send_ref
  8.3 0.0 copy-done.10
  8.3 0.8 reshape.41
  9.1 1.1 copy.19
  10.2 0.1 copy.20.k_ref
  10.3 0.0 copy-done.1
  10.3 0.0 copy-done.6
  10.3 0.0 copy-done
  10.3 4.5 %shard_map.122 = (f32[32,32,256]{2,1,0:T(8,128)S(1)}, f32[32,16,512]{2,1,0:T(8,128)S(1)}, bf16[128,4096]{1,0:T(8,128)(2,1)S(1)}) custom-call(f32[512,512]{1,0:T(8,128)S(1)} %bitcast.14, s32[1,512]{1,0:T(1,128)S(1)} %bitcast.18, bf16[4096,128]{1,0:T(8,128)(2,1)S(1)} %copy-done.1), custom_call_target="tpu_custom_call" | custom-call | flops 268435456 | bytes 2099200 | tf_op jit(solution)/shard_map/pallas_call | solution.py:54
  14.8 0.0 copy-start.7
  14.8 1.0 copy-done.7
  15.8 0.0 copy-start.8
  15.8 1.0 copy-done.8
  16.8 0.0 copy-start.9
  16.8 1.0 copy-done.9
  17.7 0.1 all-to-all-done.parts_ref
  17.8 0.4 shard_map.121
  18.2 9.4 %collective-permute-start = (bf16[128,128]{1,0:T(8,128)(2,1)S(1)}, bf16[128,128]{1,0:T(8,128)(2,1)S(1)}, u32[]{:S(2)}, u32[]{:S(2)}) collective-permute-start(bf16[128,128]{1,0:T(8,128)(2,1)S(1)} %get-tuple-element.22), channel_id=1, source_target_pairs={{0,4},{1,9},{2,14},{3,511},{4,8},{5,13},{6,18},{7,3},{8,12},{9,17}... | collective-permute-start | bytes 98312 | tf_op jit(solution)/shard_map/ppermute | solution.py:335
  27.7 10.6 %collective-permute-start.1 = (bf16[128,128]{1,0:T(8,128)(2,1)S(1)}, bf16[128,128]{1,0:T(8,128)(2,1)S(1)}, u32[]{:S(2)}, u32[]{:S(2)}) collective-permute-start(bf16[128,128]{1,0:T(8,128)(2,1)S(1)} %get-tuple-element.23), channel_id=1, source_target_pairs={{0,504},{1,501},{4,508},{5,505},{8,0},{9,509},{12,4},{13,1},{16,8}... | collective-permute-start | bytes 98312 | tf_op jit(solution)/shard_map/ppermute | solution.py:335
  38.3 9.7 %shard_map.123 = (bf16[128,128]{1,0:T(8,128)(2,1)S(1)}, bf16[128,128]{1,0:T(8,128)(2,1)S(1)}, bf16[128,128]{1,0:T(8,128)(2,1)S(1)}) custom-call(s32[1]{0:T(128)} %bitcast.3.which_ref, bf16[512,128]{1,0:T(8,128)(2,1)S(1)} %get-tuple-element.24.bar_ref, s32[32,1,256]{2,1,0:T(1,128)S(1)} %copy.20.k_ref, f32[32,16,512]{2,1,0:T(8,128)} %copy-done.9, ...), custom_call_target="tpu_custom_call" | custom-call | flops 4194304000 | bytes 163840 | tf_op jit(solution)/shard_map/pallas_call | solution.py:54
  48.0 0.0 collective-permute-done
  48.0 0.0 collective-permute-done.1
  48.0 0.7 broadcast_in_dim.9
  48.7 3.4 %all-to-all-start.2 = ((bf16[4,256,128]{2,1,0:T(8,128)(2,1)}), bf16[4,256,128]{2,1,0:T(8,128)(2,1)S(1)}, u32[]{:S(2)}, u32[]{:S(2)}) async-start(bf16[4,256,128]{2,1,0:T(8,128)(2,1)} %broadcast_in_dim.9), calls=%async_computation.2 | async-start | bytes 524288 | tf_op jit(solution)/shard_map/all_to_all | solution.py:346
  52.1 4.0 %collective-permute-start.2 = (bf16[128,128]{1,0:T(8,128)(2,1)S(1)}, bf16[128,128]{1,0:T(8,128)(2,1)S(1)}, u32[]{:S(2)}, u32[]{:S(2)}) collective-permute-start(bf16[128,128]{1,0:T(8,128)(2,1)S(1)} %get-tuple-element.28), channel_id=1, source_target_pairs={{0,508},{1,505},{2,502},{3,7},{4,0},{5,509},{6,506},{7,11},{8,4},{... | collective-permute-start | bytes 98312 | tf_op jit(solution)/shard_map/ppermute | solution.py:335
  56.1 1.9 %collective-permute-start.3 = (bf16[128,128]{1,0:T(8,128)(2,1)S(1)}, bf16[128,128]{1,0:T(8,128)(2,1)S(1)}, u32[]{:S(2)}, u32[]{:S(2)}) collective-permute-start(bf16[128,128]{1,0:T(8,128)(2,1)S(1)} %get-tuple-element.29), channel_id=1, source_target_pairs={{0,8},{1,13},{4,12},{5,17},{8,16},{9,21},{12,20},{13,25},{16,24},{... | collective-permute-start | bytes 98312 | tf_op jit(solution)/shard_map/ppermute | solution.py:335
  58.1 0.0 collective-permute-done.2
  58.1 6.0 %collective-permute-done.3 = bf16[128,128]{1,0:T(8,128)(2,1)S(1)} collective-permute-done((bf16[128,128]{1,0:T(8,128)(2,1)S(1)}, bf16[128,128]{1,0:T(8,128)(2,1)S(1)}, u32[]{:S(2)}, u32[]{:S(2)}) %collective-permute-start.3) | collective-permute-done | bytes 32800 | tf_op jit(solution)/shard_map/ppermute | solution.py:335
  64.1 0.8 broadcast_in_dim.8
  64.9 0.0 all-to-all-done.2.in_ref
  64.9 4.7 %all-to-all-start.1 = ((bf16[4,384,128]{2,1,0:T(8,128)(2,1)}), bf16[4,384,128]{2,1,0:T(8,128)(2,1)S(1)}, u32[]{:S(2)}, u32[]{:S(2)}) async-start(bf16[4,384,128]{2,1,0:T(8,128)(2,1)} %broadcast_in_dim.8), calls=%async_computation.1 | async-start | bytes 786432 | tf_op jit(solution)/shard_map/all_to_all | solution.py:346
  69.6 5.2 %shard_map.125.got_far = bf16[32,128,256]{2,1,0:T(8,128)(2,1)} custom-call(bf16[512,128]{1,0:T(8,128)(2,1)S(1)} %get-tuple-element.33.down_ref, bf16[4,256,128]{2,1,0:T(8,128)(2,1)S(1)} %all-to-all-done.2.in_ref, s32[32,1,256]{2,1,0:T(1,128)S(1)} %copy.20.k_ref), custom_call_target="tpu_custom_call" | custom-call | flops 2097152000 | bytes 425984 | tf_op jit(solution)/shard_map/pallas_call | solution.py:54
  74.8 0.0 copy-start.2
  74.8 0.0 copy-start.3
  74.8 0.0 copy-start.4
  74.8 6.6 %shard_map.126 = bf16[1280,128]{1,0:T(8,128)(2,1)S(1)} custom-call(s32[1]{0:T(128)} %bitcast.3.which_ref, bf16[512,128]{1,0:T(8,128)(2,1)S(1)} %get-tuple-element.24.bar_ref, f32[32,32,256]{2,1,0:T(8,128)} %copy-done.7, bf16[32,128,256]{2,1,0:T(8,128)(2,1)} %shard_map.125.got_far, bf16[128,4096]{1,0:T(8,128)(2,1)} %copy-done.8, bf16[512,256]{1,0:T(8,128)(2,1)} %cot_far.3), custom_call_target="tpu_custom_call" | custom-call | flops 4194304000 | bytes 131072 | tf_op jit(solution)/shard_map/pallas_call | solution.py:54
  81.4 0.0 all-to-all-done.1.got_ref
  81.4 0.0 copy-done.2
  81.4 0.0 copy-done.3
  81.4 0.0 copy-done.4
  81.5 1.3 shard_map.124
  82.7 12.4 %all_to_all.30 = bf16[16,96,128]{2,1,0:T(8,128)(2,1)S(1)} all-to-all(bf16[16,96,128]{2,1,0:T(8,128)(2,1)S(1)} %pad_maximum_fusion), channel_id=1, replica_groups=mesh['zh'=8,'zl'=2,'y'=4,'core'=2,'feat'=4] {'zl','y','core'}, dimensions={0} | all-to-all | bytes 786432 | tf_op jit(solution)/shard_map/all_to_all | solution.py:339
  95.1 0.1 reduce_sum.24
  95.2 22.7 %all_to_all.31 = bf16[8,96,128]{2,1,0:T(8,128)(2,1)S(1)} all-to-all(bf16[8,96,128]{2,1,0:T(8,128)(2,1)S(1)} %broadcast_in_dim.10), channel_id=1, replica_groups=mesh['zh'=8,'zl'=2,'y'=4,'core'=2,'feat'=4] {'zh'}, dimensions={0} | all-to-all | bytes 393216 | tf_op jit(solution)/shard_map/all_to_all | solution.py:346
  117.9 0.1 broadcast_in_dim.11
  118.0 14.5 %all_to_all.32.total_ref = bf16[16,96,128]{2,1,0:T(8,128)(2,1)S(1)} all-to-all(bf16[16,96,128]{2,1,0:T(8,128)(2,1)S(1)} %broadcast_in_dim.11), channel_id=1, replica_groups=mesh['zh'=8,'zl'=2,'y'=4,'core'=2,'feat'=4] {'zl','y','core'}, dimensions={0} | all-to-all | bytes 786432 | tf_op jit(solution)/shard_map/all_to_all | solution.py:346
  132.5 0.9 shard_map.127
  (7 shorter events, 0.1 us)
Async XLA Ops:
  0.6 7.5 %copy-start.5 = (s32[1,6,128]{2,0,1:T(1,128)S(1)}, s32[1,6,128]{2,0,1:T(1,128)}, u32[]{:S(2)}) copy-start(s32[1,6,128]{2,0,1:T(1,128)} %param.17) | copy-start | bytes 9220
  0.6 7.6 %copy-start.10 = (s32[512,16]{0,1:T(8,128)S(1)}, s32[512,16]{0,1:T(8,128)}, u32[]{:S(2)}) copy-start(s32[512,16]{0,1:T(8,128)} %param.15) | copy-start | bytes 98308
  0.7 9.6 %copy-start.1 = (bf16[4096,128]{1,0:T(8,128)(2,1)S(1)}, bf16[4096,128]{1,0:T(8,128)(2,1)}, u32[]{:S(2)}) copy-start(bf16[4096,128]{1,0:T(8,128)(2,1)} %wbil_far.1) | copy-start | bytes 3145732
  0.7 9.6 %copy-start.6 = (s32[512]{0:T(512)S(1)}, s32[512]{0:T(512)}, u32[]{:S(2)}) copy-start(s32[512]{0:T(512)} %param.16) | copy-start | bytes 6148
  0.7 9.6 %copy-start = (f32[16,32,512]{2,1,0:T(8,128)S(1)}, f32[16,32,512]{2,1,0:T(8,128)}, u32[]{:S(2)}) copy-start(f32[16,32,512]{2,1,0:T(8,128)} %param.14) | copy-start | bytes 3145732
  3.3 14.6 %all-to-all-start = ((bf16[4,1024,128]{2,1,0:T(8,128)(2,1)}), bf16[4,1024,128]{2,1,0:T(8,128)(2,1)S(1)}, u32[]{:S(2)}, u32[]{:S(2)}) async-start(bf16[4,1024,128]{2,1,0:T(8,128)(2,1)} %shard_map.120), calls=%async_computation | async-start | bytes 2097152 | tf_op jit(solution)/shard_map/all_to_all | solution.py:378
  14.8 1.0 copy-start.7
  15.8 1.0 copy-start.8
  16.8 1.0 copy-start.9
  18.2 29.7 %collective-permute-start = (bf16[128,128]{1,0:T(8,128)(2,1)S(1)}, bf16[128,128]{1,0:T(8,128)(2,1)S(1)}, u32[]{:S(2)}, u32[]{:S(2)}) collective-permute-start(bf16[128,128]{1,0:T(8,128)(2,1)S(1)} %get-tuple-element.22), channel_id=1, source_target_pairs={{0,4},{1,9},{2,14},{3,511},{4,8},{5,13},{6,18},{7,3},{8,12},{9,17}... | collective-permute-start | bytes 98312 | tf_op jit(solution)/shard_map/ppermute | solution.py:335
  27.7 20.3 %collective-permute-start.1 = (bf16[128,128]{1,0:T(8,128)(2,1)S(1)}, bf16[128,128]{1,0:T(8,128)(2,1)S(1)}, u32[]{:S(2)}, u32[]{:S(2)}) collective-permute-start(bf16[128,128]{1,0:T(8,128)(2,1)S(1)} %get-tuple-element.23), channel_id=1, source_target_pairs={{0,504},{1,501},{4,508},{5,505},{8,0},{9,509},{12,4},{13,1},{16,8}... | collective-permute-start | bytes 98312 | tf_op jit(solution)/shard_map/ppermute | solution.py:335
  48.7 16.2 %all-to-all-start.2 = ((bf16[4,256,128]{2,1,0:T(8,128)(2,1)}), bf16[4,256,128]{2,1,0:T(8,128)(2,1)S(1)}, u32[]{:S(2)}, u32[]{:S(2)}) async-start(bf16[4,256,128]{2,1,0:T(8,128)(2,1)} %broadcast_in_dim.9), calls=%async_computation.2 | async-start | bytes 524288 | tf_op jit(solution)/shard_map/all_to_all | solution.py:346
  52.1 5.9 %collective-permute-start.2 = (bf16[128,128]{1,0:T(8,128)(2,1)S(1)}, bf16[128,128]{1,0:T(8,128)(2,1)S(1)}, u32[]{:S(2)}, u32[]{:S(2)}) collective-permute-start(bf16[128,128]{1,0:T(8,128)(2,1)S(1)} %get-tuple-element.28), channel_id=1, source_target_pairs={{0,508},{1,505},{2,502},{3,7},{4,0},{5,509},{6,506},{7,11},{8,4},{... | collective-permute-start | bytes 98312 | tf_op jit(solution)/shard_map/ppermute | solution.py:335
  56.1 8.0 %collective-permute-start.3 = (bf16[128,128]{1,0:T(8,128)(2,1)S(1)}, bf16[128,128]{1,0:T(8,128)(2,1)S(1)}, u32[]{:S(2)}, u32[]{:S(2)}) collective-permute-start(bf16[128,128]{1,0:T(8,128)(2,1)S(1)} %get-tuple-element.29), channel_id=1, source_target_pairs={{0,8},{1,13},{4,12},{5,17},{8,16},{9,21},{12,20},{13,25},{16,24},{... | collective-permute-start | bytes 98312 | tf_op jit(solution)/shard_map/ppermute | solution.py:335
  64.9 16.5 %all-to-all-start.1 = ((bf16[4,384,128]{2,1,0:T(8,128)(2,1)}), bf16[4,384,128]{2,1,0:T(8,128)(2,1)S(1)}, u32[]{:S(2)}, u32[]{:S(2)}) async-start(bf16[4,384,128]{2,1,0:T(8,128)(2,1)} %broadcast_in_dim.8), calls=%async_computation.1 | async-start | bytes 786432 | tf_op jit(solution)/shard_map/all_to_all | solution.py:346
  74.8 6.6 %copy-start.2 = (bf16[512,256]{1,0:T(8,128)(2,1)S(1)}, bf16[512,256]{1,0:T(8,128)(2,1)}, u32[]{:S(2)}) copy-start(bf16[512,256]{1,0:T(8,128)(2,1)} %feats_ref.1) | copy-start | bytes 786436
  74.8 6.6 %copy-start.3 = (bf16[512,256]{1,0:T(8,128)(2,1)S(1)}, bf16[512,256]{1,0:T(8,128)(2,1)}, u32[]{:S(2)}) copy-start(bf16[512,256]{1,0:T(8,128)(2,1)} %cot_far.3) | copy-start | bytes 786436
  74.8 6.6 %copy-start.4 = (bf16[256,128]{1,0:T(8,128)(2,1)S(1)}, bf16[256,128]{1,0:T(8,128)(2,1)}, u32[]{:S(2)}) copy-start(bf16[256,128]{1,0:T(8,128)(2,1)} %wdown_ref.1) | copy-start | bytes 196612

commit v8 on v7

--- a/solution.py
+++ b/solution.py
@@ -15,7 +15,6 @@
 TN = (((0,), (0,)), ((), ()))
 DOM = ("zh", "zl", "y", "core")
 LANES = 128
-BACK_UNROLL = 8
 CHUNKS = (0, 4, 8, 16)
 STAGES = 8
 GATHER_UNROLL = 4
@@ -136,18 +135,19 @@
                 tiles.append(jnp.where(tall > i, basis_ref[at, lanes], 0.0))
                 live_ref[at, :] = tiles[-1]
             for q, tile in enumerate(chunks_swapped(tiles)):
-                by_basis_ref[8 * t + q, :, h * LANES : (h + 1) * LANES] = tile
+                by_basis_ref[8 * t + q, :, h * LANES : (h + 1) * LANES] = tile.astype(BF)
         for o in range(basis // 8):
             octet = range(8 * o, 8 * o + 8)
             tiles = [live_ref[pl.ds(b, trips, stride=basis), :] for b in octet]
             for q, tile in enumerate(chunks_swapped(tiles)):
-                by_trip_ref[8 * t + q, :, o * LANES : (o + 1) * LANES] = tile
+                by_trip_ref[8 * t + q, :, o * LANES : (o + 1) * LANES] = tile.astype(BF)
     for b in range(basis):
         block = slice(b * LANES, (b + 1) * LANES)
         turned_ref[:, block] = wbil_ref[block, :].astype(F32).T.astype(BF)
 
 
 def diagonal(rows):
+    rows = rows.astype(F32)
     count, lanes = rows.shape
     same = iota((GROUP, lanes), 0) == iota((GROUP, lanes), 1) % GROUP
     parts = []
@@ -169,10 +169,11 @@
     grad_ref,
     acc_ref,
     part_sems,
+    w_sems,
     w_ref,
     wbil_ref,
-    w_sem,
     _,
+    __,
 ):
     basis, edges, width = grad_ref.shape
     rows = k_ref.shape[2]
@@ -182,8 +183,13 @@
         at = pl.ds(b * width, (stop - b) * width)
         fetches[b] = pltpu.make_async_copy(wbil_far.at[at], wbil_ref.at[at], part_sems.at[p])
         fetches[b].start()
-    fetch_w = pltpu.make_async_copy(w_far, w_ref, w_sem)
-    fetch_w.start()
+    groups = edges // GROUP
+    some = groups // w_sems.shape[0]
+    staged = []
+    for p in range(groups // some):
+        at = pl.ds(p * some, some)
+        staged.append(pltpu.make_async_copy(w_far.at[at], w_ref.at[at], w_sems.at[p]))
+        staged[p].start()
     bar = bar_ref[...]
     for b in range(basis):
         if b in fetches:
@@ -195,16 +201,12 @@
     block = row // slots
     jump = jnp.where(block == 0, 0, edges + (block - 1) * 4 * slots - block * slots)
     target = row + jump
-    fetch_w.wait()
-
-    def body(g, carry):
-        at = pl.ds(pl.multiple_of(g * GROUP, GROUP), GROUP)
-        grad = grad_ref[:, at, :].reshape(basis * GROUP, width)
+    for g in range(groups):
+        if g % some == 0:
+            staged[g // some].wait()
+        grad = grad_ref[:, g * GROUP : (g + 1) * GROUP, :].reshape(basis * GROUP, width)
         d_rows = dot(diagonal(w_ref[g]), grad).astype(BF)
         acc_ref[...] += dot(ones_at(k_ref[g] - first, target), d_rows)
-        return carry
-
-    lax.fori_loop(0, edges // GROUP, body, 0, unroll=BACK_UNROLL)
     for j, ref in enumerate((own_ref, rem_a_ref, rem_b_ref)):
         ref[...] = acc_ref[j * slots : (j + 1) * slots, :].astype(BF)
 
@@ -380,8 +382,8 @@
     by_basis, by_trip, turned = call(
         prep_kernel,
         [
-            jax.ShapeDtypeStruct((groups, basis_total, trips * GROUP), F32),
-            jax.ShapeDtypeStruct((groups, trips, basis_total * GROUP), F32),
+            low(groups, basis_total, trips * GROUP),
+            low(groups, trips, basis_total * GROUP),
             low(width, basis_total * width),
         ],
         [pltpu.VMEM((trips * basis_total, LANES), F32)],
@@ -421,6 +423,7 @@
             pltpu.VMEM((basis_total, edges, width), BF),
             pltpu.VMEM((3 * slots, width), F32),
             pltpu.SemaphoreType.DMA((len(CHUNKS),)),
+            pltpu.SemaphoreType.DMA((STAGES,)),
         ],
         big,
         which,
@@ -440,7 +443,7 @@
         [
             pltpu.VMEM((width, table), BF),
             pltpu.VMEM((groups, width, trips * GROUP), BF),
-            pltpu.SemaphoreType.DMA((4,)),
+            pltpu.SemaphoreType.DMA((STAGES,)),
         ],
         big // 2,
         (),

time: 134 us -> 133 us (level)
  Pallas kernels: 31.1 us -> 29.6 us
    pallas_call x8, Pallas kernels: 31.1 us -> 29.6 us  [call(): pl.pallas_call(kernel, in_specs=scalars + [pl.BlockSpec(memory_space=pltp...]
  transfers between devices with their start and end apart: 7 -> 7, of which waited for: 2 -> 2; matrix products, arithmetic and copies ran while one was open for 2% -> 2% of each run, Pallas kernels for 19% -> 18%
where the time goes in v8:
time: 133 us; the launch traced here: 132 us
  blocking collectives  49.5 us (37%)
  starting transfers between devices  38.8 us (29%)
  Pallas kernels  29.6 us (22%)
  waiting for transfers between devices  7.15 us (5%)
  local copies, waits for them, and re-layouts  6.31 us (5%)
    all_to_all x2, blocking collectives, everywhere(): return lax.all_to_all(copies, axis, 0, 0)  37.2 us
    pallas_call x8, Pallas kernels, call(): pl.pallas_call(kernel, in_specs=scalars + [pl.BlockSpec(memory_space=pltp...  29.6 us
    ppermute x4, starting transfers between devices, moved(): return lax.ppermute(value, (*DOM, 'feat'), pairs)  25.9 us
    all_to_all x1, blocking collectives, scattered_sum(): arrived = lax.all_to_all(pieces, axis, 0, 0)  12.4 us
    all_to_all x2, starting transfers between devices, everywhere(): return lax.all_to_all(copies, axis, 0, 0)  8.07 us
    ppermute x4, waiting for transfers between devices, moved(): return lax.ppermute(value, (*DOM, 'feat'), pairs)  6.05 us
    all_to_all x1, starting transfers between devices, steps(): both = lax.all_to_all(both, 'feat', 0, 0)  4.84 us
  transfers between devices with their start and end apart: 7, of which 2 were waited for; matrix products, arithmetic and copies ran while one was open for 2% of the time, Pallas kernels for 18%

profile of v8, /device:TPU:1, one launch (start us, length us, event | category | flops | bytes accessed | tf_op | source)
XLA Modules:
  0.0 132.5 jit_solution(16312385916970806229)
XLA Ops:
  0.6 0.0 copy-start.5
  0.6 0.0 copy-start.10
  0.7 0.0 copy-start.1
  0.7 0.0 copy-start.6
  0.7 0.0 copy-start
  0.7 2.6 %shard_map.120 = bf16[4,1024,128]{2,1,0:T(8,128)(2,1)} custom-call(bf16[512,256]{1,0:T(8,128)(2,1)} %feats_ref.1, bf16[256,128]{1,0:T(8,128)(2,1)} %wdown_ref.1, bf16[512,256]{1,0:T(8,128)(2,1)} %cot_far.3, bf16[128,256]{1,0:T(8,128)(2,1)} %wup_far.1), custom_call_target="tpu_custom_call" | custom-call | flops 67108864 | tf_op jit(solution)/shard_map/pallas_call | solution.py:53
  3.3 4.8 %all-to-all-start = ((bf16[4,1024,128]{2,1,0:T(8,128)(2,1)}), bf16[4,1024,128]{2,1,0:T(8,128)(2,1)S(1)}, u32[]{:S(2)}, u32[]{:S(2)}) async-start(bf16[4,1024,128]{2,1,0:T(8,128)(2,1)} %shard_map.120), calls=%async_computation | async-start | bytes 2097152 | tf_op jit(solution)/shard_map/all_to_all | solution.py:380
  8.1 0.0 copy-done.5
  8.1 0.1 copy.18.send_ref
  8.3 0.0 copy-done.10
  8.3 0.8 reshape.41
  9.1 1.1 copy.19
  10.2 0.1 copy.20.k_ref
  10.3 0.0 copy-done.1
  10.3 0.0 copy-done.6
  10.3 0.0 copy-done
  10.3 3.9 %shard_map.122 = (bf16[32,32,256]{2,1,0:T(8,128)(2,1)S(1)}, bf16[32,16,512]{2,1,0:T(8,128)(2,1)S(1)}, bf16[128,4096]{1,0:T(8,128)(2,1)S(1)}) custom-call(f32[512,512]{1,0:T(8,128)S(1)} %bitcast.14, s32[1,512]{1,0:T(1,128)S(1)} %bitcast.18, bf16[4096,128]{1,0:T(8,128)(2,1)S(1)} %copy-done.1), custom_call_target="tpu_custom_call" | custom-call | flops 268435456 | bytes 2099200 | tf_op jit(solution)/shard_map/pallas_call | solution.py:53
  14.2 0.0 copy-start.7
  14.2 1.0 copy-done.7
  15.2 0.0 copy-start.8
  15.2 0.8 copy-done.8
  16.0 0.0 copy-start.9
  16.0 0.8 copy-done.9
  16.8 1.1 all-to-all-done.parts_ref
  17.8 0.4 shard_map.121
  18.2 9.4 %collective-permute-start = (bf16[128,128]{1,0:T(8,128)(2,1)S(1)}, bf16[128,128]{1,0:T(8,128)(2,1)S(1)}, u32[]{:S(2)}, u32[]{:S(2)}) collective-permute-start(bf16[128,128]{1,0:T(8,128)(2,1)S(1)} %get-tuple-element.22), channel_id=1, source_target_pairs={{0,4},{1,9},{2,14},{3,511},{4,8},{5,13},{6,18},{7,3},{8,12},{9,17}... | collective-permute-start | bytes 98312 | tf_op jit(solution)/shard_map/ppermute | solution.py:337
  27.7 10.6 %collective-permute-start.1 = (bf16[128,128]{1,0:T(8,128)(2,1)S(1)}, bf16[128,128]{1,0:T(8,128)(2,1)S(1)}, u32[]{:S(2)}, u32[]{:S(2)}) collective-permute-start(bf16[128,128]{1,0:T(8,128)(2,1)S(1)} %get-tuple-element.23), channel_id=1, source_target_pairs={{0,504},{1,501},{4,508},{5,505},{8,0},{9,509},{12,4},{13,1},{16,8}... | collective-permute-start | bytes 98312 | tf_op jit(solution)/shard_map/ppermute | solution.py:337
  38.3 10.2 %shard_map.123 = (bf16[128,128]{1,0:T(8,128)(2,1)S(1)}, bf16[128,128]{1,0:T(8,128)(2,1)S(1)}, bf16[128,128]{1,0:T(8,128)(2,1)S(1)}) custom-call(s32[1]{0:T(128)} %bitcast.3.which_ref, bf16[512,128]{1,0:T(8,128)(2,1)S(1)} %get-tuple-element.24.bar_ref, s32[32,1,256]{2,1,0:T(1,128)S(1)} %copy.20.k_ref, bf16[32,16,512]{2,1,0:T(8,128)(2,1)} %copy-done.9, ...), custom_call_target="tpu_custom_call" | custom-call | flops 4194304000 | bytes 163840 | tf_op jit(solution)/shard_map/pallas_call | solution.py:53
  48.5 0.0 collective-permute-done
  48.5 0.0 collective-permute-done.1
  48.5 0.7 broadcast_in_dim.9
  49.3 3.4 %all-to-all-start.2 = ((bf16[4,256,128]{2,1,0:T(8,128)(2,1)}), bf16[4,256,128]{2,1,0:T(8,128)(2,1)S(1)}, u32[]{:S(2)}, u32[]{:S(2)}) async-start(bf16[4,256,128]{2,1,0:T(8,128)(2,1)} %broadcast_in_dim.9), calls=%async_computation.2 | async-start | bytes 524288 | tf_op jit(solution)/shard_map/all_to_all | solution.py:348
  52.7 4.0 %collective-permute-start.2 = (bf16[128,128]{1,0:T(8,128)(2,1)S(1)}, bf16[128,128]{1,0:T(8,128)(2,1)S(1)}, u32[]{:S(2)}, u32[]{:S(2)}) collective-permute-start(bf16[128,128]{1,0:T(8,128)(2,1)S(1)} %get-tuple-element.28), channel_id=1, source_target_pairs={{0,508},{1,505},{2,502},{3,7},{4,0},{5,509},{6,506},{7,11},{8,4},{... | collective-permute-start | bytes 98312 | tf_op jit(solution)/shard_map/ppermute | solution.py:337
  56.7 1.9 %collective-permute-start.3 = (bf16[128,128]{1,0:T(8,128)(2,1)S(1)}, bf16[128,128]{1,0:T(8,128)(2,1)S(1)}, u32[]{:S(2)}, u32[]{:S(2)}) collective-permute-start(bf16[128,128]{1,0:T(8,128)(2,1)S(1)} %get-tuple-element.29), channel_id=1, source_target_pairs={{0,8},{1,13},{4,12},{5,17},{8,16},{9,21},{12,20},{13,25},{16,24},{... | collective-permute-start | bytes 98312 | tf_op jit(solution)/shard_map/ppermute | solution.py:337
  58.6 0.0 collective-permute-done.2
  58.6 6.0 %collective-permute-done.3 = bf16[128,128]{1,0:T(8,128)(2,1)S(1)} collective-permute-done((bf16[128,128]{1,0:T(8,128)(2,1)S(1)}, bf16[128,128]{1,0:T(8,128)(2,1)S(1)}, u32[]{:S(2)}, u32[]{:S(2)}) %collective-permute-start.3) | collective-permute-done | bytes 32800 | tf_op jit(solution)/shard_map/ppermute | solution.py:337
  64.7 0.8 broadcast_in_dim.8
  65.5 0.0 all-to-all-done.2.in_ref
  65.5 4.7 %all-to-all-start.1 = ((bf16[4,384,128]{2,1,0:T(8,128)(2,1)}), bf16[4,384,128]{2,1,0:T(8,128)(2,1)S(1)}, u32[]{:S(2)}, u32[]{:S(2)}) async-start(bf16[4,384,128]{2,1,0:T(8,128)(2,1)} %broadcast_in_dim.8), calls=%async_computation.1 | async-start | bytes 786432 | tf_op jit(solution)/shard_map/all_to_all | solution.py:348
  70.2 3.7 %shard_map.125.got_far = bf16[32,128,256]{2,1,0:T(8,128)(2,1)} custom-call(bf16[512,128]{1,0:T(8,128)(2,1)S(1)} %get-tuple-element.33.down_ref, bf16[4,256,128]{2,1,0:T(8,128)(2,1)S(1)} %all-to-all-done.2.in_ref, s32[32,1,256]{2,1,0:T(1,128)S(1)} %copy.20.k_ref), custom_call_target="tpu_custom_call" | custom-call | flops 2097152000 | bytes 425984 | tf_op jit(solution)/shard_map/pallas_call | solution.py:53
  73.9 0.0 copy-start.2
  73.9 0.0 copy-start.3
  73.9 0.0 copy-start.4
  73.9 6.6 %shard_map.126 = bf16[1280,128]{1,0:T(8,128)(2,1)S(1)} custom-call(s32[1]{0:T(128)} %bitcast.3.which_ref, bf16[512,128]{1,0:T(8,128)(2,1)S(1)} %get-tuple-element.24.bar_ref, bf16[32,32,256]{2,1,0:T(8,128)(2,1)} %copy-done.8, bf16[32,128,256]{2,1,0:T(8,128)(2,1)} %shard_map.125.got_far, bf16[128,4096]{1,0:T(8,128)(2,1)} %copy-done.7, bf16[512,256]{1,0:T(8,128)(2,1)} %cot_far.3), custom_call_target="tpu_custom_call" | custom-call | flops 4194304000 | bytes 131072 | tf_op jit(solution)/shard_map/pallas_call | solution.py:53
  80.5 0.0 all-to-all-done.1.got_ref
  80.5 0.0 copy-done.2
  80.5 0.0 copy-done.3
  80.6 0.0 copy-done.4
  80.6 1.3 shard_map.124
  81.9 12.4 %all_to_all.30 = bf16[16,96,128]{2,1,0:T(8,128)(2,1)S(1)} all-to-all(bf16[16,96,128]{2,1,0:T(8,128)(2,1)S(1)} %pad_maximum_fusion), channel_id=1, replica_groups=mesh['zh'=8,'zl'=2,'y'=4,'core'=2,'feat'=4] {'zl','y','core'}, dimensions={0} | all-to-all | bytes 786432 | tf_op jit(solution)/shard_map/all_to_all | solution.py:341
  94.2 0.1 reduce_sum.24
  94.3 22.7 %all_to_all.31 = bf16[8,96,128]{2,1,0:T(8,128)(2,1)S(1)} all-to-all(bf16[8,96,128]{2,1,0:T(8,128)(2,1)S(1)} %broadcast_in_dim.10), channel_id=1, replica_groups=mesh['zh'=8,'zl'=2,'y'=4,'core'=2,'feat'=4] {'zh'}, dimensions={0} | all-to-all | bytes 393216 | tf_op jit(solution)/shard_map/all_to_all | solution.py:348
  117.0 0.1 broadcast_in_dim.11
  117.1 14.5 %all_to_all.32.total_ref = bf16[16,96,128]{2,1,0:T(8,128)(2,1)S(1)} all-to-all(bf16[16,96,128]{2,1,0:T(8,128)(2,1)S(1)} %broadcast_in_dim.11), channel_id=1, replica_groups=mesh['zh'=8,'zl'=2,'y'=4,'core'=2,'feat'=4] {'zl','y','core'}, dimensions={0} | all-to-all | bytes 786432 | tf_op jit(solution)/shard_map/all_to_all | solution.py:348
  131.6 0.9 shard_map.127
  (7 shorter events, 0.1 us)
Async XLA Ops:
  0.6 7.5 %copy-start.5 = (s32[1,6,128]{2,0,1:T(1,128)S(1)}, s32[1,6,128]{2,0,1:T(1,128)}, u32[]{:S(2)}) copy-start(s32[1,6,128]{2,0,1:T(1,128)} %param.17) | copy-start | bytes 9220
  0.6 7.6 %copy-start.10 = (s32[512,16]{0,1:T(8,128)S(1)}, s32[512,16]{0,1:T(8,128)}, u32[]{:S(2)}) copy-start(s32[512,16]{0,1:T(8,128)} %param.15) | copy-start | bytes 98308
  0.7 9.6 %copy-start.1 = (bf16[4096,128]{1,0:T(8,128)(2,1)S(1)}, bf16[4096,128]{1,0:T(8,128)(2,1)}, u32[]{:S(2)}) copy-start(bf16[4096,128]{1,0:T(8,128)(2,1)} %wbil_far.1) | copy-start | bytes 3145732
  0.7 9.6 %copy-start.6 = (s32[512]{0:T(512)S(1)}, s32[512]{0:T(512)}, u32[]{:S(2)}) copy-start(s32[512]{0:T(512)} %param.16) | copy-start | bytes 6148
  0.7 9.6 %copy-start = (f32[16,32,512]{2,1,0:T(8,128)S(1)}, f32[16,32,512]{2,1,0:T(8,128)}, u32[]{:S(2)}) copy-start(f32[16,32,512]{2,1,0:T(8,128)} %param.14) | copy-start | bytes 3145732
  3.3 14.6 %all-to-all-start = ((bf16[4,1024,128]{2,1,0:T(8,128)(2,1)}), bf16[4,1024,128]{2,1,0:T(8,128)(2,1)S(1)}, u32[]{:S(2)}, u32[]{:S(2)}) async-start(bf16[4,1024,128]{2,1,0:T(8,128)(2,1)} %shard_map.120), calls=%async_computation | async-start | bytes 2097152 | tf_op jit(solution)/shard_map/all_to_all | solution.py:380
  14.2 1.0 copy-start.7
  15.2 0.8 copy-start.8
  16.0 0.8 copy-start.9
  18.2 30.3 %collective-permute-start = (bf16[128,128]{1,0:T(8,128)(2,1)S(1)}, bf16[128,128]{1,0:T(8,128)(2,1)S(1)}, u32[]{:S(2)}, u32[]{:S(2)}) collective-permute-start(bf16[128,128]{1,0:T(8,128)(2,1)S(1)} %get-tuple-element.22), channel_id=1, source_target_pairs={{0,4},{1,9},{2,14},{3,511},{4,8},{5,13},{6,18},{7,3},{8,12},{9,17}... | collective-permute-start | bytes 98312 | tf_op jit(solution)/shard_map/ppermute | solution.py:337
  27.7 20.9 %collective-permute-start.1 = (bf16[128,128]{1,0:T(8,128)(2,1)S(1)}, bf16[128,128]{1,0:T(8,128)(2,1)S(1)}, u32[]{:S(2)}, u32[]{:S(2)}) collective-permute-start(bf16[128,128]{1,0:T(8,128)(2,1)S(1)} %get-tuple-element.23), channel_id=1, source_target_pairs={{0,504},{1,501},{4,508},{5,505},{8,0},{9,509},{12,4},{13,1},{16,8}... | collective-permute-start | bytes 98312 | tf_op jit(solution)/shard_map/ppermute | solution.py:337
  49.3 16.2 %all-to-all-start.2 = ((bf16[4,256,128]{2,1,0:T(8,128)(2,1)}), bf16[4,256,128]{2,1,0:T(8,128)(2,1)S(1)}, u32[]{:S(2)}, u32[]{:S(2)}) async-start(bf16[4,256,128]{2,1,0:T(8,128)(2,1)} %broadcast_in_dim.9), calls=%async_computation.2 | async-start | bytes 524288 | tf_op jit(solution)/shard_map/all_to_all | solution.py:348
  52.7 5.9 %collective-permute-start.2 = (bf16[128,128]{1,0:T(8,128)(2,1)S(1)}, bf16[128,128]{1,0:T(8,128)(2,1)S(1)}, u32[]{:S(2)}, u32[]{:S(2)}) collective-permute-start(bf16[128,128]{1,0:T(8,128)(2,1)S(1)} %get-tuple-element.28), channel_id=1, source_target_pairs={{0,508},{1,505},{2,502},{3,7},{4,0},{5,509},{6,506},{7,11},{8,4},{... | collective-permute-start | bytes 98312 | tf_op jit(solution)/shard_map/ppermute | solution.py:337
  56.7 8.0 %collective-permute-start.3 = (bf16[128,128]{1,0:T(8,128)(2,1)S(1)}, bf16[128,128]{1,0:T(8,128)(2,1)S(1)}, u32[]{:S(2)}, u32[]{:S(2)}) collective-permute-start(bf16[128,128]{1,0:T(8,128)(2,1)S(1)} %get-tuple-element.29), channel_id=1, source_target_pairs={{0,8},{1,13},{4,12},{5,17},{8,16},{9,21},{12,20},{13,25},{16,24},{... | collective-permute-start | bytes 98312 | tf_op jit(solution)/shard_map/ppermute | solution.py:337
  65.5 15.0 %all-to-all-start.1 = ((bf16[4,384,128]{2,1,0:T(8,128)(2,1)}), bf16[4,384,128]{2,1,0:T(8,128)(2,1)S(1)}, u32[]{:S(2)}, u32[]{:S(2)}) async-start(bf16[4,384,128]{2,1,0:T(8,128)(2,1)} %broadcast_in_dim.8), calls=%async_computation.1 | async-start | bytes 786432 | tf_op jit(solution)/shard_map/all_to_all | solution.py:348
  73.9 6.6 %copy-start.2 = (bf16[512,256]{1,0:T(8,128)(2,1)S(1)}, bf16[512,256]{1,0:T(8,128)(2,1)}, u32[]{:S(2)}) copy-start(bf16[512,256]{1,0:T(8,128)(2,1)} %feats_ref.1) | copy-start | bytes 786436
  73.9 6.6 %copy-start.3 = (bf16[512,256]{1,0:T(8,128)(2,1)S(1)}, bf16[512,256]{1,0:T(8,128)(2,1)}, u32[]{:S(2)}) copy-start(bf16[512,256]{1,0:T(8,128)(2,1)} %cot_far.3) | copy-start | bytes 786436
  73.9 6.6 %copy-start.4 = (bf16[256,128]{1,0:T(8,128)(2,1)S(1)}, bf16[256,128]{1,0:T(8,128)(2,1)}, u32[]{:S(2)}) copy-start(bf16[256,128]{1,0:T(8,128)(2,1)} %wdown_ref.1) | copy-start | bytes 196612

commit v9 on v8

--- a/solution.py
+++ b/solution.py
@@ -17,6 +17,8 @@
 LANES = 128
 CHUNKS = (0, 4, 8, 16)
 STAGES = 8
+HALVES = 2
+UNROLL = 4
 GATHER_UNROLL = 4
 VMEM_BYTES = 20 << 20
 GROUP = 16
@@ -201,12 +203,17 @@
     block = row // slots
     jump = jnp.where(block == 0, 0, edges + (block - 1) * 4 * slots - block * slots)
     target = row + jump
-    for g in range(groups):
-        if g % some == 0:
-            staged[g // some].wait()
-        grad = grad_ref[:, g * GROUP : (g + 1) * GROUP, :].reshape(basis * GROUP, width)
+
+    def body(g, carry):
+        at = pl.ds(pl.multiple_of(g * GROUP, GROUP), GROUP)
+        grad = grad_ref[:, at, :].reshape(basis * GROUP, width)
         d_rows = dot(diagonal(w_ref[g]), grad).astype(BF)
         acc_ref[...] += dot(ones_at(k_ref[g] - first, target), d_rows)
+        return carry
+
+    for p in range(groups // some):
+        staged[p].wait()
+        lax.fori_loop(p * some, (p + 1) * some, body, 0, unroll=UNROLL)
     for j, ref in enumerate((own_ref, rem_a_ref, rem_b_ref)):
         ref[...] = acc_ref[j * slots : (j + 1) * slots, :].astype(BF)
 
@@ -275,12 +282,17 @@
     fetch_cot = pltpu.make_async_copy(cot_far, cot_ref, cot_sem)
     fetch_wbil.start()
     fetch_cot.start()
-    for g in range(groups):
-        if g % some == 0:
-            for copy in staged[g // some]:
-                copy.wait()
+
+    def add_up(g, carry):
+        at = pl.ds(pl.multiple_of(g * GROUP, GROUP), GROUP)
         total = dot(diagonal(w_ref[g]), got_ref[g], NT).astype(BF)
-        sum_ref[:, g * GROUP : (g + 1) * GROUP, :] = total.reshape(basis, GROUP, width)
+        sum_ref[:, at, :] = total.reshape(basis, GROUP, width)
+        return carry
+
+    for p in range(stages):
+        for copy in staged[p]:
+            copy.wait()
+        lax.fori_loop(p * some, (p + 1) * some, add_up, 0, unroll=UNROLL)
     fetch_wbil.wait()
     fetch_cot.wait()
     agg = jnp.zeros((width, edges), F32)
@@ -423,7 +435,7 @@
             pltpu.VMEM((basis_total, edges, width), BF),
             pltpu.VMEM((3 * slots, width), F32),
             pltpu.SemaphoreType.DMA((len(CHUNKS),)),
-            pltpu.SemaphoreType.DMA((STAGES,)),
+            pltpu.SemaphoreType.DMA((HALVES,)),
         ],
         big,
         which,
@@ -455,7 +467,7 @@
     early = call(
         fore_kernel,
         low(own_basis * width + span, width),
-        [pltpu.VMEM((basis_total, edges, width), BF), pltpu.SemaphoreType.DMA((2, STAGES))],
+        [pltpu.VMEM((basis_total, edges, width), BF), pltpu.SemaphoreType.DMA((2, HALVES))],
         big,
         which,
         bar,

time: 133 us -> 135 us (1.015)
  Pallas kernels: 29.6 us -> 31.7 us
    pallas_call x8, Pallas kernels: 29.6 us -> 31.7 us  [call(): pl.pallas_call(kernel, in_specs=scalars + [pl.BlockSpec(memory_space=pltp...]
  transfers between devices with their start and end apart: 7 -> 7, of which waited for: 2 -> 2; matrix products, arithmetic and copies ran while one was open for 2% -> 2% of each run, Pallas kernels for 18% -> 20%
where the time goes in v9:
time: 135 us; the launch traced here: 134 us
  blocking collectives  49.3 us (37%)
  starting transfers between devices  38.8 us (29%)
  Pallas kernels  31.7 us (23%)
  waiting for transfers between devices  7.15 us (5%)
  local copies, waits for them, and re-layouts  6.31 us (5%)
    all_to_all x2, blocking collectives, everywhere(): return lax.all_to_all(copies, axis, 0, 0)  37.2 us
    pallas_call x8, Pallas kernels, call(): pl.pallas_call(kernel, in_specs=scalars + [pl.BlockSpec(memory_space=pltp...  31.7 us
    ppermute x4, starting transfers between devices, moved(): return lax.ppermute(value, (*DOM, 'feat'), pairs)  25.9 us
    all_to_all x1, blocking collectives, scattered_sum(): arrived = lax.all_to_all(pieces, axis, 0, 0)  12.2 us
    all_to_all x2, starting transfers between devices, everywhere(): return lax.all_to_all(copies, axis, 0, 0)  8.07 us
    ppermute x4, waiting for transfers between devices, moved(): return lax.ppermute(value, (*DOM, 'feat'), pairs)  6.05 us
    all_to_all x1, starting transfers between devices, steps(): both = lax.all_to_all(both, 'feat', 0, 0)  4.84 us
  transfers between devices with their start and end apart: 7, of which 2 were waited for; matrix products, arithmetic and copies ran while one was open for 2% of the time, Pallas kernels for 20%

profile of v9, /device:TPU:1, one launch (start us, length us, event | category | flops | bytes accessed | tf_op | source)
XLA Modules:
  0.0 134.4 jit_solution(1423574667483162102)
XLA Ops:
  0.6 0.0 copy-start.5
  0.6 0.0 copy-start.10
  0.7 0.0 copy-start.1
  0.7 0.0 copy-start.6
  0.7 0.0 copy-start
  0.7 2.6 %shard_map.120 = bf16[4,1024,128]{2,1,0:T(8,128)(2,1)} custom-call(bf16[512,256]{1,0:T(8,128)(2,1)} %feats_ref.1, bf16[256,128]{1,0:T(8,128)(2,1)} %wdown_ref.1, bf16[512,256]{1,0:T(8,128)(2,1)} %cot_far.3, bf16[128,256]{1,0:T(8,128)(2,1)} %wup_far.1), custom_call_target="tpu_custom_call" | custom-call | flops 67108864 | tf_op jit(solution)/shard_map/pallas_call | solution.py:55
  3.3 4.8 %all-to-all-start = ((bf16[4,1024,128]{2,1,0:T(8,128)(2,1)}), bf16[4,1024,128]{2,1,0:T(8,128)(2,1)S(1)}, u32[]{:S(2)}, u32[]{:S(2)}) async-start(bf16[4,1024,128]{2,1,0:T(8,128)(2,1)} %shard_map.120), calls=%async_computation | async-start | bytes 2097152 | tf_op jit(solution)/shard_map/all_to_all | solution.py:392
  8.1 0.0 copy-done.5
  8.1 0.1 copy.18.send_ref
  8.3 0.0 copy-done.10
  8.3 0.8 reshape.41
  9.1 1.1 copy.19
  10.2 0.1 copy.20.k_ref
  10.3 0.0 copy-done.1
  10.3 0.0 copy-done.6
  10.3 0.0 copy-done
  10.3 3.9 %shard_map.122 = (bf16[32,32,256]{2,1,0:T(8,128)(2,1)S(1)}, bf16[32,16,512]{2,1,0:T(8,128)(2,1)S(1)}, bf16[128,4096]{1,0:T(8,128)(2,1)S(1)}) custom-call(f32[512,512]{1,0:T(8,128)S(1)} %bitcast.14, s32[1,512]{1,0:T(1,128)S(1)} %bitcast.18, bf16[4096,128]{1,0:T(8,128)(2,1)S(1)} %copy-done.1), custom_call_target="tpu_custom_call" | custom-call | flops 268435456 | bytes 2099200 | tf_op jit(solution)/shard_map/pallas_call | solution.py:55
  14.2 0.0 copy-start.7
  14.2 1.0 copy-done.7
  15.2 0.0 copy-start.8
  15.2 0.8 copy-done.8
  16.0 0.0 copy-start.9
  16.0 0.8 copy-done.9
  16.8 1.1 all-to-all-done.parts_ref
  17.8 0.4 shard_map.121
  18.2 9.4 %collective-permute-start = (bf16[128,128]{1,0:T(8,128)(2,1)S(1)}, bf16[128,128]{1,0:T(8,128)(2,1)S(1)}, u32[]{:S(2)}, u32[]{:S(2)}) collective-permute-start(bf16[128,128]{1,0:T(8,128)(2,1)S(1)} %get-tuple-element.22), channel_id=1, source_target_pairs={{0,4},{1,9},{2,14},{3,511},{4,8},{5,13},{6,18},{7,3},{8,12},{9,17}... | collective-permute-start | bytes 98312 | tf_op jit(solution)/shard_map/ppermute | solution.py:349
  27.6 10.6 %collective-permute-start.1 = (bf16[128,128]{1,0:T(8,128)(2,1)S(1)}, bf16[128,128]{1,0:T(8,128)(2,1)S(1)}, u32[]{:S(2)}, u32[]{:S(2)}) collective-permute-start(bf16[128,128]{1,0:T(8,128)(2,1)S(1)} %get-tuple-element.23), channel_id=1, source_target_pairs={{0,504},{1,501},{4,508},{5,505},{8,0},{9,509},{12,4},{13,1},{16,8}... | collective-permute-start | bytes 98312 | tf_op jit(solution)/shard_map/ppermute | solution.py:349
  38.3 12.0 %shard_map.123 = (bf16[128,128]{1,0:T(8,128)(2,1)S(1)}, bf16[128,128]{1,0:T(8,128)(2,1)S(1)}, bf16[128,128]{1,0:T(8,128)(2,1)S(1)}) custom-call(s32[1]{0:T(128)} %bitcast.3.which_ref, bf16[512,128]{1,0:T(8,128)(2,1)S(1)} %get-tuple-element.24.bar_ref, s32[32,1,256]{2,1,0:T(1,128)S(1)} %copy.20.k_ref, bf16[32,16,512]{2,1,0:T(8,128)(2,1)} %copy-done.9, ...), custom_call_target="tpu_custom_call" | custom-call | flops 4194304000 | bytes 163840 | tf_op jit(solution)/shard_map/pallas_call | solution.py:55
  50.2 0.0 collective-permute-done
  50.2 0.0 collective-permute-done.1
  50.3 0.7 broadcast_in_dim.9
  51.0 3.4 %all-to-all-start.2 = ((bf16[4,256,128]{2,1,0:T(8,128)(2,1)}), bf16[4,256,128]{2,1,0:T(8,128)(2,1)S(1)}, u32[]{:S(2)}, u32[]{:S(2)}) async-start(bf16[4,256,128]{2,1,0:T(8,128)(2,1)} %broadcast_in_dim.9), calls=%async_computation.2 | async-start | bytes 524288 | tf_op jit(solution)/shard_map/all_to_all | solution.py:360
  54.4 4.0 %collective-permute-start.2 = (bf16[128,128]{1,0:T(8,128)(2,1)S(1)}, bf16[128,128]{1,0:T(8,128)(2,1)S(1)}, u32[]{:S(2)}, u32[]{:S(2)}) collective-permute-start(bf16[128,128]{1,0:T(8,128)(2,1)S(1)} %get-tuple-element.28), channel_id=1, source_target_pairs={{0,508},{1,505},{2,502},{3,7},{4,0},{5,509},{6,506},{7,11},{8,4},{... | collective-permute-start | bytes 98312 | tf_op jit(solution)/shard_map/ppermute | solution.py:349
  58.4 1.9 %collective-permute-start.3 = (bf16[128,128]{1,0:T(8,128)(2,1)S(1)}, bf16[128,128]{1,0:T(8,128)(2,1)S(1)}, u32[]{:S(2)}, u32[]{:S(2)}) collective-permute-start(bf16[128,128]{1,0:T(8,128)(2,1)S(1)} %get-tuple-element.29), channel_id=1, source_target_pairs={{0,8},{1,13},{4,12},{5,17},{8,16},{9,21},{12,20},{13,25},{16,24},{... | collective-permute-start | bytes 98312 | tf_op jit(solution)/shard_map/ppermute | solution.py:349
  60.4 0.0 collective-permute-done.2
  60.4 6.0 %collective-permute-done.3 = bf16[128,128]{1,0:T(8,128)(2,1)S(1)} collective-permute-done((bf16[128,128]{1,0:T(8,128)(2,1)S(1)}, bf16[128,128]{1,0:T(8,128)(2,1)S(1)}, u32[]{:S(2)}, u32[]{:S(2)}) %collective-permute-start.3) | collective-permute-done | bytes 32800 | tf_op jit(solution)/shard_map/ppermute | solution.py:349
  66.4 0.8 broadcast_in_dim.8
  67.2 0.0 all-to-all-done.2.in_ref
  67.2 4.7 %all-to-all-start.1 = ((bf16[4,384,128]{2,1,0:T(8,128)(2,1)}), bf16[4,384,128]{2,1,0:T(8,128)(2,1)S(1)}, u32[]{:S(2)}, u32[]{:S(2)}) async-start(bf16[4,384,128]{2,1,0:T(8,128)(2,1)} %broadcast_in_dim.8), calls=%async_computation.1 | async-start | bytes 786432 | tf_op jit(solution)/shard_map/all_to_all | solution.py:360
  71.9 3.7 %shard_map.125.got_far = bf16[32,128,256]{2,1,0:T(8,128)(2,1)} custom-call(bf16[512,128]{1,0:T(8,128)(2,1)S(1)} %get-tuple-element.33.down_ref, bf16[4,256,128]{2,1,0:T(8,128)(2,1)S(1)} %all-to-all-done.2.in_ref, s32[32,1,256]{2,1,0:T(1,128)S(1)} %copy.20.k_ref), custom_call_target="tpu_custom_call" | custom-call | flops 2097152000 | bytes 425984 | tf_op jit(solution)/shard_map/pallas_call | solution.py:55
  75.6 0.0 copy-start.2
  75.6 0.0 copy-start.3
  75.6 0.0 copy-start.4
  75.7 7.0 %shard_map.126 = bf16[1280,128]{1,0:T(8,128)(2,1)S(1)} custom-call(s32[1]{0:T(128)} %bitcast.3.which_ref, bf16[512,128]{1,0:T(8,128)(2,1)S(1)} %get-tuple-element.24.bar_ref, bf16[32,32,256]{2,1,0:T(8,128)(2,1)} %copy-done.8, bf16[32,128,256]{2,1,0:T(8,128)(2,1)} %shard_map.125.got_far, bf16[128,4096]{1,0:T(8,128)(2,1)} %copy-done.7, bf16[512,256]{1,0:T(8,128)(2,1)} %cot_far.3), custom_call_target="tpu_custom_call" | custom-call | flops 4194304000 | bytes 131072 | tf_op jit(solution)/shard_map/pallas_call | solution.py:55
  82.6 0.0 all-to-all-done.1.got_ref
  82.6 0.0 copy-done.2
  82.6 0.0 copy-done.3
  82.6 0.0 copy-done.4
  82.7 1.3 shard_map.124
  84.0 12.2 %all_to_all.30 = bf16[16,96,128]{2,1,0:T(8,128)(2,1)S(1)} all-to-all(bf16[16,96,128]{2,1,0:T(8,128)(2,1)S(1)} %pad_maximum_fusion), channel_id=1, replica_groups=mesh['zh'=8,'zl'=2,'y'=4,'core'=2,'feat'=4] {'zl','y','core'}, dimensions={0} | all-to-all | bytes 786432 | tf_op jit(solution)/shard_map/all_to_all | solution.py:353
  96.1 0.1 reduce_sum.24
  96.2 22.7 %all_to_all.31 = bf16[8,96,128]{2,1,0:T(8,128)(2,1)S(1)} all-to-all(bf16[8,96,128]{2,1,0:T(8,128)(2,1)S(1)} %broadcast_in_dim.10), channel_id=1, replica_groups=mesh['zh'=8,'zl'=2,'y'=4,'core'=2,'feat'=4] {'zh'}, dimensions={0} | all-to-all | bytes 393216 | tf_op jit(solution)/shard_map/all_to_all | solution.py:360
  118.9 0.1 broadcast_in_dim.11
  119.0 14.5 %all_to_all.32.total_ref = bf16[16,96,128]{2,1,0:T(8,128)(2,1)S(1)} all-to-all(bf16[16,96,128]{2,1,0:T(8,128)(2,1)S(1)} %broadcast_in_dim.11), channel_id=1, replica_groups=mesh['zh'=8,'zl'=2,'y'=4,'core'=2,'feat'=4] {'zl','y','core'}, dimensions={0} | all-to-all | bytes 786432 | tf_op jit(solution)/shard_map/all_to_all | solution.py:360
  133.5 0.9 shard_map.127
  (7 shorter events, 0.1 us)
Async XLA Ops:
  0.6 7.5 %copy-start.5 = (s32[1,6,128]{2,0,1:T(1,128)S(1)}, s32[1,6,128]{2,0,1:T(1,128)}, u32[]{:S(2)}) copy-start(s32[1,6,128]{2,0,1:T(1,128)} %param.17) | copy-start | bytes 9220
  0.6 7.6 %copy-start.10 = (s32[512,16]{0,1:T(8,128)S(1)}, s32[512,16]{0,1:T(8,128)}, u32[]{:S(2)}) copy-start(s32[512,16]{0,1:T(8,128)} %param.15) | copy-start | bytes 98308
  0.7 9.6 %copy-start.1 = (bf16[4096,128]{1,0:T(8,128)(2,1)S(1)}, bf16[4096,128]{1,0:T(8,128)(2,1)}, u32[]{:S(2)}) copy-start(bf16[4096,128]{1,0:T(8,128)(2,1)} %wbil_far.1) | copy-start | bytes 3145732
  0.7 9.6 %copy-start.6 = (s32[512]{0:T(512)S(1)}, s32[512]{0:T(512)}, u32[]{:S(2)}) copy-start(s32[512]{0:T(512)} %param.16) | copy-start | bytes 6148
  0.7 9.6 %copy-start = (f32[16,32,512]{2,1,0:T(8,128)S(1)}, f32[16,32,512]{2,1,0:T(8,128)}, u32[]{:S(2)}) copy-start(f32[16,32,512]{2,1,0:T(8,128)} %param.14) | copy-start | bytes 3145732
  3.3 14.6 %all-to-all-start = ((bf16[4,1024,128]{2,1,0:T(8,128)(2,1)}), bf16[4,1024,128]{2,1,0:T(8,128)(2,1)S(1)}, u32[]{:S(2)}, u32[]{:S(2)}) async-start(bf16[4,1024,128]{2,1,0:T(8,128)(2,1)} %shard_map.120), calls=%async_computation | async-start | bytes 2097152 | tf_op jit(solution)/shard_map/all_to_all | solution.py:392
  14.2 1.0 copy-start.7
  15.2 0.8 copy-start.8
  16.0 0.8 copy-start.9
  18.2 32.0 %collective-permute-start = (bf16[128,128]{1,0:T(8,128)(2,1)S(1)}, bf16[128,128]{1,0:T(8,128)(2,1)S(1)}, u32[]{:S(2)}, u32[]{:S(2)}) collective-permute-start(bf16[128,128]{1,0:T(8,128)(2,1)S(1)} %get-tuple-element.22), channel_id=1, source_target_pairs={{0,4},{1,9},{2,14},{3,511},{4,8},{5,13},{6,18},{7,3},{8,12},{9,17}... | collective-permute-start | bytes 98312 | tf_op jit(solution)/shard_map/ppermute | solution.py:349
  27.6 22.6 %collective-permute-start.1 = (bf16[128,128]{1,0:T(8,128)(2,1)S(1)}, bf16[128,128]{1,0:T(8,128)(2,1)S(1)}, u32[]{:S(2)}, u32[]{:S(2)}) collective-permute-start(bf16[128,128]{1,0:T(8,128)(2,1)S(1)} %get-tuple-element.23), channel_id=1, source_target_pairs={{0,504},{1,501},{4,508},{5,505},{8,0},{9,509},{12,4},{13,1},{16,8}... | collective-permute-start | bytes 98312 | tf_op jit(solution)/shard_map/ppermute | solution.py:349
  51.0 16.2 %all-to-all-start.2 = ((bf16[4,256,128]{2,1,0:T(8,128)(2,1)}), bf16[4,256,128]{2,1,0:T(8,128)(2,1)S(1)}, u32[]{:S(2)}, u32[]{:S(2)}) async-start(bf16[4,256,128]{2,1,0:T(8,128)(2,1)} %broadcast_in_dim.9), calls=%async_computation.2 | async-start | bytes 524288 | tf_op jit(solution)/shard_map/all_to_all | solution.py:360
  54.4 5.9 %collective-permute-start.2 = (bf16[128,128]{1,0:T(8,128)(2,1)S(1)}, bf16[128,128]{1,0:T(8,128)(2,1)S(1)}, u32[]{:S(2)}, u32[]{:S(2)}) collective-permute-start(bf16[128,128]{1,0:T(8,128)(2,1)S(1)} %get-tuple-element.28), channel_id=1, source_target_pairs={{0,508},{1,505},{2,502},{3,7},{4,0},{5,509},{6,506},{7,11},{8,4},{... | collective-permute-start | bytes 98312 | tf_op jit(solution)/shard_map/ppermute | solution.py:349
  58.4 8.0 %collective-permute-start.3 = (bf16[128,128]{1,0:T(8,128)(2,1)S(1)}, bf16[128,128]{1,0:T(8,128)(2,1)S(1)}, u32[]{:S(2)}, u32[]{:S(2)}) collective-permute-start(bf16[128,128]{1,0:T(8,128)(2,1)S(1)} %get-tuple-element.29), channel_id=1, source_target_pairs={{0,8},{1,13},{4,12},{5,17},{8,16},{9,21},{12,20},{13,25},{16,24},{... | collective-permute-start | bytes 98312 | tf_op jit(solution)/shard_map/ppermute | solution.py:349
  67.2 15.4 %all-to-all-start.1 = ((bf16[4,384,128]{2,1,0:T(8,128)(2,1)}), bf16[4,384,128]{2,1,0:T(8,128)(2,1)S(1)}, u32[]{:S(2)}, u32[]{:S(2)}) async-start(bf16[4,384,128]{2,1,0:T(8,128)(2,1)} %broadcast_in_dim.8), calls=%async_computation.1 | async-start | bytes 786432 | tf_op jit(solution)/shard_map/all_to_all | solution.py:360
  75.6 7.0 %copy-start.2 = (bf16[512,256]{1,0:T(8,128)(2,1)S(1)}, bf16[512,256]{1,0:T(8,128)(2,1)}, u32[]{:S(2)}) copy-start(bf16[512,256]{1,0:T(8,128)(2,1)} %feats_ref.1) | copy-start | bytes 786436
  75.6 7.0 %copy-start.3 = (bf16[512,256]{1,0:T(8,128)(2,1)S(1)}, bf16[512,256]{1,0:T(8,128)(2,1)}, u32[]{:S(2)}) copy-start(bf16[512,256]{1,0:T(8,128)(2,1)} %cot_far.3) | copy-start | bytes 786436
  75.6 7.0 %copy-start.4 = (bf16[256,128]{1,0:T(8,128)(2,1)S(1)}, bf16[256,128]{1,0:T(8,128)(2,1)}, u32[]{:S(2)}) copy-start(bf16[256,128]{1,0:T(8,128)(2,1)} %wdown_ref.1) | copy-start | bytes 196612
